TPU v7x, 128 devices: a whole 4x4x4 slice. The times are simulated.
128 devices in a mesh: tile: 16 (over y_lo, x, core), subap: 8 (over y_hi, z).
Axes of the slice: x: 4, y: 4 (y_hi: 2, y_lo: 2; y = y_hi * 2 + y_lo), z: 4, core: 2. Of those that a mesh axis runs over, the one named last changes fastest.
Arguments:
- pulses: bfloat16 [16, 8, 2, 128, 16384], P('tile', 'subap'), may hold values from -6 to 6
- footprint: int32 [16, 8, 32], P('tile', 'subap'), may hold values from 0 to 47, as said below
- offsets: int32 [48], replicated, may hold values from 0 to 15872
- azimuth: bfloat16 [48, 16, 8, 2, 256, 128], P('tile', None, 'subap'), may hold values from -0.09375 to 0.09375
- range_interp: bfloat16 [48, 2, 512, 256], P('tile'), may hold values from -0.1875 to 0.1875
Outputs:
- image: float32 [48, 2, 256, 256], P('tile', None, 'subap')
Inputs may be any that keep to these rules, and one draw needn't show every extreme that they name: For every o, footprint[k, s, o * 2 : (o + 1) * 2] holds 2 different tiles of o * 3 to (o + 1) * 3 - 1.
All inputs are finite; a program needn't handle non-finite values.
Results may differ from a plain program's by a relative error of at most 0.0029.
Values may be sent and summed in bfloat16 or wider, within the bound.
No kernel may reach another device: no remote copies, remote signals or barrier semaphores. Data moves between devices by JAX's collectives and lax.ppermute only.
A program may use at most 128 MiB of HBM per device.

v0:
```python
import jax
import jax.numpy as jnp
from jax import lax
from jax.sharding import PartitionSpec as P


def combine(prod):
    real = prod[..., 0, 0, :, :] - prod[..., 1, 1, :, :]
    imag = prod[..., 0, 1, :, :] + prod[..., 1, 0, :, :]
    return jnp.stack([real, imag], axis=-3)


def on_device(pulses, footprint, offsets, azimuth, range_interp):
    tiles = offsets.shape[0]
    width = range_interp.shape[2]
    block = pulses[0, 0]

    def cut(start):
        return lax.dynamic_slice_in_dim(block, start, width, 2)

    windows = jax.vmap(cut)(offsets)
    tile_ids = jnp.arange(tiles, dtype=jnp.int32)
    hit = jnp.any(footprint[0, 0][None, :] == tile_ids[:, None], axis=1).astype(jnp.bfloat16)
    windows = windows * hit[:, None, None, None]
    arrived = lax.all_to_all(windows[:, None], "tile", split_axis=0, concat_axis=1, tiled=True)
    prod = jnp.einsum(
        "tkcpr,tdru->tkcdpu", arrived, range_interp, preferred_element_type=jnp.float32
    )
    ranged = combine(prod).astype(jnp.bfloat16)
    sub_image = combine(
        jnp.einsum(
            "tkcap,tkdpu->tcdau", azimuth[:, :, 0], ranged, preferred_element_type=jnp.float32
        )
    )
    raw = lax.psum(sub_image, "subap")
    power = jnp.mean(raw * raw, axis=(1, 2, 3))
    height = raw.shape[2] // lax.axis_size("subap")
    own_rows = lax.dynamic_slice_in_dim(raw, lax.axis_index("subap") * height, height, 2)
    return own_rows / jnp.sqrt(power + 1e-06)[:, None, None, None]


def solution(mesh):
    in_specs = (
        P("tile", "subap", None, None, None),
        P("tile", "subap", None),
        P(),
        P("tile", None, "subap", None, None, None),
        P("tile", None, None, None),
    )
    out_specs = P("tile", None, "subap", None)
    return jax.shard_map(
        on_device, mesh=mesh, in_specs=in_specs, out_specs=out_specs, check_vma=False
    )
```

profile of v0, /device:TPU:0, one launch (start us, length us, event | category | flops | bytes accessed | tf_op | source)
XLA Modules:
  0.0 380.4 jit_solution(2117407463803907995)
XLA Ops:
  6.5 0.0 copy-start
  6.5 0.0 all-reduce.3.cloned.1.call-start
  6.5 21.2 %copy.46 = bf16[1,1,2,128,16384]{3,2,4,1,0:T(2,128)(2,1)} copy(bf16[1,1,2,128,16384]{4,3,2,1,0:T(8,128)(2,1)} %param.5) | data formatting | bytes 16777216 | tf_op args[0]
  27.8 0.0 copy-done.2
  27.8 0.1 fusion.21
  27.9 30.5 %gather_fusion = bf16[48,2,128,512]{2,1,3,0:T(2,128)(2,1)} fusion(bf16[2,128,16384]{1,0,2:T(2,128)(2,1)} %bitcast.66, s32[48]{0:T(128)S(1)} %fusion.23), kind=kCustom, calls=%fused_computation | custom fusion | bytes 25166400 | tf_op jit(solution)/shard_map/vmap()/gather | solution.py:19
  58.4 13.9 %fusion.2 = bf16[48,1,2,128,512]{3,2,4,1,0:T(2,128)(2,1)S(1)} fusion(bf16[48,2,128,512]{2,1,3,0:T(2,128)(2,1)} %gather_fusion, bf16[48]{0:T(256)(128)(2,1)S(1)} %convert_element_type.8), kind=kLoop, calls=%fused_computation.4 | loop fusion | flops 6291456 | bytes 25165920 | tf_op jit(solution)/shard_map/mul | solution.py:24
  72.3 145.5 %all_to_all.18 = bf16[48,1,2,128,512]{3,2,4,1,0:T(2,128)(2,1)} all-to-all(bf16[48,1,2,128,512]{3,2,4,1,0:T(2,128)(2,1)S(1)} %fusion.2), channel_id=1, replica_groups=mesh['tile'=16,'subap'=8] {'tile'}, dimensions={0} | all-to-all | bytes 25165824 | tf_op jit(solution)/shard_map/all_to_all | solution.py:25
  217.8 30.9 %copy.49 = bf16[16,3,1,2,128,512]{5,4,3,0,1,2:T(8,128)(2,1)} copy(bf16[16,3,1,2,128,512]{4,3,5,1,0,2:T(2,128)(2,1)} %bitcast.67) | data formatting | bytes 25165824 | tf_op jit(solution)/shard_map/all_to_all | solution.py:25
  248.7 0.0 copy-done
  248.7 14.4 %fusion.3 = f32[3,16,2,2,128,256]{5,4,3,2,1,0:T(8,128)} fusion(bf16[16,3,1,2,128,512]{5,4,3,0,1,2:T(8,128)(2,1)} %copy.49, bf16[3,2,512,256]{3,2,1,0:T(8,128)(2,1)S(1)} %copy-done), kind=kOutput, calls=%fused_computation.5 | convolution fusion | flops 6442450944 | bytes 39321600 | tf_op jit(solution)/shard_map/tkcpr,tdru->tkcdpu/dot_general | solution.py:26
  263.2 6.0 %fusion.13 = bf16[3,16,1,128,256]{4,3,1,0,2:T(8,128)(2,1)S(1)} fusion(f32[3,16,2,2,128,256]{5,4,3,2,1,0:T(8,128)} %fusion.3), kind=kLoop, calls=%fused_computation.17 | loop fusion | flops 3145728 | bytes 15728640 | tf_op jit(solution)/shard_map/sub | solution.py:8
  269.2 0.0 slice-start.1
  269.2 5.8 %fusion.14 = bf16[3,16,1,128,256]{4,3,1,0,2:T(8,128)(2,1)S(1)} fusion(f32[3,16,2,2,128,256]{5,4,3,2,1,0:T(8,128)} %fusion.3), kind=kLoop, calls=%fused_computation.18 | loop fusion | flops 3145728 | bytes 15728640 | tf_op jit(solution)/shard_map/add | solution.py:9
  275.0 0.0 slice-done
  275.0 0.0 slice-done.1
  275.0 0.0 copy-start.1
  275.0 3.4 fusion.15
  278.4 0.2 fusion.20
  278.7 1.3 pad_maximum_fusion
  279.9 0.0 all-reduce.3.cloned.1.call-update
  279.9 90.3 %all-reduce.3.cloned.1.call-done = f32[3,2,256,256]{3,2,1,0:T(8,128)} async-done(((f32[3,2,256,256]{3,2,1,0:T(8,128)}), f32[3,2,256,256]{3,2,1,0:T(8,128)}) %all-reduce.3.cloned.1.call-update) | async-done | bytes 1572880 | tf_op jit(solution)/shard_map/psum | solution.py:35
  370.2 1.7 multiply_reduce_fusion
  371.9 1.7 dynamic-slice_divide_fusion
  (9 shorter events, 0.0 us)
Async XLA Ops:
  6.5 242.2 %copy-start = (bf16[3,2,512,256]{3,2,1,0:T(8,128)(2,1)S(1)}, bf16[3,2,512,256]{3,2,1,0:T(8,128)(2,1)}, u32[]{:S(2)}) copy-start(bf16[3,2,512,256]{3,2,1,0:T(8,128)(2,1)} %param.9) | copy-start | bytes 4718596
  6.5 21.2 %copy-start.2 = (s32[48]{0:T(128)S(1)}, s32[48]{0:T(128)}, u32[]{:S(2)}) copy-start(s32[48]{0:T(128)} %param.7) | copy-start | bytes 580
  6.5 21.3 %copy-start.3 = (s32[1,1,32]{2,1,0:T(1,128)S(1)}, s32[1,1,32]{2,1,0:T(1,128)}, u32[]{:S(2)}) copy-start(s32[1,1,32]{2,1,0:T(1,128)} %param.6) | copy-start | bytes 388
  6.5 363.7 %all-reduce.3.cloned.1.call-start = ((), (), s32[]{:S(2)}) async-start(), calls=%async_computation.1 | async-start | bytes 3145728 | tf_op jit(solution)/shard_map/psum | solution.py:35
  263.2 11.8 %slice-start = ((s8[6291456]{0:T(1024)(128)(4,1)}), s8[4194304]{0:T(1024)(128)(4,1)S(1)}, s32[]{:S(2)}) async-start(s8[6291456]{0:T(1024)(128)(4,1)} %bitcast.68), calls=%async_computation.2 | async-start | bytes 8388608
  269.2 5.8 %slice-start.1 = ((s8[6291456]{0:T(1024)(128)(4,1)}), s8[2097152]{0:T(1024)(128)(4,1)S(1)}, s32[]{:S(2)}) async-start(s8[6291456]{0:T(1024)(128)(4,1)} %bitcast.68), calls=%async_computation.3 | async-start | bytes 4194304
  275.0 98.6 %copy-start.1 = (bf16[3,2,512,256]{3,2,1,0:T(8,128)(2,1)S(1)}, bf16[3,2,512,256]{3,2,1,0:T(8,128)(2,1)}, u32[]{:S(2)}) copy-start(bf16[3,2,512,256]{3,2,1,0:T(8,128)(2,1)} %param.9) | copy-start | bytes 4718596
Sparse Core Ops, SparseCore 0:
  280.1 90.1 all-reduce.2
where the time goes:
time: 382 us; the launch traced here: 380 us
  blocking collectives  145 us (38%)
  waiting for transfers between devices  90.3 us (24%)
  local copies, waits for them, and re-layouts  82.7 us (22%)
  other arithmetic  30.7 us (8%)
  matrix products  17.8 us (5%)
  between operations  13.5 us (4%)
    all_to_all x1, blocking collectives, on_device(): lax.all_to_all(windows[:, None], 'tile', split_axis=0, concat_axis=1, til...  145 us
    psum x1, waiting for transfers between devices, on_device(): raw = lax.psum(sub_image, 'subap')  90.3 us
    all_to_all x1, local copies, waits for them, and re-layouts, on_device(): lax.all_to_all(windows[:, None], 'tile', split_axis=0, concat_axis=1, til...  30.9 us
    gather x1, local copies, waits for them, and re-layouts, cut(): return lax.dynamic_slice_in_dim(block, start, width, 2)  30.5 us
    unnamed x13, local copies, waits for them, and re-layouts  21.3 us
    dot_general x1, matrix products, on_device(): jnp.einsum('tkcpr,tdru->tkcdpu', arrived, range_interp, preferred_element...  14.4 us
    mul x1, other arithmetic, on_device(): windows = windows * hit[:, None, None, None]  13.9 us
  transfers between devices with their start and end apart: 1, of which 1 were waited for; matrix products, arithmetic and copies ran while one was open for 0% of the time, Pallas kernels for 0%

commit v1 on v0

v1 whole, which is shorter than its diff:
```python
import functools

import jax
import jax.numpy as jnp
from jax import lax
from jax.experimental import pallas as pl
from jax.experimental.pallas import tpu as pltpu
from jax.sharding import PartitionSpec as P

LANES = 128
ANY = pl.BlockSpec(memory_space=pl.ANY)
SMEM = pl.BlockSpec(memory_space=pltpu.SMEM)
VMEM = pl.BlockSpec(memory_space=pltpu.VMEM)


def extract_kernel(count, width, base_ref, shift_ref, block, out, wide, cut, in_sem, out_sem):
    span = wide.shape[2]

    def fetch(i):
        at = pl.multiple_of(base_ref[i], LANES)
        return pltpu.make_async_copy(block.at[:, pl.ds(at, span)], wide.at[i], in_sem.at[i])

    def send(i):
        return pltpu.make_async_copy(cut.at[i], out.at[i], out_sem.at[i])

    def first(i, c):
        fetch(i).start()
        return c

    lax.fori_loop(0, count, first, 0)

    def step(i, c):
        fetch(i).wait()
        rows = wide[i].astype(jnp.float32)
        turned = pltpu.roll(rows, span - shift_ref[i], 1)
        cut[i] = turned[:, :width].astype(cut.dtype)
        send(i).start()
        return c

    lax.fori_loop(0, count, step, 0)

    def last(i, c):
        send(i).wait()
        return c

    lax.fori_loop(0, count, last, 0)


def extract(block, base, shift, width):
    count, rows = base.shape[0], block.shape[0]
    span = width + LANES
    return pl.pallas_call(
        functools.partial(extract_kernel, count, width),
        out_shape=jax.ShapeDtypeStruct((count, rows, width), block.dtype),
        in_specs=[SMEM, SMEM, ANY],
        out_specs=ANY,
        scratch_shapes=[
            pltpu.VMEM((count, rows, span), block.dtype),
            pltpu.VMEM((count, rows, width), block.dtype),
            pltpu.SemaphoreType.DMA((count,)),
            pltpu.SemaphoreType.DMA((count,)),
        ],
        compiler_params=pltpu.CompilerParams(vmem_limit_bytes=48 << 20),
        cost_estimate=pl.CostEstimate(
            flops=0, transcendentals=0, bytes_accessed=count * rows * (span + width) * 2
        ),
    )(base, shift, block)


def compute_kernel(slots, local_ref, window, azimuth, table, out, sub, held, sem):
    source = pl.program_id(0)
    pulses = window.shape[2] // 2
    copies = []
    for slot in range(slots):
        tile = local_ref[source, slot]
        copies.append(
            pltpu.make_async_copy(azimuth.at[tile, source], held.at[slot], sem.at[slot])
        )
        copies[-1].start()

    @pl.when(source == 0)
    def _():
        sub[...] = jnp.zeros_like(sub)

    for slot in range(slots):
        tile = local_ref[source, slot]
        x = window[0, slot]
        pr = jnp.dot(x, table[tile, 0], preferred_element_type=jnp.float32)
        pi = jnp.dot(x, table[tile, 1], preferred_element_type=jnp.float32)
        rr = (pr[:pulses] - pi[pulses:]).astype(x.dtype)
        ri = (pi[:pulses] + pr[pulses:]).astype(x.dtype)
        right = jnp.concatenate(
            [jnp.concatenate([rr, ri], 1), jnp.concatenate([-ri, rr], 1)], 0
        )
        copies[slot].wait()
        left = jnp.concatenate([held[slot, 0], held[slot, 1]], 1)
        both = jnp.dot(left, right, preferred_element_type=jnp.float32)
        width = rr.shape[1]
        sub[tile, 0] += both[:, :width]
        sub[tile, 1] += both[:, width:]

    @pl.when(source == pl.num_programs(0) - 1)
    def _():
        groups, rows = out.shape[0], out.shape[3]
        for g in range(groups):
            out[g] = sub[:, :, g * rows : (g + 1) * rows, :].astype(out.dtype)


def compute(windows, local, azimuth, table, groups):
    sources, slots, both, width = windows.shape
    tiles, _, parts, height, pulses = azimuth.shape
    across = table.shape[3]
    rows = height // groups
    gs = pltpu.PrefetchScalarGridSpec(
        num_scalar_prefetch=1,
        grid=(sources,),
        in_specs=[
            pl.BlockSpec((1, slots, both, width), lambda i, l: (i, 0, 0, 0)),
            ANY,
            pl.BlockSpec(table.shape, lambda i, l: (0, 0, 0, 0)),
        ],
        out_specs=pl.BlockSpec((groups, tiles, parts, rows, across), lambda i, l: (0,) * 5),
        scratch_shapes=[
            pltpu.VMEM((tiles, parts, height, across), jnp.float32),
            pltpu.VMEM((slots, parts, height, pulses), azimuth.dtype),
            pltpu.SemaphoreType.DMA((slots,)),
        ],
    )
    return pl.pallas_call(
        functools.partial(compute_kernel, slots),
        out_shape=jax.ShapeDtypeStruct((groups, tiles, parts, rows, across), jnp.bfloat16),
        grid_spec=gs,
        compiler_params=pltpu.CompilerParams(vmem_limit_bytes=32 << 20),
    )(local, windows, azimuth, table)


def on_device(pulses, footprint, offsets, azimuth, range_interp):
    width = range_interp.shape[2]
    held = range_interp.shape[0]
    owners = lax.axis_size("tile")
    subaps = lax.axis_size("subap")
    block = pulses.reshape(-1, pulses.shape[-1])
    listed = footprint.reshape(owners, -1)
    slots = listed.shape[1]
    listed = jnp.sort(listed, axis=1)
    starts = jnp.take(offsets, listed.reshape(-1))
    base = jnp.minimum(starts // LANES * LANES, block.shape[1] - width - LANES)
    windows = extract(block, base, starts - base, width)
    windows = windows.reshape(owners, slots, block.shape[0], width)
    arrived = lax.all_to_all(windows, "tile", split_axis=0, concat_axis=0, tiled=True)
    local = lax.all_to_all(listed, "tile", split_axis=0, concat_axis=0, tiled=True)
    local = local - lax.axis_index("tile") * held
    parts = compute(arrived, local, azimuth[:, :, 0], range_interp, subaps)
    got = lax.all_to_all(parts, "subap", split_axis=0, concat_axis=0, tiled=True)
    raw = jnp.sum(got.astype(jnp.float32), axis=0)
    total = jnp.sum(raw * raw, axis=(1, 2, 3))
    hop = 1
    while hop < subaps:
        total = total + lax.ppermute(total, "subap", [(i, i ^ hop) for i in range(subaps)])
        hop *= 2
    power = total / (raw.size // held * subaps)
    return raw / jnp.sqrt(power + 1e-06)[:, None, None, None]


def solution(mesh):
    in_specs = (
        P("tile", "subap", None, None, None),
        P("tile", "subap", None),
        P(),
        P("tile", None, "subap", None, None, None),
        P("tile", None, None, None),
    )
    out_specs = P("tile", None, "subap", None)
    return jax.shard_map(
        on_device, mesh=mesh, in_specs=in_specs, out_specs=out_specs, check_vma=False
    )
```

time: 382 us -> 208 us (0.54)
  blocking collectives: 145 us -> 21.9 us
  local copies, waits for them, and re-layouts: 82.7 us -> 5.28 us
  Pallas kernels: 0 us -> 38.4 us
  waiting for transfers between devices: 90.3 us -> 125 us
  other arithmetic: 30.7 us -> 2.98 us
  matrix products: 17.8 us -> 0 us
  between operations: 13.5 us -> 0.11 us
  starting transfers between devices: 0.01 us -> 13.2 us
    all_to_all x1, blocking collectives: 145 us -> 21.9 us  [on_device(): lax.all_to_all(parts, 'subap', split_axis=0, concat_axis=0, tiled=True)]
    all_to_all x0 -> x2, waiting for transfers between devices: none -> 113 us  [the longest x1 113 us: on_device(): lax.all_to_all(windows, 'tile', split_axis=0, concat_axis=0, tiled=True)]
    psum x1 -> x0, waiting for transfers between devices: 90.3 us -> none  [on_device(): raw = lax.psum(sub_image, 'subap')]
    pallas_call x0 -> x2, Pallas kernels: none -> 38.4 us  [the longest x1 28 us: compute(): pl.pallas_call(functools.partial(compute_kernel, slots), out_shape=jax.Sh...]
    all_to_all x1 -> x2, local copies, waits for them, and re-layouts: 30.9 us -> 0.76 us  [on_device(): lax.all_to_all(listed, 'tile', split_axis=0, concat_axis=0, tiled=True)]
    gather x1, local copies, waits for them, and re-layouts: 30.5 us -> 0.7 us  [on_device(): starts = jnp.take(offsets, listed.reshape(-1))]
    unnamed x13 -> x7, local copies, waits for them, and re-layouts: 21.3 us -> 3.31 us
    dot_general x2 -> x0, matrix products: 17.8 us -> none  [the longest x1 14.4 us: on_device(): jnp.einsum('tkcpr,tdru->tkcdpu', arrived, range_interp, preferred_element...]
  transfers between devices with their start and end apart: 1 -> 5, of which waited for: 1 -> 4; matrix products, arithmetic and copies ran while one was open for 0% -> 1% of each run, Pallas kernels for 0% -> 5%
where the time goes in v1:
time: 208 us; the launch traced here: 207 us
  waiting for transfers between devices  125 us (60%)
  Pallas kernels  38.4 us (18%)
  blocking collectives  21.9 us (11%)
  starting transfers between devices  13.2 us (6%)
  local copies, waits for them, and re-layouts  5.28 us (3%)
  other arithmetic  2.98 us (1%)
    all_to_all x1, waiting for transfers between devices, on_device(): lax.all_to_all(windows, 'tile', split_axis=0, concat_axis=0, tiled=True)  113 us
    pallas_call x1, Pallas kernels, compute(): pl.pallas_call(functools.partial(compute_kernel, slots), out_shape=jax.Sh...  28 us
    all_to_all x1, blocking collectives, on_device(): lax.all_to_all(parts, 'subap', split_axis=0, concat_axis=0, tiled=True)  21.9 us
    ppermute x3, waiting for transfers between devices, on_device(): lax.ppermute(total, 'subap', [(i, i ^ hop) for i in range(subaps)])  11.8 us
    pallas_call x1, Pallas kernels, extract(): pl.pallas_call(functools.partial(extract_kernel, count, width), out_shape...  10.5 us
    all_to_all x1, starting transfers between devices, on_device(): lax.all_to_all(windows, 'tile', split_axis=0, concat_axis=0, tiled=True)  5.91 us
    all_to_all x1, starting transfers between devices, on_device(): lax.all_to_all(listed, 'tile', split_axis=0, concat_axis=0, tiled=True)  5.5 us
  transfers between devices with their start and end apart: 5, of which 4 were waited for; matrix products, arithmetic and copies ran while one was open for 1% of the time, Pallas kernels for 5%

profile of v1, /device:TPU:0, one launch (start us, length us, event | category | flops | bytes accessed | tf_op | source)
XLA Modules:
  0.0 206.6 jit_solution(14989394116494719628)
XLA Ops:
  0.0 0.5 broadcast.50
  0.5 1.3 reduce.3
  2.0 0.6 sort.15
  2.6 0.7 copy.19
  3.3 5.5 %all-to-all-start = ((s32[16,1,2]{2,1,0:T(1,128)}), s32[16,1,2]{2,1,0:T(1,128)S(1)}, u32[]{:S(2)}, u32[]{:S(2)}) async-start(s32[16,1,2]{2,1,0:T(1,128)} %copy.19), calls=%async_computation | async-start | bytes 16384 | tf_op jit(solution)/shard_map/all_to_all | solution.py:151
  8.9 0.1 reshape.55
  9.0 0.1 reshape.54
  9.1 0.7 gather_fusion
  9.8 10.5 %shard_map.55 = bf16[32,256,512]{2,1,0:T(8,128)(2,1)} custom-call(s32[32]{0:T(128)S(1)} %get-tuple-element.9.base_ref, s32[32]{0:T(128)S(1)} %get-tuple-element.8.shift_ref, bf16[256,16384]{1,0:T(8,128)(2,1)} %bitcast.10), custom_call_target="tpu_custom_call" | custom-call | bytes 18874368 | tf_op jit(solution)/shard_map/pallas_call | solution.py:52
  20.3 5.9 %all-to-all-start.1 = ((bf16[16,2,256,512]{3,2,1,0:T(8,128)(2,1)}), bf16[16,2,256,512]{3,2,1,0:T(8,128)(2,1)}, u32[]{:S(2)}, u32[]{:S(2)}) async-start(bf16[16,2,256,512]{3,2,1,0:T(8,128)(2,1)} %bitcast.9), calls=%async_computation.1 | async-start | bytes 16777216 | tf_op jit(solution)/shard_map/all_to_all | solution.py:150
  26.3 0.1 copy.23.local_ref
  26.4 112.8 %all-to-all-done.1.window = bf16[16,2,256,512]{3,2,1,0:T(8,128)(2,1)} async-done(((bf16[16,2,256,512]{3,2,1,0:T(8,128)(2,1)}), bf16[16,2,256,512]{3,2,1,0:T(8,128)(2,1)}, u32[]{:S(2)}, u32[]{:S(2)}) %all-to-all-start.1) | async-done | bytes 8388640 | tf_op jit(solution)/shard_map/all_to_all | solution.py:150
  139.3 2.8 %copy-done.1 = bf16[3,16,1,2,256,128]{5,4,3,2,1,0:T(8,128)(2,1)S(1)} copy-done((bf16[3,16,1,2,256,128]{5,4,3,2,1,0:T(8,128)(2,1)S(1)}, bf16[3,16,1,2,256,128]{5,4,3,2,1,0:T(8,128)(2,1)}, u32[]{:S(2)}) %copy-start.1) | copy-done | bytes 6291480
  142.0 28.0 %shard_map.56 = bf16[8,3,2,32,256]{4,3,2,1,0:T(8,128)(2,1)S(1)} custom-call(s32[16,2]{1,0:T(8,128)S(1)} %copy.23.local_ref, bf16[16,2,256,512]{3,2,1,0:T(8,128)(2,1)} %all-to-all-done.1.window, bf16[3,16,2,256,128]{4,3,2,1,0:T(8,128)(2,1)S(1)} %bitcast.8, bf16[3,2,512,256]{3,2,1,0:T(8,128)(2,1)S(1)} %copy-done.2), custom_call_target="tpu_custom_call" | custom-call | tf_op jit(solution)/shard_map/pallas_call | solution.py:129
  170.0 21.9 %all_to_all.19 = bf16[8,3,2,32,256]{4,3,2,1,0:T(8,128)(2,1)S(1)} all-to-all(bf16[8,3,2,32,256]{4,3,2,1,0:T(8,128)(2,1)S(1)} %shard_map.56), channel_id=1, replica_groups=mesh['tile'=16,'subap'=8] {'subap'}, dimensions={0} | all-to-all | bytes 1572864 | tf_op jit(solution)/shard_map/all_to_all | solution.py:154
  191.9 0.1 convert_reduce_fusion
  192.0 0.1 multiply_reduce_fusion
  192.1 0.2 collective-permute-start
  192.4 3.3 %collective-permute-done = f32[3]{0:T(128)S(1)} collective-permute-done((f32[3]{0:T(128)S(1)}, f32[3]{0:T(128)S(1)}, u32[]{:S(2)}, u32[]{:S(2)}) %collective-permute-start) | collective-permute-done | bytes 44 | tf_op jit(solution)/shard_map/ppermute | solution.py:159
  195.7 0.9 collective-permute-start.1
  196.6 4.1 %collective-permute-done.1 = f32[3]{0:T(128)S(1)} collective-permute-done((f32[3]{0:T(128)S(1)}, f32[3]{0:T(128)S(1)}, u32[]{:S(2)}, u32[]{:S(2)}) %collective-permute-start.1) | collective-permute-done | bytes 44 | tf_op jit(solution)/shard_map/ppermute | solution.py:159
  200.7 0.7 collective-permute-start.2
  201.4 4.3 %collective-permute-done.2 = f32[3]{0:T(128)S(1)} collective-permute-done((f32[3]{0:T(128)S(1)}, f32[3]{0:T(128)S(1)}, u32[]{:S(2)}, u32[]{:S(2)}) %collective-permute-start.2) | collective-permute-done | bytes 44 | tf_op jit(solution)/shard_map/ppermute | solution.py:159
  205.8 0.8 broadcast_divide_fusion
  (18 shorter events, 0.4 us)
Async XLA Ops:
  0.0 9.1 %copy-start = (s32[48]{0:T(128)S(1)}, s32[48]{0:T(128)}, u32[]{:S(2)}) copy-start(s32[48]{0:T(128)} %param.7) | copy-start | bytes 580
  3.3 17.0 %all-to-all-start = ((s32[16,1,2]{2,1,0:T(1,128)}), s32[16,1,2]{2,1,0:T(1,128)S(1)}, u32[]{:S(2)}, u32[]{:S(2)}) async-start(s32[16,1,2]{2,1,0:T(1,128)} %copy.19), calls=%async_computation | async-start | bytes 16384 | tf_op jit(solution)/shard_map/all_to_all | solution.py:151
  20.3 118.9 %copy-start.2 = (bf16[3,2,512,256]{3,2,1,0:T(8,128)(2,1)S(1)}, bf16[3,2,512,256]{3,2,1,0:T(8,128)(2,1)}, u32[]{:S(2)}) copy-start(bf16[3,2,512,256]{3,2,1,0:T(8,128)(2,1)} %table.1) | copy-start | bytes 4718596
  20.3 118.9 %all-to-all-start.1 = ((bf16[16,2,256,512]{3,2,1,0:T(8,128)(2,1)}), bf16[16,2,256,512]{3,2,1,0:T(8,128)(2,1)}, u32[]{:S(2)}, u32[]{:S(2)}) async-start(bf16[16,2,256,512]{3,2,1,0:T(8,128)(2,1)} %bitcast.9), calls=%async_computation.1 | async-start | bytes 16777216 | tf_op jit(solution)/shard_map/all_to_all | solution.py:150
  139.3 2.8 %copy-start.1 = (bf16[3,16,1,2,256,128]{5,4,3,2,1,0:T(8,128)(2,1)S(1)}, bf16[3,16,1,2,256,128]{5,4,3,2,1,0:T(8,128)(2,1)}, u32[]{:S(2)}) copy-start(bf16[3,16,1,2,256,128]{5,4,3,2,1,0:T(8,128)(2,1)} %param.8) | copy-start | bytes 18874372
  192.1 3.6 %collective-permute-start = (f32[3]{0:T(128)S(1)}, f32[3]{0:T(128)S(1)}, u32[]{:S(2)}, u32[]{:S(2)}) collective-permute-start(f32[3]{0:T(128)S(1)} %multiply_reduce_fusion), channel_id=1, source_target_pairs={{0,1},{1,0},{2,3},{3,2},{4,5},{5,4},{6,7},{7,6},{8,9},{9,8},{10,11... | collective-permute-start | bytes 44 | tf_op jit(solution)/shard_map/ppermute | solution.py:159
  195.7 5.0 %collective-permute-start.1 = (f32[3]{0:T(128)S(1)}, f32[3]{0:T(128)S(1)}, u32[]{:S(2)}, u32[]{:S(2)}) collective-permute-start(f32[3]{0:T(128)S(1)} %add.38), channel_id=1, source_target_pairs={{0,2},{1,3},{2,0},{3,1},{4,6},{5,7},{6,4},{7,5},{8,10},{9,11},{10,... | collective-permute-start | bytes 44 | tf_op jit(solution)/shard_map/ppermute | solution.py:159
  200.7 5.0 %collective-permute-start.2 = (f32[3]{0:T(128)S(1)}, f32[3]{0:T(128)S(1)}, u32[]{:S(2)}, u32[]{:S(2)}) collective-permute-start(f32[3]{0:T(128)S(1)} %add.39), channel_id=1, source_target_pairs={{0,4},{1,5},{2,6},{3,7},{4,0},{5,1},{6,2},{7,3},{8,12},{9,13},{10,... | collective-permute-start | bytes 44 | tf_op jit(solution)/shard_map/ppermute | solution.py:159

commit v2 on v0

v2 whole, which is shorter than its diff:
```python
import functools

import jax
import jax.numpy as jnp
from jax import lax
from jax.experimental import pallas as pl
from jax.experimental.pallas import tpu as pltpu
from jax.sharding import PartitionSpec as P

LANES = 128
XS, CORES = 4, 2
ANY = pl.BlockSpec(memory_space=pl.ANY)
SMEM = pl.BlockSpec(memory_space=pltpu.SMEM)
VMEM = pl.BlockSpec(memory_space=pltpu.VMEM)


def place(index):
    return index // (XS * CORES), index // CORES % XS, index % CORES


def toward(index, dy, dx, dc):
    y, x, c = place(index)
    return ((y ^ dy) * XS + (x + dx) % XS) * CORES + (c ^ dc)


def pairs(count, dy, dx, dc):
    return [(i, toward(i, dy, dx, dc)) for i in range(count)]


def cut_kernel(pieces, held, footprint_hbm, offsets_hbm, block, *refs):
    outs, refs = refs[: len(pieces)], refs[len(pieces) :]
    footprint, offsets, wide, cut, note, scalar_sem, in_sem, out_sem, note_sem = refs
    scalars = [
        pltpu.make_async_copy(footprint_hbm, footprint, scalar_sem.at[0]),
        pltpu.make_async_copy(offsets_hbm, offsets, scalar_sem.at[1]),
    ]
    for copy in scalars:
        copy.start()
    me = lax.axis_index("tile")
    rows, span = wide.shape[1:]
    width = cut.shape[2]
    slots = outs[0].shape[1] // rows
    lane = lax.broadcasted_iota(jnp.int32, note.shape[1:], 1)
    for copy in scalars:
        copy.wait()
    steps, notes = [], []
    for out, (dy, dx, cores) in zip(outs, pieces):
        for at, dc in enumerate(cores):
            owner = toward(me, dy, dx, dc)
            ids = jnp.zeros(lane.shape, jnp.int32)
            for slot in range(slots):
                tile = footprint[owner * slots + slot]
                start = offsets[tile]
                base = jnp.minimum(start // LANES * LANES, block.shape[1] - span)
                i = len(steps)
                src = block.at[:, pl.ds(pl.multiple_of(base, LANES), span)]
                get = pltpu.make_async_copy(src, wide.at[i], in_sem.at[i])
                dst = out.at[at, slot * rows : (slot + 1) * rows]
                put = pltpu.make_async_copy(cut.at[i], dst, out_sem.at[i])
                get.start()
                steps.append((get, put, start - base))
                ids = jnp.where(lane // LANES == slot, tile - owner * held, ids)
            j = len(notes)
            note[j] = ids.astype(note.dtype)
            told = pltpu.make_async_copy(note.at[j], out.at[at, slots * rows :], note_sem.at[j])
            told.start()
            notes.append(told)
    for i, (get, put, shift) in enumerate(steps):
        get.wait()
        turned = pltpu.roll(wide[i].astype(jnp.float32), lax.rem(span - shift, span), 1)
        cut[i] = turned[:, :width].astype(cut.dtype)
        put.start()
    for _, put, _ in steps:
        put.wait()
    for told in notes:
        told.wait()


def cut_windows(pieces, footprint, offsets, block, held, slots, width):
    rows = block.shape[0]
    span = width + LANES
    whole = sum(len(cores) for _, _, cores in pieces)
    count = slots * whole
    return pl.pallas_call(
        functools.partial(cut_kernel, pieces, held),
        out_shape=[
            jax.ShapeDtypeStruct((len(cores), slots * rows + NOTE, width), block.dtype)
            for _, _, cores in pieces
        ],
        in_specs=[ANY] * 3,
        out_specs=[ANY] * len(pieces),
        scratch_shapes=[
            pltpu.SMEM(footprint.shape, footprint.dtype),
            pltpu.SMEM(offsets.shape, offsets.dtype),
            pltpu.VMEM((count, rows, span), block.dtype),
            pltpu.VMEM((count, rows, width), block.dtype),
            pltpu.VMEM((whole, NOTE, width), block.dtype),
            pltpu.SemaphoreType.DMA((2,)),
            pltpu.SemaphoreType.DMA((count,)),
            pltpu.SemaphoreType.DMA((count,)),
            pltpu.SemaphoreType.DMA((whole,)),
        ],
        compiler_params=pltpu.CompilerParams(vmem_limit_bytes=16 << 20),
        cost_estimate=pl.CostEstimate(
            flops=0, transcendentals=0, bytes_accessed=count * rows * (span + width) * 2
        ),
    )(footprint, offsets, block)


def add_kernel(sources, slots, first, last, *refs):
    windows, refs = refs[: len(sources)], refs[len(sources) :]
    azimuth, table, refs = refs[0], refs[1], refs[2:]
    if first:
        out, sub = refs
        sub[...] = jnp.zeros_like(sub)
    elif last:
        before, out, sub = refs
        sub[...] = before[...]
    else:
        before, out = refs
        sub = out
        sub[...] = before[...]
    me = lax.axis_index("tile")
    both = (windows[0].shape[1] - NOTE) // slots
    half = both // 2
    tiles = []
    for window in windows:
        note = window[0, slots * both :, :].astype(jnp.float32)
        for slot in range(slots):
            tile = jnp.max(note[:, slot * LANES : (slot + 1) * LANES])
            tiles.append(tile.astype(jnp.int32))
    for at, (window, (dy, dx, dc)) in enumerate(zip(windows, sources)):
        source = toward(me, dy, XS - dx, dc)
        for slot in range(slots):
            tile = tiles[at * slots + slot]
            x = window[0, slot * both : (slot + 1) * both]
            pr = jnp.dot(x, table[tile, 0], preferred_element_type=jnp.float32)
            pi = jnp.dot(x, table[tile, 1], preferred_element_type=jnp.float32)
            rr = (pr[:half] - pi[half:]).astype(x.dtype)
            ri = (pi[:half] + pr[half:]).astype(x.dtype)
            a = azimuth[tile, source]
            left = jnp.concatenate([a[0], a[1]], 1)
            sub[tile, 0] += jnp.dot(
                left, jnp.concatenate([rr, -ri], 0), preferred_element_type=jnp.float32
            )
            sub[tile, 1] += jnp.dot(
                left, jnp.concatenate([ri, rr], 0), preferred_element_type=jnp.float32
            )
    if last:
        rows = out.shape[3]
        for g in range(out.shape[0]):
            out[g] = sub[:, :, g * rows : (g + 1) * rows, :].astype(out.dtype)
    elif first:
        out[...] = sub[...]


def add(sources, slots, windows, azimuth, table, before, groups):
    tiles, _, parts, height, _ = azimuth.shape
    across = table.shape[3]
    whole = (tiles, parts, height, across)
    first, last = before is None, groups is not None
    shape = (groups, tiles, parts, height // groups, across) if last else whole
    operands = (*windows, azimuth, table) + (() if first else (before,))
    extra = first or last
    return pl.pallas_call(
        functools.partial(add_kernel, sources, slots, first, last),
        out_shape=jax.ShapeDtypeStruct(shape, jnp.bfloat16 if last else jnp.float32),
        in_specs=[VMEM] * len(operands),
        out_specs=VMEM,
        scratch_shapes=[pltpu.VMEM(whole, jnp.float32)] if extra else [],
        input_output_aliases={} if extra else {len(operands) - 1: 0},
        compiler_params=pltpu.CompilerParams(vmem_limit_bytes=16 << 20),
        cost_estimate=pl.CostEstimate(
            flops=len(sources) * 400_000_000, transcendentals=0, bytes_accessed=6_000_000
        ),
    )(*operands)


NOTE = 8
FLOWS = ((1, 2), (1, 1), (0, 3), (1, 3), (0, 1), (0, 2), (1, 0))
ROUNDS = ((0,), (1, 2), (3, 4), (5, 6))
AHEAD = 4


def after(x, y):
    return lax.optimization_barrier((x, y))


def on_device(pulses, footprint, offsets, azimuth, range_interp):
    held, _, width, _ = range_interp.shape
    owners = lax.axis_size("tile")
    subaps = lax.axis_size("subap")
    block = pulses.reshape(-1, pulses.shape[-1])
    footprint = footprint.reshape(-1)
    slots = footprint.shape[0] // owners
    azimuth = azimuth[:, :, 0]
    send = lambda x, dy, dx, dc: lax.ppermute(x, "tile", pairs(owners, dy, dx, dc))
    windows = []
    for at, flows in enumerate(ROUNDS):
        pieces = [(*FLOWS[f], (0, 1)) for f in flows]
        if at == 1:
            pieces += [(0, 0, (0,)), (0, 0, (1,))]
        made = cut_windows(pieces, footprint, offsets, block, held, slots, width)
        windows += made[: len(flows)]
        if at == 1:
            mine, other = made[len(flows) :]
            other = send(other, 0, 0, 1)
    got = []
    for f, w in enumerate(windows):
        if f >= AHEAD:
            w, got[f - AHEAD] = after(w, got[f - AHEAD])
        got.append(send(w, *FLOWS[f], 0))
    sub, ready, sources = None, [mine, other], [(0, 0, 0), (0, 0, 1)]
    for f, w in enumerate(got):
        dy, dx = FLOWS[f]
        passed = send(w[1:], 0, 0, 1)
        ready[0], w = after(ready[0], w)
        sub = add(sources, slots, ready, azimuth, range_interp, sub, None)
        if f + 1 < len(got):
            got[f + 1], sub = after(got[f + 1], sub)
        ready, sources = [w[:1], passed], [(dy, dx, 0), (dy, dx, 1)]
    sub = add(sources, slots, ready, azimuth, range_interp, sub, subaps)
    got = lax.all_to_all(sub, "subap", split_axis=0, concat_axis=0, tiled=True)
    raw = jnp.sum(got.astype(jnp.float32), axis=0)
    total = jnp.sum(raw * raw, axis=(1, 2, 3))
    hop = 1
    while hop < subaps:
        total = total + lax.ppermute(total, "subap", [(i, i ^ hop) for i in range(subaps)])
        hop *= 2
    power = total / (raw[0].size * subaps)
    return raw / jnp.sqrt(power + 1e-06)[:, None, None, None]


def solution(mesh):
    in_specs = (
        P("tile", "subap", None, None, None),
        P("tile", "subap", None),
        P(),
        P("tile", None, "subap", None, None, None),
        P("tile", None, None, None),
    )
    out_specs = P("tile", None, "subap", None)
    return jax.shard_map(
        on_device, mesh=mesh, in_specs=in_specs, out_specs=out_specs, check_vma=False
    )
```

time: 382 us -> 155 us (0.41)
  blocking collectives: 145 us -> 22.3 us
  local copies, waits for them, and re-layouts: 82.7 us -> 5.2 us
  Pallas kernels: 0 us -> 34 us
  other arithmetic: 30.7 us -> 1.03 us
  starting transfers between devices: 0.01 us -> 22.3 us
  waiting for transfers between devices: 90.3 us -> 68.2 us
  matrix products: 17.8 us -> 0 us
  between operations: 13.5 us -> 0.32 us
    all_to_all x1, blocking collectives: 145 us -> 22.3 us  [on_device(): got = lax.all_to_all(sub, 'subap', split_axis=0, concat_axis=0, tiled=True)]
    psum x1 -> x0, waiting for transfers between devices: 90.3 us -> none  [on_device(): raw = lax.psum(sub_image, 'subap')]
    ppermute x0 -> x18, waiting for transfers between devices: none -> 68.2 us  [the longest x15 56.3 us: on_device(): lax.ppermute(x, 'tile', pairs(owners, dy, dx, dc))]
    pallas_call x0 -> x12, Pallas kernels: none -> 34 us  [the longest x8 20.5 us: add(): pl.pallas_call(functools.partial(add_kernel, sources, slots, first, last)...]
    all_to_all x1 -> x0, local copies, waits for them, and re-layouts: 30.9 us -> none  [on_device(): lax.all_to_all(windows[:, None], 'tile', split_axis=0, concat_axis=1, til...]
    gather x1 -> x0, local copies, waits for them, and re-layouts: 30.5 us -> none  [cut(): return lax.dynamic_slice_in_dim(block, start, width, 2)]
    ppermute x0 -> x18, starting transfers between devices: none -> 22.3 us  [the longest x15 20.5 us: on_device(): lax.ppermute(x, 'tile', pairs(owners, dy, dx, dc))]
    dot_general x2 -> x0, matrix products: 17.8 us -> none  [the longest x1 14.4 us: on_device(): jnp.einsum('tkcpr,tdru->tkcdpu', arrived, range_interp, preferred_element...]
  transfers between devices with their start and end apart: 1 -> 18, of which waited for: 1 -> 7; matrix products, arithmetic and copies ran while one was open for 0% -> 0% of each run, Pallas kernels for 0% -> 19%
where the time goes in v2:
time: 155 us; the launch traced here: 153 us
  waiting for transfers between devices  68.2 us (44%)
  Pallas kernels  34 us (22%)
  starting transfers between devices  22.3 us (14%)
  blocking collectives  22.3 us (14%)
  local copies, waits for them, and re-layouts  5.2 us (3%)
    ppermute x15, waiting for transfers between devices, on_device(): lax.ppermute(x, 'tile', pairs(owners, dy, dx, dc))  56.3 us
    all_to_all x1, blocking collectives, on_device(): got = lax.all_to_all(sub, 'subap', split_axis=0, concat_axis=0, tiled=True)  22.3 us
    pallas_call x8, Pallas kernels, add(): pl.pallas_call(functools.partial(add_kernel, sources, slots, first, last)...  20.5 us
    ppermute x15, starting transfers between devices, on_device(): lax.ppermute(x, 'tile', pairs(owners, dy, dx, dc))  20.5 us
    pallas_call x4, Pallas kernels, cut_windows(): pl.pallas_call(functools.partial(cut_kernel, pieces, held), out_shape=[ja...  13.4 us
    ppermute x3, waiting for transfers between devices, on_device(): lax.ppermute(total, 'subap', [(i, i ^ hop) for i in range(subaps)])  11.8 us
    unnamed x12, local copies, waits for them, and re-layouts  4.7 us
  transfers between devices with their start and end apart: 18, of which 7 were waited for; matrix products, arithmetic and copies ran while one was open for 0% of the time, Pallas kernels for 19%

profile of v2, /device:TPU:0, one launch (start us, length us, event | category | flops | bytes accessed | tf_op | source)
XLA Modules:
  0.0 153.3 jit_solution(2992095336528069271)
XLA Ops:
  0.0 3.4 %copy-done = bf16[1,1,2,128,16384]{4,3,2,1,0:T(8,128)(2,1)S(1)} copy-done((bf16[1,1,2,128,16384]{4,3,2,1,0:T(8,128)(2,1)S(1)}, bf16[1,1,2,128,16384]{4,3,2,1,0:T(8,128)(2,1)}, u32[]{:S(2)}) %copy-start) | copy-done | bytes 8388632
  6.7 4.2 %collective-permute-start = (bf16[2,520,512]{2,1,0:T(8,128)(2,1)S(1)}, bf16[2,520,512]{2,1,0:T(8,128)(2,1)S(1)}, u32[]{:S(2)}, u32[]{:S(2)}) collective-permute-start(bf16[2,520,512]{2,1,0:T(8,128)(2,1)S(1)} %shard_map.57), channel_id=1, source_target_pairs={{0,96},{8,104},{16,112},{24,120},{32,64},{40,72},{48,80},{56,88},{... | collective-permute-start | bytes 3194888 | tf_op jit(solution)/shard_map/ppermute | solution.py:197
  10.9 4.8 %shard_map.55 = (bf16[2,520,512]{2,1,0:T(8,128)(2,1)S(1)}, bf16[2,520,512]{2,1,0:T(8,128)(2,1)S(1)}, bf16[1,520,512]{2,1,0:T(8,128)(2,1)S(1)}, bf16[1,520,512]{2,1,0:T(8,128)(2,1)S(1)}) custom-call(s32[32]{0:T(128)S(1)} %bitcast.18, s32[48]{0:T(128)S(1)} %copy-done.3, bf16[256,16384]{1,0:T(8,128)(2,1)S(1)} %bitcast.14), custom_call_target="tpu_custom_call" | custom-call | bytes 7077888 | tf_op jit(solution)/shard_map/pallas_call | solution.py:84
  16.2 2.6 %collective-permute-start.3 = (bf16[2,520,512]{2,1,0:T(8,128)(2,1)S(1)}, bf16[2,520,512]{2,1,0:T(8,128)(2,1)S(1)}, u32[]{:S(2)}, u32[]{:S(2)}) collective-permute-start(bf16[2,520,512]{2,1,0:T(8,128)(2,1)S(1)} %get-tuple-element.57), channel_id=1, source_target_pairs={{0,48},{8,56},{16,0},{24,8},{32,16},{40,24},{48,32},{56,40},{64,11... | collective-permute-start | bytes 3194888 | tf_op jit(solution)/shard_map/ppermute | solution.py:197
  18.8 3.4 %shard_map.56 = (bf16[2,520,512]{2,1,0:T(8,128)(2,1)S(1)}, bf16[2,520,512]{2,1,0:T(8,128)(2,1)S(1)}) custom-call(s32[32]{0:T(128)S(1)} %bitcast.19, s32[48]{0:T(128)S(1)} %copy-done.3, bf16[256,16384]{1,0:T(8,128)(2,1)S(1)} %bitcast.15), custom_call_target="tpu_custom_call" | custom-call | bytes 4718592 | tf_op jit(solution)/shard_map/pallas_call | solution.py:84
  22.2 13.4 %collective-permute-done = bf16[2,520,512]{2,1,0:T(8,128)(2,1)S(1)} collective-permute-done((bf16[2,520,512]{2,1,0:T(8,128)(2,1)S(1)}, bf16[2,520,512]{2,1,0:T(8,128)(2,1)S(1)}, u32[]{:S(2)}, u32[]{:S(2)}) %collective-permute-start) | collective-permute-done | bytes 1064992 | tf_op jit(solution)/shard_map/ppermute | solution.py:197
  35.7 5.2 %collective-permute-start.5 = (bf16[2,520,512]{2,1,0:T(8,128)(2,1)S(1)}, bf16[2,520,512]{2,1,0:T(8,128)(2,1)S(1)}, u32[]{:S(2)}, u32[]{:S(2)}) collective-permute-start(bf16[2,520,512]{2,1,0:T(8,128)(2,1)S(1)} %get-tuple-element.63), channel_id=1, source_target_pairs={{0,112},{8,120},{16,64},{24,72},{32,80},{40,88},{48,96},{56,104},{... | collective-permute-start | bytes 3194888 | tf_op jit(solution)/shard_map/ppermute | solution.py:197
  40.9 3.4 %shard_map.58 = (bf16[2,520,512]{2,1,0:T(8,128)(2,1)S(1)}, bf16[2,520,512]{2,1,0:T(8,128)(2,1)S(1)}) custom-call(s32[32]{0:T(128)S(1)} %bitcast.20, s32[48]{0:T(128)S(1)} %copy-done.3, bf16[256,16384]{1,0:T(8,128)(2,1)S(1)} %bitcast.16), custom_call_target="tpu_custom_call" | custom-call | bytes 4718592 | tf_op jit(solution)/shard_map/pallas_call | solution.py:84
  44.3 13.4 %collective-permute-done.1 = bf16[2,520,512]{2,1,0:T(8,128)(2,1)S(1)} collective-permute-done((bf16[2,520,512]{2,1,0:T(8,128)(2,1)S(1)}, bf16[2,520,512]{2,1,0:T(8,128)(2,1)S(1)}, u32[]{:S(2)}, u32[]{:S(2)}) %collective-permute-start.1) | collective-permute-done | bytes 1064992 | tf_op jit(solution)/shard_map/ppermute | solution.py:197
  59.0 2.6 %shard_map.59.refs_4_ = f32[3,2,256,256]{3,2,1,0:T(8,128)S(1)} custom-call(bf16[1,520,512]{2,1,0:T(8,128)(2,1)S(1)} %get-tuple-element.52.refs_0_, bf16[1,520,512]{2,1,0:T(8,128)(2,1)S(1)} %collective-permute-done.2.refs_1_, bf16[3,16,2,256,128]{4,3,2,1,0:T(8,128)(2,1)S(1)} %bitcast.5, bf16[3,2,512,256]{3,2,1,0:T(8,128)(2,1)S(1)} %copy-done.1), custom_call_target="tpu_custom_call" | custom-call | flops 800000000 | bytes 6000000 | tf_op jit(solution)/shard_map/pallas_call | solution.py:165
  61.8 2.6 %shard_map.60.refs_4_ = f32[3,2,256,256]{3,2,1,0:T(8,128)S(1)} custom-call(bf16[1,520,512]{2,1,0:T(8,128)(2,1)S(1)} %slice.42.refs_0_, bf16[1,520,512]{2,1,0:T(8,128)(2,1)S(1)} %collective-permute-done.4.refs_1_, bf16[3,16,2,256,128]{4,3,2,1,0:T(8,128)(2,1)S(1)} %bitcast.6, bf16[3,2,512,256]{3,2,1,0:T(8,128)(2,1)S(1)} %copy-done.1, ...), custom_call_target="tpu_custom_call", output_to_operand_aliasing={{}: (4, {})} | custom-call | flops 800000000 | bytes 6000000 | tf_op jit(solution)/shard_map/pallas_call | solution.py:165
  65.0 2.7 %collective-permute-start.9 = (bf16[2,520,512]{2,1,0:T(8,128)(2,1)S(1)}, bf16[2,520,512]{2,1,0:T(8,128)(2,1)S(1)}, u32[]{:S(2)}, u32[]{:S(2)}) collective-permute-start(bf16[2,520,512]{2,1,0:T(8,128)(2,1)S(1)} %get-tuple-element.73), channel_id=1, source_target_pairs={{0,32},{8,40},{16,48},{24,56},{32,0},{40,8},{48,16},{56,24},{64,96... | collective-permute-start | bytes 3194888 | tf_op jit(solution)/shard_map/ppermute | solution.py:197
  69.3 2.6 %shard_map.61.refs_4_ = f32[3,2,256,256]{3,2,1,0:T(8,128)S(1)} custom-call(bf16[1,520,512]{2,1,0:T(8,128)(2,1)S(1)} %slice.43.refs_0_, bf16[1,520,512]{2,1,0:T(8,128)(2,1)S(1)} %collective-permute-done.6.refs_1_, bf16[3,16,2,256,128]{4,3,2,1,0:T(8,128)(2,1)S(1)} %bitcast.7, bf16[3,2,512,256]{3,2,1,0:T(8,128)(2,1)S(1)} %copy-done.1, ...), custom_call_target="tpu_custom_call", output_to_operand_aliasing={{}: (4, {})} | custom-call | flops 800000000 | bytes 6000000 | tf_op jit(solution)/shard_map/pallas_call | solution.py:165
  71.9 9.5 %collective-permute-done.5 = bf16[2,520,512]{2,1,0:T(8,128)(2,1)S(1)} collective-permute-done((bf16[2,520,512]{2,1,0:T(8,128)(2,1)S(1)}, bf16[2,520,512]{2,1,0:T(8,128)(2,1)S(1)}, u32[]{:S(2)}, u32[]{:S(2)}) %collective-permute-start.5) | collective-permute-done | bytes 1064992 | tf_op jit(solution)/shard_map/ppermute | solution.py:197
  81.6 2.6 %shard_map.62.refs_4_ = f32[3,2,256,256]{3,2,1,0:T(8,128)S(1)} custom-call(bf16[1,520,512]{2,1,0:T(8,128)(2,1)S(1)} %slice.45.refs_0_, bf16[1,520,512]{2,1,0:T(8,128)(2,1)S(1)} %collective-permute-done.8.refs_1_, bf16[3,16,2,256,128]{4,3,2,1,0:T(8,128)(2,1)S(1)} %bitcast.8, bf16[3,2,512,256]{3,2,1,0:T(8,128)(2,1)S(1)} %copy-done.1, ...), custom_call_target="tpu_custom_call", output_to_operand_aliasing={{}: (4, {})} | custom-call | flops 800000000 | bytes 6000000 | tf_op jit(solution)/shard_map/pallas_call | solution.py:165
  85.1 2.6 %shard_map.63.refs_4_ = f32[3,2,256,256]{3,2,1,0:T(8,128)S(1)} custom-call(bf16[1,520,512]{2,1,0:T(8,128)(2,1)S(1)} %slice.47.refs_0_, bf16[1,520,512]{2,1,0:T(8,128)(2,1)S(1)} %collective-permute-done.10.refs_1_, bf16[3,16,2,256,128]{4,3,2,1,0:T(8,128)(2,1)S(1)} %bitcast.9, bf16[3,2,512,256]{3,2,1,0:T(8,128)(2,1)S(1)} %copy-done.1, ...), custom_call_target="tpu_custom_call", output_to_operand_aliasing={{}: (4, {})} | custom-call | flops 800000000 | bytes 6000000 | tf_op jit(solution)/shard_map/pallas_call | solution.py:165
  87.7 20.0 %collective-permute-done.9 = bf16[2,520,512]{2,1,0:T(8,128)(2,1)S(1)} collective-permute-done((bf16[2,520,512]{2,1,0:T(8,128)(2,1)S(1)}, bf16[2,520,512]{2,1,0:T(8,128)(2,1)S(1)}, u32[]{:S(2)}, u32[]{:S(2)}) %collective-permute-start.9) | collective-permute-done | bytes 1064992 | tf_op jit(solution)/shard_map/ppermute | solution.py:197
  107.9 2.6 %shard_map.64.refs_4_ = f32[3,2,256,256]{3,2,1,0:T(8,128)S(1)} custom-call(bf16[1,520,512]{2,1,0:T(8,128)(2,1)S(1)} %slice.49.refs_0_, bf16[1,520,512]{2,1,0:T(8,128)(2,1)S(1)} %collective-permute-done.12.refs_1_, bf16[3,16,2,256,128]{4,3,2,1,0:T(8,128)(2,1)S(1)} %bitcast.10, bf16[3,2,512,256]{3,2,1,0:T(8,128)(2,1)S(1)} %copy-done.1, ...), custom_call_target="tpu_custom_call", output_to_operand_aliasing={{}: (4, {})} | custom-call | flops 800000000 | bytes 6000000 | tf_op jit(solution)/shard_map/pallas_call | solution.py:165
  111.2 2.6 %shard_map.65.refs_4_ = f32[3,2,256,256]{3,2,1,0:T(8,128)S(1)} custom-call(bf16[1,520,512]{2,1,0:T(8,128)(2,1)S(1)} %slice.51.refs_0_, bf16[1,520,512]{2,1,0:T(8,128)(2,1)S(1)} %collective-permute-done.14.refs_1_, bf16[3,16,2,256,128]{4,3,2,1,0:T(8,128)(2,1)S(1)} %bitcast.11, bf16[3,2,512,256]{3,2,1,0:T(8,128)(2,1)S(1)} %copy-done.1, ...), custom_call_target="tpu_custom_call", output_to_operand_aliasing={{}: (4, {})} | custom-call | flops 800000000 | bytes 6000000 | tf_op jit(solution)/shard_map/pallas_call | solution.py:165
  113.8 2.5 %shard_map.66 = bf16[8,3,2,32,256]{4,3,2,1,0:T(8,128)(2,1)S(1)} custom-call(bf16[1,520,512]{2,1,0:T(8,128)(2,1)S(1)} %slice.53.refs_0_, bf16[1,520,512]{2,1,0:T(8,128)(2,1)S(1)} %collective-permute-done.13.refs_1_, bf16[3,16,2,256,128]{4,3,2,1,0:T(8,128)(2,1)S(1)} %bitcast.12, bf16[3,2,512,256]{3,2,1,0:T(8,128)(2,1)S(1)} %copy-done.1, ...), custom_call_target="tpu_custom_call" | custom-call | flops 800000000 | bytes 6000000 | tf_op jit(solution)/shard_map/pallas_call | solution.py:165
  116.3 22.3 %all_to_all.5 = bf16[8,3,2,32,256]{4,3,2,1,0:T(8,128)(2,1)S(1)} all-to-all(bf16[8,3,2,32,256]{4,3,2,1,0:T(8,128)(2,1)S(1)} %shard_map.66), channel_id=1, replica_groups=mesh['tile'=16,'subap'=8] {'subap'}, dimensions={0} | all-to-all | bytes 1572864 | tf_op jit(solution)/shard_map/all_to_all | solution.py:223
  139.1 3.3 %collective-permute-done.15 = f32[3]{0:T(128)S(1)} collective-permute-done((f32[3]{0:T(128)S(1)}, f32[3]{0:T(128)S(1)}, u32[]{:S(2)}, u32[]{:S(2)}) %collective-permute-start.15) | collective-permute-done | bytes 44 | tf_op jit(solution)/shard_map/ppermute | solution.py:228
  143.3 4.1 %collective-permute-done.16 = f32[3]{0:T(128)S(1)} collective-permute-done((f32[3]{0:T(128)S(1)}, f32[3]{0:T(128)S(1)}, u32[]{:S(2)}, u32[]{:S(2)}) %collective-permute-start.16) | collective-permute-done | bytes 44 | tf_op jit(solution)/shard_map/ppermute | solution.py:228
  148.1 4.3 %collective-permute-done.17 = f32[3]{0:T(128)S(1)} collective-permute-done((f32[3]{0:T(128)S(1)}, f32[3]{0:T(128)S(1)}, u32[]{:S(2)}, u32[]{:S(2)}) %collective-permute-start.17) | collective-permute-done | bytes 44 | tf_op jit(solution)/shard_map/ppermute | solution.py:228
  (58 shorter events, 12.4 us)
Async XLA Ops:
  0.0 3.4 %copy-start = (bf16[1,1,2,128,16384]{4,3,2,1,0:T(8,128)(2,1)S(1)}, bf16[1,1,2,128,16384]{4,3,2,1,0:T(8,128)(2,1)}, u32[]{:S(2)}) copy-start(bf16[1,1,2,128,16384]{4,3,2,1,0:T(8,128)(2,1)} %param.5) | copy-start | bytes 25165828
  3.4 0.7 copy-start.2
  4.0 0.7 copy-start.3
  6.7 28.9 %collective-permute-start = (bf16[2,520,512]{2,1,0:T(8,128)(2,1)S(1)}, bf16[2,520,512]{2,1,0:T(8,128)(2,1)S(1)}, u32[]{:S(2)}, u32[]{:S(2)}) collective-permute-start(bf16[2,520,512]{2,1,0:T(8,128)(2,1)S(1)} %shard_map.57), channel_id=1, source_target_pairs={{0,96},{8,104},{16,112},{24,120},{32,64},{40,72},{48,80},{56,88},{... | collective-permute-start | bytes 3194888 | tf_op jit(solution)/shard_map/ppermute | solution.py:197
  15.6 42.0 %collective-permute-start.1 = (bf16[2,520,512]{2,1,0:T(8,128)(2,1)S(1)}, bf16[2,520,512]{2,1,0:T(8,128)(2,1)S(1)}, u32[]{:S(2)}, u32[]{:S(2)}) collective-permute-start(bf16[2,520,512]{2,1,0:T(8,128)(2,1)S(1)} %get-tuple-element.50), channel_id=1, source_target_pairs={{0,80},{8,88},{16,96},{24,104},{32,112},{40,120},{48,64},{56,72},{... | collective-permute-start | bytes 3194888 | tf_op jit(solution)/shard_map/ppermute | solution.py:197
  16.2 45.6 %collective-permute-start.3 = (bf16[2,520,512]{2,1,0:T(8,128)(2,1)S(1)}, bf16[2,520,512]{2,1,0:T(8,128)(2,1)S(1)}, u32[]{:S(2)}, u32[]{:S(2)}) collective-permute-start(bf16[2,520,512]{2,1,0:T(8,128)(2,1)S(1)} %get-tuple-element.57), channel_id=1, source_target_pairs={{0,48},{8,56},{16,0},{24,8},{32,16},{40,24},{48,32},{56,40},{64,11... | collective-permute-start | bytes 3194888 | tf_op jit(solution)/shard_map/ppermute | solution.py:197
  18.8 40.2 %collective-permute-start.2 = (bf16[1,520,512]{2,1,0:T(8,128)(2,1)S(1)}, bf16[1,520,512]{2,1,0:T(8,128)(2,1)S(1)}, u32[]{:S(2)}, u32[]{:S(2)}) collective-permute-start(bf16[1,520,512]{2,1,0:T(8,128)(2,1)S(1)} %get-tuple-element.53), channel_id=1, source_target_pairs={{0,8},{8,0},{16,24},{24,16},{32,40},{40,32},{48,56},{56,48},{64,72... | collective-permute-start | bytes 1597448 | tf_op jit(solution)/shard_map/ppermute | solution.py:197
  18.8 40.2 %slice-start = ((s8[6291456]{0:T(1024)(128)(4,1)}), s8[4194304]{0:T(1024)(128)(4,1)S(1)}, s32[]{:S(2)}) async-start(s8[6291456]{0:T(1024)(128)(4,1)} %bitcast.3), calls=%async_computation.1 | async-start | bytes 8388608
  35.6 23.4 %slice-start.1 = ((s8[6291456]{0:T(1024)(128)(4,1)}), s8[2097152]{0:T(1024)(128)(4,1)S(1)}, s32[]{:S(2)}) async-start(s8[6291456]{0:T(1024)(128)(4,1)} %bitcast.3), calls=%async_computation.2 | async-start | bytes 4194304
  35.6 26.1 %collective-permute-start.4 = (bf16[1,520,512]{2,1,0:T(8,128)(2,1)S(1)}, bf16[1,520,512]{2,1,0:T(8,128)(2,1)S(1)}, u32[]{:S(2)}, u32[]{:S(2)}) collective-permute-start(bf16[1,520,512]{2,1,0:T(8,128)(2,1)S(1)} %slice.44), channel_id=1, source_target_pairs={{0,8},{8,0},{16,24},{24,16},{32,40},{40,32},{48,56},{56,48},{64,72... | collective-permute-start | bytes 1597448 | tf_op jit(solution)/shard_map/ppermute | solution.py:197
  35.7 45.7 %collective-permute-start.5 = (bf16[2,520,512]{2,1,0:T(8,128)(2,1)S(1)}, bf16[2,520,512]{2,1,0:T(8,128)(2,1)S(1)}, u32[]{:S(2)}, u32[]{:S(2)}) collective-permute-start(bf16[2,520,512]{2,1,0:T(8,128)(2,1)S(1)} %get-tuple-element.63), channel_id=1, source_target_pairs={{0,112},{8,120},{16,64},{24,72},{32,80},{40,88},{48,96},{56,104},{... | collective-permute-start | bytes 3194888 | tf_op jit(solution)/shard_map/ppermute | solution.py:197
  40.9 18.1 %copy-start.1 = (bf16[3,2,512,256]{3,2,1,0:T(8,128)(2,1)S(1)}, bf16[3,2,512,256]{3,2,1,0:T(8,128)(2,1)}, u32[]{:S(2)}) copy-start(bf16[3,2,512,256]{3,2,1,0:T(8,128)(2,1)} %refs_3_.15) | copy-start | bytes 4718596
  57.7 26.6 %collective-permute-start.7 = (bf16[2,520,512]{2,1,0:T(8,128)(2,1)S(1)}, bf16[2,520,512]{2,1,0:T(8,128)(2,1)S(1)}, u32[]{:S(2)}, u32[]{:S(2)}) collective-permute-start(bf16[2,520,512]{2,1,0:T(8,128)(2,1)S(1)} %get-tuple-element.68), channel_id=1, source_target_pairs={{0,16},{8,24},{16,32},{24,40},{32,48},{40,56},{48,0},{56,8},{64,80... | collective-permute-start | bytes 3194888 | tf_op jit(solution)/shard_map/ppermute | solution.py:197
  61.6 6.1 %collective-permute-start.6 = (bf16[1,520,512]{2,1,0:T(8,128)(2,1)S(1)}, bf16[1,520,512]{2,1,0:T(8,128)(2,1)S(1)}, u32[]{:S(2)}, u32[]{:S(2)}) collective-permute-start(bf16[1,520,512]{2,1,0:T(8,128)(2,1)S(1)} %slice.46), channel_id=1, source_target_pairs={{0,8},{8,0},{16,24},{24,16},{32,40},{40,32},{48,56},{56,48},{64,72... | collective-permute-start | bytes 1597448 | tf_op jit(solution)/shard_map/ppermute | solution.py:197
  64.4 17.2 %collective-permute-start.8 = (bf16[1,520,512]{2,1,0:T(8,128)(2,1)S(1)}, bf16[1,520,512]{2,1,0:T(8,128)(2,1)S(1)}, u32[]{:S(2)}, u32[]{:S(2)}) collective-permute-start(bf16[1,520,512]{2,1,0:T(8,128)(2,1)S(1)} %slice.48), channel_id=1, source_target_pairs={{0,8},{8,0},{16,24},{24,16},{32,40},{40,32},{48,56},{56,48},{64,72... | collective-permute-start | bytes 1597448 | tf_op jit(solution)/shard_map/ppermute | solution.py:197
  65.0 42.8 %collective-permute-start.9 = (bf16[2,520,512]{2,1,0:T(8,128)(2,1)S(1)}, bf16[2,520,512]{2,1,0:T(8,128)(2,1)S(1)}, u32[]{:S(2)}, u32[]{:S(2)}) collective-permute-start(bf16[2,520,512]{2,1,0:T(8,128)(2,1)S(1)} %get-tuple-element.73), channel_id=1, source_target_pairs={{0,32},{8,40},{16,48},{24,56},{32,0},{40,8},{48,16},{56,24},{64,96... | collective-permute-start | bytes 3194888 | tf_op jit(solution)/shard_map/ppermute | solution.py:197
  67.7 42.8 %collective-permute-start.11 = (bf16[2,520,512]{2,1,0:T(8,128)(2,1)S(1)}, bf16[2,520,512]{2,1,0:T(8,128)(2,1)S(1)}, u32[]{:S(2)}, u32[]{:S(2)}) collective-permute-start(bf16[2,520,512]{2,1,0:T(8,128)(2,1)S(1)} %get-tuple-element.78), channel_id=1, source_target_pairs={{0,64},{8,72},{16,80},{24,88},{32,96},{40,104},{48,112},{56,120},{... | collective-permute-start | bytes 3194888 | tf_op jit(solution)/shard_map/ppermute | solution.py:197
  81.5 3.6 %collective-permute-start.10 = (bf16[1,520,512]{2,1,0:T(8,128)(2,1)S(1)}, bf16[1,520,512]{2,1,0:T(8,128)(2,1)S(1)}, u32[]{:S(2)}, u32[]{:S(2)}) collective-permute-start(bf16[1,520,512]{2,1,0:T(8,128)(2,1)S(1)} %slice.50), channel_id=1, source_target_pairs={{0,8},{8,0},{16,24},{24,16},{32,40},{40,32},{48,56},{56,48},{64,72... | collective-permute-start | bytes 1597448 | tf_op jit(solution)/shard_map/ppermute | solution.py:197
  84.3 23.6 %collective-permute-start.12 = (bf16[1,520,512]{2,1,0:T(8,128)(2,1)S(1)}, bf16[1,520,512]{2,1,0:T(8,128)(2,1)S(1)}, u32[]{:S(2)}, u32[]{:S(2)}) collective-permute-start(bf16[1,520,512]{2,1,0:T(8,128)(2,1)S(1)} %slice.52), channel_id=1, source_target_pairs={{0,8},{8,0},{16,24},{24,16},{32,40},{40,32},{48,56},{56,48},{64,72... | collective-permute-start | bytes 1597448 | tf_op jit(solution)/shard_map/ppermute | solution.py:197
  107.8 3.4 %collective-permute-start.14 = (bf16[1,520,512]{2,1,0:T(8,128)(2,1)S(1)}, bf16[1,520,512]{2,1,0:T(8,128)(2,1)S(1)}, u32[]{:S(2)}, u32[]{:S(2)}) collective-permute-start(bf16[1,520,512]{2,1,0:T(8,128)(2,1)S(1)} %slice.55), channel_id=1, source_target_pairs={{0,8},{8,0},{16,24},{24,16},{32,40},{40,32},{48,56},{56,48},{64,72... | collective-permute-start | bytes 1597448 | tf_op jit(solution)/shard_map/ppermute | solution.py:197
  110.5 3.2 %collective-permute-start.13 = (bf16[1,520,512]{2,1,0:T(8,128)(2,1)S(1)}, bf16[1,520,512]{2,1,0:T(8,128)(2,1)S(1)}, u32[]{:S(2)}, u32[]{:S(2)}) collective-permute-start(bf16[1,520,512]{2,1,0:T(8,128)(2,1)S(1)} %slice.54), channel_id=1, source_target_pairs={{0,8},{8,0},{16,24},{24,16},{32,40},{40,32},{48,56},{56,48},{64,72... | collective-permute-start | bytes 1597448 | tf_op jit(solution)/shard_map/ppermute | solution.py:197
  138.8 3.6 %collective-permute-start.15 = (f32[3]{0:T(128)S(1)}, f32[3]{0:T(128)S(1)}, u32[]{:S(2)}, u32[]{:S(2)}) collective-permute-start(f32[3]{0:T(128)S(1)} %multiply_reduce_fusion), channel_id=1, source_target_pairs={{0,1},{1,0},{2,3},{3,2},{4,5},{5,4},{6,7},{7,6},{8,9},{9,8},{10,11... | collective-permute-start | bytes 44 | tf_op jit(solution)/shard_map/ppermute | solution.py:228
  142.4 5.0 %collective-permute-start.16 = (f32[3]{0:T(128)S(1)}, f32[3]{0:T(128)S(1)}, u32[]{:S(2)}, u32[]{:S(2)}) collective-permute-start(f32[3]{0:T(128)S(1)} %add.12), channel_id=1, source_target_pairs={{0,2},{1,3},{2,0},{3,1},{4,6},{5,7},{6,4},{7,5},{8,10},{9,11},{10,... | collective-permute-start | bytes 44 | tf_op jit(solution)/shard_map/ppermute | solution.py:228
  147.5 5.0 %collective-permute-start.17 = (f32[3]{0:T(128)S(1)}, f32[3]{0:T(128)S(1)}, u32[]{:S(2)}, u32[]{:S(2)}) collective-permute-start(f32[3]{0:T(128)S(1)} %add.13), channel_id=1, source_target_pairs={{0,4},{1,5},{2,6},{3,7},{4,0},{5,1},{6,2},{7,3},{8,12},{9,13},{10,... | collective-permute-start | bytes 44 | tf_op jit(solution)/shard_map/ppermute | solution.py:228

commit v3 on v2

v3 whole, which is shorter than its diff:
```python
import functools

import jax
import jax.numpy as jnp
from jax import lax
from jax.experimental import pallas as pl
from jax.experimental.pallas import tpu as pltpu
from jax.sharding import PartitionSpec as P

LANES = 128
XS, CORES = 4, 2
ANY = pl.BlockSpec(memory_space=pl.ANY)
HBM = pl.BlockSpec(memory_space=pltpu.HBM)
VMEM = pl.BlockSpec(memory_space=pltpu.VMEM)


def place(index):
    return index // (XS * CORES), index // CORES % XS, index % CORES


def toward(index, dy, dx, dc):
    y, x, c = place(index)
    return ((y ^ dy) * XS + (x + dx) % XS) * CORES + (c ^ dc)


def pairs(count, dy, dx, dc):
    return [(i, toward(i, dy, dx, dc)) for i in range(count)]


def cut_kernel(pieces, fills, held, footprint_hbm, offsets_hbm, block, *refs):
    swapped, refs = (refs[0], refs[1:]) if fills else (None, refs)
    outs, refs = refs[: len(pieces)], refs[len(pieces) :]
    footprint, offsets, wide, cut, note, scalar_sem, in_sem, out_sem, note_sem, fill_sem = refs
    scalars = [
        pltpu.make_async_copy(footprint_hbm, footprint, scalar_sem.at[0]),
        pltpu.make_async_copy(offsets_hbm, offsets, scalar_sem.at[1]),
    ]
    for copy in scalars:
        copy.start()
    filling = []
    for n, (source, piece, at) in enumerate(fills):
        filling.append(
            pltpu.make_async_copy(swapped.at[source], outs[piece].at[at], fill_sem.at[n])
        )
        filling[-1].start()
    me = lax.axis_index("tile")
    rows, span = wide.shape[1:]
    width = cut.shape[2]
    slots = outs[0].shape[1] // rows
    lane = lax.broadcasted_iota(jnp.int32, note.shape[1:], 1)
    for copy in scalars:
        copy.wait()
    steps, notes = [], []
    for out, parts in zip(outs, pieces):
        for at, to in parts:
            owner = toward(me, *to)
            ids = jnp.zeros(lane.shape, jnp.int32)
            for slot in range(slots):
                tile = footprint[owner * slots + slot]
                start = offsets[tile]
                base = jnp.minimum(start // LANES * LANES, block.shape[1] - span)
                i = len(steps)
                src = block.at[:, pl.ds(pl.multiple_of(base, LANES), span)]
                get = pltpu.make_async_copy(src, wide.at[i], in_sem.at[i])
                dst = out.at[at, slot * rows : (slot + 1) * rows]
                put = pltpu.make_async_copy(cut.at[i], dst, out_sem.at[i])
                get.start()
                steps.append((get, put, start - base))
                ids = jnp.where(lane // LANES == slot, tile - owner * held, ids)
            j = len(notes)
            note[j] = ids.astype(note.dtype)
            told = pltpu.make_async_copy(note.at[j], out.at[at, slots * rows :], note_sem.at[j])
            told.start()
            notes.append(told)
    for i, (get, put, shift) in enumerate(steps):
        get.wait()
        turned = pltpu.roll(wide[i].astype(jnp.float32), lax.rem(span - shift, span), 1)
        cut[i] = turned[:, :width].astype(cut.dtype)
        put.start()
    for _, put, _ in steps:
        put.wait()
    for copy in notes + filling:
        copy.wait()


def cut_windows(pieces, sizes, fills, footprint, offsets, block, held, slots, width, swapped=None):
    rows = block.shape[0]
    span = width + LANES
    whole = sum(len(parts) for parts in pieces)
    count = slots * whole
    operands = (footprint, offsets, block) + (() if swapped is None else (swapped,))
    return pl.pallas_call(
        functools.partial(cut_kernel, pieces, fills, held),
        out_shape=[
            jax.ShapeDtypeStruct((size, slots * rows + NOTE, width), block.dtype)
            for size in sizes
        ],
        in_specs=[HBM] * len(operands),
        out_specs=[ANY] * len(pieces),
        scratch_shapes=[
            pltpu.SMEM(footprint.shape, footprint.dtype),
            pltpu.SMEM(offsets.shape, offsets.dtype),
            pltpu.VMEM((count, rows, span), block.dtype),
            pltpu.VMEM((count, rows, width), block.dtype),
            pltpu.VMEM((whole, NOTE, width), block.dtype),
            pltpu.SemaphoreType.DMA((2,)),
            pltpu.SemaphoreType.DMA((count,)),
            pltpu.SemaphoreType.DMA((count,)),
            pltpu.SemaphoreType.DMA((whole,)),
            pltpu.SemaphoreType.DMA((max(len(fills), 1),)),
        ],
        compiler_params=pltpu.CompilerParams(vmem_limit_bytes=16 << 20),
        cost_estimate=pl.CostEstimate(
            flops=0, transcendentals=0, bytes_accessed=count * rows * (span + width) * 2
        ),
    )(*operands)


def add_kernel(sources, slots, first, last, *refs):
    count = len(sources)
    windows, refs = refs[:count], refs[count:]
    azimuth, table, refs = refs[0], refs[1], refs[2:]
    if first:
        (sub,) = refs
        sub[...] = jnp.zeros_like(sub)
    else:
        before, refs = refs[0], refs[1:]
        outs, sub = (refs[:-1], refs[-1]) if last else ((), refs[0])
        sub[...] = before[...]
    me = lax.axis_index("tile")
    both = (windows[0].shape[1] - NOTE) // slots
    half = both // 2
    work, packed = [], None
    for window, parts in zip(windows, sources):
        for at, (dy, dx, dc) in enumerate(parts):
            note = window[at, slots * both :, :].astype(jnp.float32)
            for slot in range(slots):
                ids = note[:, slot * LANES : (slot + 1) * LANES] * float(BASE ** len(work))
                packed = ids if packed is None else packed + ids
                x = (window, at, slice(slot * both, (slot + 1) * both))
                work.append((x, toward(me, dy, XS - dx, dc)))
    packed = jnp.max(packed).astype(jnp.int32)
    for n, ((window, at, span), source) in enumerate(work):
        tile = (packed >> (n * (BASE.bit_length() - 1))) & (BASE - 1)
        x = window[at, span]
        pr = jnp.dot(x, table[tile, 0], preferred_element_type=jnp.float32)
        pi = jnp.dot(x, table[tile, 1], preferred_element_type=jnp.float32)
        rr = (pr[:half] - pi[half:]).astype(x.dtype)
        ri = (pi[:half] + pr[half:]).astype(x.dtype)
        right = jnp.concatenate([rr, ri], 1)
        width = rr.shape[1]
        ar = jnp.dot(azimuth[tile, source, 0], right, preferred_element_type=jnp.float32)
        ai = jnp.dot(azimuth[tile, source, 1], right, preferred_element_type=jnp.float32)
        sub[tile, 0] += ar[:, :width] - ai[:, width:]
        sub[tile, 1] += ar[:, width:] + ai[:, :width]
    if last:
        z = lax.axis_index("subap") % ZS
        halves = sub.shape[2] // outs[0].shape[2] // ZS * 2
        rows = outs[0].shape[2] // halves
        for dz, out in enumerate(outs):
            for y in range(halves):
                at = pl.multiple_of(((z + dz) % ZS + y * ZS) * rows, rows)
                out[:, :, y * rows : (y + 1) * rows] = sub[:, :, pl.ds(at, rows)].astype(out.dtype)


def add(sources, slots, windows, azimuth, table, before, last):
    tiles, _, parts, height, _ = azimuth.shape
    whole = (tiles, parts, height, table.shape[3])
    first = before is None
    shape = jax.ShapeDtypeStruct(whole, jnp.float32)
    if last:
        cut = (tiles, parts, height // ZS, table.shape[3])
        shape = [
            jax.ShapeDtypeStruct(cut, jnp.bfloat16 if dz else jnp.float32) for dz in range(ZS)
        ]
    operands = (*windows, azimuth, table) + (() if first else (before,))
    return pl.pallas_call(
        functools.partial(add_kernel, sources, slots, first, last),
        out_shape=shape,
        in_specs=[VMEM] * len(operands),
        out_specs=[VMEM] * ZS if last else VMEM,
        scratch_shapes=[pltpu.VMEM(whole, jnp.float32)] if last else [],
        input_output_aliases={} if first or last else {len(operands) - 1: 0},
        compiler_params=pltpu.CompilerParams(vmem_limit_bytes=16 << 20),
        cost_estimate=pl.CostEstimate(
            flops=sum(len(p) for p in sources) * 400_000_000,
            transcendentals=0,
            bytes_accessed=6_000_000,
        ),
    )(*operands)


NOTE = 8
BASE = 4
ZS = 4
DIRECT = (1, 2)
FLOWS = ((1, 1), (0, 3), (0, 2), (1, 0), (1, 3), (0, 1))
EARLY = 3
AHEAD = 3


def after(x, y):
    return lax.optimization_barrier((x, y))


def on_device(pulses, footprint, offsets, azimuth, range_interp):
    held, _, width, _ = range_interp.shape
    owners = lax.axis_size("tile")
    pin = lambda x: pltpu.with_memory_space_constraint(x, pltpu.HBM)
    block = pin(pulses.reshape(-1, pulses.shape[-1]))
    footprint = pin(footprint.reshape(-1))
    slots = footprint.shape[0] // owners
    azimuth = azimuth[:, :, 0]
    send = lambda x, dy, dx, dc: lax.ppermute(x, "tile", pairs(owners, dy, dx, dc))
    cut = functools.partial(
        cut_windows,
        footprint=footprint,
        offsets=pin(offsets),
        block=block,
        held=held,
        slots=slots,
        width=width,
    )
    (first,) = cut([[(0, (*DIRECT, 0)), (1, (*DIRECT, 1))]], [2], [])
    first, cut.keywords["footprint"] = after(first, footprint)
    flows, made = [DIRECT], [first]
    for at, group in enumerate((FLOWS[:EARLY], FLOWS[EARLY:])):
        to = [(*f, 1) for f in group] + ([(0, 0, 1)] if at == 0 else [])
        (other,) = cut([list(enumerate(to))], [len(to)], [])
        other = send(other, 0, 0, 1)
        other, cut.keywords["footprint"] = after(other, cut.keywords["footprint"])
        to = [(*f, 0) for f in group] + ([(0, 0, 0)] if at == 0 else [])
        filled = cut(
            [[(0, t)] for t in to],
            [2] * len(to),
            [(n, n, 1) for n in range(len(to))],
            swapped=other,
        )
        flows += group
        made += filled[: len(group)]
        if at == 0:
            here = filled[-1]
    work = [([here], [[(0, 0, 0), (0, 0, 1)]])]
    sub, done = None, 0
    for f, (flow, w) in enumerate(zip(flows, made)):
        while done <= f - AHEAD:
            sub = add(work[done][1], slots, work[done][0], azimuth, range_interp, sub, False)
            done += 1
            w, sub = after(w, sub)
        w = send(w, *flow, 0)
        if f == 0:
            work.append(([w[:1], send(w[1:], 0, 0, 1)], [[(*flow, 0)], [(*flow, 1)]]))
        else:
            work.append(([w], [[(*flow, 0), (*flow, 1)]]))
    for windows, chips in work[done:-1]:
        sub = add(chips, slots, windows, azimuth, range_interp, sub, False)
    own, *away = add(work[-1][1], slots, work[-1][0], azimuth, range_interp, sub, True)

    subaps = lax.axis_size("subap")
    near = lambda x, dy, dz: lax.ppermute(
        x,
        "subap",
        [(i, (i // ZS ^ dy) * ZS + (i + dz) % ZS) for i in range(subaps)],
    )
    order = sorted(range(1, ZS), key=lambda dz: -min(dz, ZS - dz))
    for part in [near(away[dz - 1], 0, dz) for dz in order]:
        own = own + part.astype(jnp.float32)
    raw = own + near(own.astype(jnp.bfloat16), 1, 0).astype(jnp.float32)
    total = jnp.sum(raw * raw, axis=(1, 2, 3))
    total = total + sum(near(total, 0, dz) for dz in order)
    power = total / (raw[0].size * ZS)
    rows = raw.shape[2] // 2
    raw = lax.dynamic_slice_in_dim(raw, lax.axis_index("subap") // ZS * rows, rows, 2)
    return raw / jnp.sqrt(power + 1e-06)[:, None, None, None]


def solution(mesh):
    in_specs = (
        P("tile", "subap", None, None, None),
        P("tile", "subap", None),
        P(),
        P("tile", None, "subap", None, None, None),
        P("tile", None, None, None),
    )
    out_specs = P("tile", None, "subap", None)
    return jax.shard_map(
        on_device, mesh=mesh, in_specs=in_specs, out_specs=out_specs, check_vma=False
    )
```

time: 155 us -> 142 us (0.916)
  blocking collectives: 22.3 us -> 0 us
  starting transfers between devices: 22.3 us -> 34.8 us
  local copies, waits for them, and re-layouts: 5.2 us -> 0.08 us
  Pallas kernels: 34 us -> 37.2 us
  waiting for transfers between devices: 68.2 us -> 65.4 us
    all_to_all x1 -> x0, blocking collectives: 22.3 us -> none  [on_device(): got = lax.all_to_all(sub, 'subap', split_axis=0, concat_axis=0, tiled=True)]
    ppermute x3 -> x7, starting transfers between devices: 1.83 us -> 16 us  [on_device(): lax.ppermute(x, 'subap', [(i, (i // ZS ^ dy) * ZS + (i + dz) % ZS) for i...]
    pallas_call x4 -> x5, Pallas kernels: 13.4 us -> 18.4 us  [cut_windows(): pl.pallas_call(functools.partial(cut_kernel, pieces, fills, held), out_sh...]
    unnamed x12 -> x6, local copies, waits for them, and re-layouts: 4.7 us -> 0.02 us
    ppermute x15 -> x10, waiting for transfers between devices: 56.3 us -> 52.4 us  [on_device(): lax.ppermute(x, 'tile', pairs(owners, dy, dx, dc))]
    pallas_call x8, Pallas kernels: 20.5 us -> 18.7 us  [add(): pl.pallas_call(functools.partial(add_kernel, sources, slots, first, last)...]
    ppermute x15 -> x10, starting transfers between devices: 20.5 us -> 18.7 us  [on_device(): lax.ppermute(x, 'tile', pairs(owners, dy, dx, dc))]
    ppermute x3 -> x7, waiting for transfers between devices: 11.8 us -> 13 us  [on_device(): lax.ppermute(x, 'subap', [(i, (i // ZS ^ dy) * ZS + (i + dz) % ZS) for i...]
  transfers between devices with their start and end apart: 18 -> 17, of which waited for: 7 -> 10; matrix products, arithmetic and copies ran while one was open for 0% -> 0% of each run, Pallas kernels for 19% -> 20%
where the time goes in v3:
time: 142 us; the launch traced here: 139 us
  waiting for transfers between devices  65.4 us (46%)
  Pallas kernels  37.2 us (26%)
  starting transfers between devices  34.8 us (25%)
    ppermute x10, waiting for transfers between devices, on_device(): lax.ppermute(x, 'tile', pairs(owners, dy, dx, dc))  52.4 us
    ppermute x10, starting transfers between devices, on_device(): lax.ppermute(x, 'tile', pairs(owners, dy, dx, dc))  18.7 us
    pallas_call x8, Pallas kernels, add(): pl.pallas_call(functools.partial(add_kernel, sources, slots, first, last)...  18.7 us
    pallas_call x5, Pallas kernels, cut_windows(): pl.pallas_call(functools.partial(cut_kernel, pieces, fills, held), out_sh...  18.4 us
    ppermute x7, starting transfers between devices, on_device(): lax.ppermute(x, 'subap', [(i, (i // ZS ^ dy) * ZS + (i + dz) % ZS) for i...  16 us
    ppermute x7, waiting for transfers between devices, on_device(): lax.ppermute(x, 'subap', [(i, (i // ZS ^ dy) * ZS + (i + dz) % ZS) for i...  13 us
  transfers between devices with their start and end apart: 17, of which 10 were waited for; matrix products, arithmetic and copies ran while one was open for 0% of the time, Pallas kernels for 20%

profile of v3, /device:TPU:0, one launch (start us, length us, event | category | flops | bytes accessed | tf_op | source)
XLA Modules:
  0.0 138.8 jit_solution(13366604094157143689)
XLA Ops:
  0.0 2.8 %shard_map.55 = bf16[2,520,512]{2,1,0:T(8,128)(2,1)S(1)} custom-call(s32[32]{0:T(128)} %bitcast.18, s32[48]{0:T(128)} %offsets_hbm.9, bf16[256,16384]{1,0:T(8,128)(2,1)} %bitcast.13), custom_call_target="tpu_custom_call" | custom-call | bytes 2359296 | tf_op jit(solution)/shard_map/pallas_call | solution.py:92
  2.9 4.0 %shard_map.56 = bf16[4,520,512]{2,1,0:T(8,128)(2,1)S(1)} custom-call(s32[32]{0:T(128)} %bitcast.19, s32[48]{0:T(128)} %offsets_hbm.9, bf16[256,16384]{1,0:T(8,128)(2,1)} %bitcast.14), custom_call_target="tpu_custom_call" | custom-call | bytes 4718592 | tf_op jit(solution)/shard_map/pallas_call | solution.py:92
  7.0 4.2 %collective-permute-start.4 = (bf16[2,520,512]{2,1,0:T(8,128)(2,1)S(1)}, bf16[2,520,512]{2,1,0:T(8,128)(2,1)S(1)}, u32[]{:S(2)}, u32[]{:S(2)}) collective-permute-start(bf16[2,520,512]{2,1,0:T(8,128)(2,1)S(1)} %shard_map.55), channel_id=1, source_target_pairs={{0,96},{8,104},{16,112},{24,120},{32,64},{40,72},{48,80},{56,88},{... | collective-permute-start | bytes 3194888 | tf_op jit(solution)/shard_map/ppermute | solution.py:214
  11.2 4.0 %shard_map.57 = bf16[3,520,512]{2,1,0:T(8,128)(2,1)S(1)} custom-call(s32[32]{0:T(128)} %bitcast.20, s32[48]{0:T(128)} %offsets_hbm.9, bf16[256,16384]{1,0:T(8,128)(2,1)} %bitcast.15), custom_call_target="tpu_custom_call" | custom-call | bytes 3538944 | tf_op jit(solution)/shard_map/pallas_call | solution.py:92
  15.4 4.2 %shard_map.59 = (bf16[2,520,512]{2,1,0:T(8,128)(2,1)S(1)}, bf16[2,520,512]{2,1,0:T(8,128)(2,1)S(1)}, bf16[2,520,512]{2,1,0:T(8,128)(2,1)S(1)}, bf16[2,520,512]{2,1,0:T(8,128)(2,1)S(1)}) custom-call(s32[32]{0:T(128)} %bitcast.21, s32[48]{0:T(128)} %offsets_hbm.9, bf16[256,16384]{1,0:T(8,128)(2,1)} %bitcast.16, ...), custom_call_target="tpu_custom_call" | custom-call | bytes 4718592 | tf_op jit(solution)/shard_map/pallas_call | solution.py:92
  19.6 2.6 %collective-permute-start.3 = (bf16[2,520,512]{2,1,0:T(8,128)(2,1)S(1)}, bf16[2,520,512]{2,1,0:T(8,128)(2,1)S(1)}, u32[]{:S(2)}, u32[]{:S(2)}) collective-permute-start(bf16[2,520,512]{2,1,0:T(8,128)(2,1)S(1)} %get-tuple-element.38), channel_id=1, source_target_pairs={{0,80},{8,88},{16,96},{24,104},{32,112},{40,120},{48,64},{56,72},{... | collective-permute-start | bytes 3194888 | tf_op jit(solution)/shard_map/ppermute | solution.py:214
  24.0 11.9 %collective-permute-done.4 = bf16[2,520,512]{2,1,0:T(8,128)(2,1)S(1)} collective-permute-done((bf16[2,520,512]{2,1,0:T(8,128)(2,1)S(1)}, bf16[2,520,512]{2,1,0:T(8,128)(2,1)S(1)}, u32[]{:S(2)}, u32[]{:S(2)}) %collective-permute-start.4) | collective-permute-done | bytes 1064992 | tf_op jit(solution)/shard_map/ppermute | solution.py:214
  38.2 3.4 %collective-permute-start.9 = (bf16[2,520,512]{2,1,0:T(8,128)(2,1)S(1)}, bf16[2,520,512]{2,1,0:T(8,128)(2,1)S(1)}, u32[]{:S(2)}, u32[]{:S(2)}) collective-permute-start(bf16[2,520,512]{2,1,0:T(8,128)(2,1)S(1)} %get-tuple-element.49), channel_id=1, source_target_pairs={{0,32},{8,40},{16,48},{24,56},{32,0},{40,8},{48,16},{56,24},{64,96... | collective-permute-start | bytes 3194888 | tf_op jit(solution)/shard_map/ppermute | solution.py:214
  41.6 2.4 %shard_map.61.refs_3_ = f32[3,2,256,256]{3,2,1,0:T(8,128)S(1)} custom-call(bf16[1,520,512]{2,1,0:T(8,128)(2,1)S(1)} %get-tuple-element.58.refs_0_, bf16[1,520,512]{2,1,0:T(8,128)(2,1)S(1)} %collective-permute-done.5.refs_1_, bf16[3,16,2,256,128]{4,3,2,1,0:T(8,128)(2,1)S(1)} %bitcast.6, ...), custom_call_target="tpu_custom_call", output_to_operand_aliasing={{}: (4, {})} | custom-call | flops 800000000 | bytes 6000000 | tf_op jit(solution)/shard_map/pallas_call | solution.py:177
  44.0 3.5 %shard_map.58 = (bf16[2,520,512]{2,1,0:T(8,128)(2,1)S(1)}, bf16[2,520,512]{2,1,0:T(8,128)(2,1)S(1)}, bf16[2,520,512]{2,1,0:T(8,128)(2,1)S(1)}) custom-call(s32[32]{0:T(128)} %bitcast.22, s32[48]{0:T(128)} %offsets_hbm.9, bf16[256,16384]{1,0:T(8,128)(2,1)} %bitcast.17, bf16[3,520,512]{2,1,0:T(8,128)(2,1)S(1)} %collective-permute-done.1.refs_0_), custom_call_target="tpu_custom_call" | custom-call | bytes 3538944 | tf_op jit(solution)/shard_map/pallas_call | solution.py:92
  49.1 9.1 %collective-permute-done.3.refs_0_ = bf16[2,520,512]{2,1,0:T(8,128)(2,1)S(1)} collective-permute-done((bf16[2,520,512]{2,1,0:T(8,128)(2,1)S(1)}, bf16[2,520,512]{2,1,0:T(8,128)(2,1)S(1)}, u32[]{:S(2)}, u32[]{:S(2)}) %collective-permute-start.3) | collective-permute-done | bytes 1064992 | tf_op jit(solution)/shard_map/ppermute | solution.py:214
  60.6 4.4 %collective-permute-start.7 = (bf16[2,520,512]{2,1,0:T(8,128)(2,1)S(1)}, bf16[2,520,512]{2,1,0:T(8,128)(2,1)S(1)}, u32[]{:S(2)}, u32[]{:S(2)}) collective-permute-start(bf16[2,520,512]{2,1,0:T(8,128)(2,1)S(1)} %get-tuple-element.47), channel_id=1, source_target_pairs={{0,112},{8,120},{16,64},{24,72},{32,80},{40,88},{48,96},{56,104},{... | collective-permute-start | bytes 3194888 | tf_op jit(solution)/shard_map/ppermute | solution.py:214
  65.1 2.4 %shard_map.63.refs_3_ = f32[3,2,256,256]{3,2,1,0:T(8,128)S(1)} custom-call(bf16[2,520,512]{2,1,0:T(8,128)(2,1)S(1)} %collective-permute-done.2.refs_0_, bf16[3,16,2,256,128]{4,3,2,1,0:T(8,128)(2,1)S(1)} %bitcast.8, bf16[3,2,512,256]{3,2,1,0:T(8,128)(2,1)S(1)} %copy-done, f32[3,2,256,256]{3,2,1,0:T(8,128)S(1)} %shard_map.62.refs_3_), custom_call_target="tpu_custom_call", output_to_operand_aliasing={{}: (3, {})} | custom-call | flops 800000000 | bytes 6000000 | tf_op jit(solution)/shard_map/pallas_call | solution.py:177
  67.8 16.2 %collective-permute-done.9.refs_0_ = bf16[2,520,512]{2,1,0:T(8,128)(2,1)S(1)} collective-permute-done((bf16[2,520,512]{2,1,0:T(8,128)(2,1)S(1)}, bf16[2,520,512]{2,1,0:T(8,128)(2,1)S(1)}, u32[]{:S(2)}, u32[]{:S(2)}) %collective-permute-start.9) | collective-permute-done | bytes 1064992 | tf_op jit(solution)/shard_map/ppermute | solution.py:214
  84.0 2.4 %shard_map.64.refs_3_ = f32[3,2,256,256]{3,2,1,0:T(8,128)S(1)} custom-call(bf16[2,520,512]{2,1,0:T(8,128)(2,1)S(1)} %collective-permute-done.9.refs_0_, bf16[3,16,2,256,128]{4,3,2,1,0:T(8,128)(2,1)S(1)} %bitcast.9, bf16[3,2,512,256]{3,2,1,0:T(8,128)(2,1)S(1)} %copy-done, f32[3,2,256,256]{3,2,1,0:T(8,128)S(1)} %shard_map.63.refs_3_), custom_call_target="tpu_custom_call", output_to_operand_aliasing={{}: (3, {})} | custom-call | flops 800000000 | bytes 6000000 | tf_op jit(solution)/shard_map/pallas_call | solution.py:177
  86.4 2.4 %shard_map.65.refs_3_ = f32[3,2,256,256]{3,2,1,0:T(8,128)S(1)} custom-call(bf16[2,520,512]{2,1,0:T(8,128)(2,1)S(1)} %collective-permute-done.8.refs_0_, bf16[3,16,2,256,128]{4,3,2,1,0:T(8,128)(2,1)S(1)} %bitcast.10, bf16[3,2,512,256]{3,2,1,0:T(8,128)(2,1)S(1)} %copy-done, f32[3,2,256,256]{3,2,1,0:T(8,128)S(1)} %shard_map.64.refs_3_), custom_call_target="tpu_custom_call", output_to_operand_aliasing={{}: (3, {})} | custom-call | flops 800000000 | bytes 6000000 | tf_op jit(solution)/shard_map/pallas_call | solution.py:177
  88.8 15.2 %collective-permute-done.7.refs_0_ = bf16[2,520,512]{2,1,0:T(8,128)(2,1)S(1)} collective-permute-done((bf16[2,520,512]{2,1,0:T(8,128)(2,1)S(1)}, bf16[2,520,512]{2,1,0:T(8,128)(2,1)S(1)}, u32[]{:S(2)}, u32[]{:S(2)}) %collective-permute-start.7) | collective-permute-done | bytes 1064992 | tf_op jit(solution)/shard_map/ppermute | solution.py:214
  104.0 2.4 %shard_map.66.refs_3_ = f32[3,2,256,256]{3,2,1,0:T(8,128)S(1)} custom-call(bf16[2,520,512]{2,1,0:T(8,128)(2,1)S(1)} %collective-permute-done.7.refs_0_, bf16[3,16,2,256,128]{4,3,2,1,0:T(8,128)(2,1)S(1)} %bitcast.11, bf16[3,2,512,256]{3,2,1,0:T(8,128)(2,1)S(1)} %copy-done, f32[3,2,256,256]{3,2,1,0:T(8,128)S(1)} %shard_map.65.refs_3_), custom_call_target="tpu_custom_call", output_to_operand_aliasing={{}: (3, {})} | custom-call | flops 800000000 | bytes 6000000 | tf_op jit(solution)/shard_map/pallas_call | solution.py:177
  108.7 4.0 %collective-permute-start.10 = (bf16[3,2,64,256]{3,2,1,0:T(8,128)(2,1)S(1)}, bf16[3,2,64,256]{3,2,1,0:T(8,128)(2,1)S(1)}, u32[]{:S(2)}, u32[]{:S(2)}) collective-permute-start(bf16[3,2,64,256]{3,2,1,0:T(8,128)(2,1)S(1)} %get-tuple-element.52), channel_id=1, source_target_pairs={{0,2},{1,3},{2,0},{3,1},{4,6},{5,7},{6,4},{7,5},{8,10},{9,11},{10,... | collective-permute-start | bytes 589832 | tf_op jit(solution)/shard_map/ppermute | solution.py:260
  115.8 2.5 %collective-permute-done.10 = bf16[3,2,64,256]{3,2,1,0:T(8,128)(2,1)S(1)} collective-permute-done((bf16[3,2,64,256]{3,2,1,0:T(8,128)(2,1)S(1)}, bf16[3,2,64,256]{3,2,1,0:T(8,128)(2,1)S(1)}, u32[]{:S(2)}, u32[]{:S(2)}) %collective-permute-start.10) | collective-permute-done | bytes 196640 | tf_op jit(solution)/shard_map/ppermute | solution.py:260
  118.3 3.4 %collective-permute-done.11 = bf16[3,2,64,256]{3,2,1,0:T(8,128)(2,1)S(1)} collective-permute-done((bf16[3,2,64,256]{3,2,1,0:T(8,128)(2,1)S(1)}, bf16[3,2,64,256]{3,2,1,0:T(8,128)(2,1)S(1)}, u32[]{:S(2)}, u32[]{:S(2)}) %collective-permute-start.11) | collective-permute-done | bytes 196640 | tf_op jit(solution)/shard_map/ppermute | solution.py:260
  122.6 3.0 %collective-permute-start.13 = (bf16[3,2,64,256]{3,2,1,0:T(8,128)(2,1)S(1)}, bf16[3,2,64,256]{3,2,1,0:T(8,128)(2,1)S(1)}, u32[]{:S(2)}, u32[]{:S(2)}) collective-permute-start(bf16[3,2,64,256]{3,2,1,0:T(8,128)(2,1)S(1)} %fusion), channel_id=1, source_target_pairs={{0,4},{1,5},{2,6},{3,7},{4,0},{5,1},{6,2},{7,3},{8,12},{9,13},{10,... | collective-permute-start | bytes 589832 | tf_op jit(solution)/shard_map/ppermute | solution.py:260
  125.6 4.4 %collective-permute-done.13 = bf16[3,2,64,256]{3,2,1,0:T(8,128)(2,1)S(1)} collective-permute-done((bf16[3,2,64,256]{3,2,1,0:T(8,128)(2,1)S(1)}, bf16[3,2,64,256]{3,2,1,0:T(8,128)(2,1)S(1)}, u32[]{:S(2)}, u32[]{:S(2)}) %collective-permute-start.13) | collective-permute-done | bytes 196640 | tf_op jit(solution)/shard_map/ppermute | solution.py:260
  130.3 2.6 %collective-permute-start.14 = (f32[3]{0:T(128)S(1)}, f32[3]{0:T(128)S(1)}, u32[]{:S(2)}, u32[]{:S(2)}) collective-permute-start(f32[3]{0:T(128)S(1)} %get-tuple-element.55), channel_id=1, source_target_pairs={{0,2},{1,3},{2,0},{3,1},{4,6},{5,7},{6,4},{7,5},{8,10},{9,11},{10,... | collective-permute-start | bytes 44 | tf_op jit(solution)/shard_map/ppermute | solution.py:260
  (35 shorter events, 21.2 us)
Async XLA Ops:
  6.9 4.3 %collective-permute-start = (bf16[4,520,512]{2,1,0:T(8,128)(2,1)S(1)}, bf16[4,520,512]{2,1,0:T(8,128)(2,1)S(1)}, u32[]{:S(2)}, u32[]{:S(2)}) collective-permute-start(bf16[4,520,512]{2,1,0:T(8,128)(2,1)S(1)} %shard_map.56), channel_id=1, source_target_pairs={{0,8},{8,0},{16,24},{24,16},{32,40},{40,32},{48,56},{56,48},{64,72... | collective-permute-start | bytes 6389768 | tf_op jit(solution)/shard_map/ppermute | solution.py:214
  7.0 28.8 %collective-permute-start.4 = (bf16[2,520,512]{2,1,0:T(8,128)(2,1)S(1)}, bf16[2,520,512]{2,1,0:T(8,128)(2,1)S(1)}, u32[]{:S(2)}, u32[]{:S(2)}) collective-permute-start(bf16[2,520,512]{2,1,0:T(8,128)(2,1)S(1)} %shard_map.55), channel_id=1, source_target_pairs={{0,96},{8,104},{16,112},{24,120},{32,64},{40,72},{48,80},{56,88},{... | collective-permute-start | bytes 3194888 | tf_op jit(solution)/shard_map/ppermute | solution.py:214
  11.2 24.8 %slice-start = ((s8[6291456]{0:T(1024)(128)(4,1)}), s8[4194304]{0:T(1024)(128)(4,1)S(1)}, s32[]{:S(2)}) async-start(s8[6291456]{0:T(1024)(128)(4,1)} %bitcast.3), calls=%async_computation | async-start | bytes 8388608
  15.1 20.8 %slice-start.1 = ((s8[6291456]{0:T(1024)(128)(4,1)}), s8[2097152]{0:T(1024)(128)(4,1)S(1)}, s32[]{:S(2)}) async-start(s8[6291456]{0:T(1024)(128)(4,1)} %bitcast.3), calls=%async_computation.1 | async-start | bytes 4194304
  15.2 28.8 %collective-permute-start.1 = (bf16[3,520,512]{2,1,0:T(8,128)(2,1)S(1)}, bf16[3,520,512]{2,1,0:T(8,128)(2,1)S(1)}, u32[]{:S(2)}, u32[]{:S(2)}) collective-permute-start(bf16[3,520,512]{2,1,0:T(8,128)(2,1)S(1)} %shard_map.57), channel_id=1, source_target_pairs={{0,8},{8,0},{16,24},{24,16},{32,40},{40,32},{48,56},{56,48},{64,72... | collective-permute-start | bytes 4792328 | tf_op jit(solution)/shard_map/ppermute | solution.py:214
  19.6 38.7 %collective-permute-start.3 = (bf16[2,520,512]{2,1,0:T(8,128)(2,1)S(1)}, bf16[2,520,512]{2,1,0:T(8,128)(2,1)S(1)}, u32[]{:S(2)}, u32[]{:S(2)}) collective-permute-start(bf16[2,520,512]{2,1,0:T(8,128)(2,1)S(1)} %get-tuple-element.38), channel_id=1, source_target_pairs={{0,80},{8,88},{16,96},{24,104},{32,112},{40,120},{48,64},{56,72},{... | collective-permute-start | bytes 3194888 | tf_op jit(solution)/shard_map/ppermute | solution.py:214
  22.2 13.8 %copy-start = (bf16[3,2,512,256]{3,2,1,0:T(8,128)(2,1)S(1)}, bf16[3,2,512,256]{3,2,1,0:T(8,128)(2,1)}, u32[]{:S(2)}) copy-start(bf16[3,2,512,256]{3,2,1,0:T(8,128)(2,1)} %refs_2_.13) | copy-start | bytes 4718596
  22.2 42.8 %collective-permute-start.2 = (bf16[2,520,512]{2,1,0:T(8,128)(2,1)S(1)}, bf16[2,520,512]{2,1,0:T(8,128)(2,1)S(1)}, u32[]{:S(2)}, u32[]{:S(2)}) collective-permute-start(bf16[2,520,512]{2,1,0:T(8,128)(2,1)S(1)} %get-tuple-element.36), channel_id=1, source_target_pairs={{0,48},{8,56},{16,0},{24,8},{32,16},{40,24},{48,32},{56,40},{64,11... | collective-permute-start | bytes 3194888 | tf_op jit(solution)/shard_map/ppermute | solution.py:214
  35.9 5.7 %collective-permute-start.5 = (bf16[1,520,512]{2,1,0:T(8,128)(2,1)S(1)}, bf16[1,520,512]{2,1,0:T(8,128)(2,1)S(1)}, u32[]{:S(2)}, u32[]{:S(2)}) collective-permute-start(bf16[1,520,512]{2,1,0:T(8,128)(2,1)S(1)} %get-tuple-element.57), channel_id=1, source_target_pairs={{0,8},{8,0},{16,24},{24,16},{32,40},{40,32},{48,56},{56,48},{64,72... | collective-permute-start | bytes 1597448 | tf_op jit(solution)/shard_map/ppermute | solution.py:214
  38.2 45.8 %collective-permute-start.9 = (bf16[2,520,512]{2,1,0:T(8,128)(2,1)S(1)}, bf16[2,520,512]{2,1,0:T(8,128)(2,1)S(1)}, u32[]{:S(2)}, u32[]{:S(2)}) collective-permute-start(bf16[2,520,512]{2,1,0:T(8,128)(2,1)S(1)} %get-tuple-element.49), channel_id=1, source_target_pairs={{0,32},{8,40},{16,48},{24,56},{32,0},{40,8},{48,16},{56,24},{64,96... | collective-permute-start | bytes 3194888 | tf_op jit(solution)/shard_map/ppermute | solution.py:214
  47.4 39.0 %collective-permute-start.8 = (bf16[2,520,512]{2,1,0:T(8,128)(2,1)S(1)}, bf16[2,520,512]{2,1,0:T(8,128)(2,1)S(1)}, u32[]{:S(2)}, u32[]{:S(2)}) collective-permute-start(bf16[2,520,512]{2,1,0:T(8,128)(2,1)S(1)} %get-tuple-element.48), channel_id=1, source_target_pairs={{0,64},{8,72},{16,80},{24,88},{32,96},{40,104},{48,112},{56,120},{... | collective-permute-start | bytes 3194888 | tf_op jit(solution)/shard_map/ppermute | solution.py:214
  60.6 43.4 %collective-permute-start.7 = (bf16[2,520,512]{2,1,0:T(8,128)(2,1)S(1)}, bf16[2,520,512]{2,1,0:T(8,128)(2,1)S(1)}, u32[]{:S(2)}, u32[]{:S(2)}) collective-permute-start(bf16[2,520,512]{2,1,0:T(8,128)(2,1)S(1)} %get-tuple-element.47), channel_id=1, source_target_pairs={{0,112},{8,120},{16,64},{24,72},{32,80},{40,88},{48,96},{56,104},{... | collective-permute-start | bytes 3194888 | tf_op jit(solution)/shard_map/ppermute | solution.py:214
  67.5 39.0 %collective-permute-start.6 = (bf16[2,520,512]{2,1,0:T(8,128)(2,1)S(1)}, bf16[2,520,512]{2,1,0:T(8,128)(2,1)S(1)}, u32[]{:S(2)}, u32[]{:S(2)}) collective-permute-start(bf16[2,520,512]{2,1,0:T(8,128)(2,1)S(1)} %get-tuple-element.46), channel_id=1, source_target_pairs={{0,16},{8,24},{16,32},{24,40},{32,48},{40,56},{48,0},{56,8},{64,80... | collective-permute-start | bytes 3194888 | tf_op jit(solution)/shard_map/ppermute | solution.py:214
  108.7 9.7 %collective-permute-start.10 = (bf16[3,2,64,256]{3,2,1,0:T(8,128)(2,1)S(1)}, bf16[3,2,64,256]{3,2,1,0:T(8,128)(2,1)S(1)}, u32[]{:S(2)}, u32[]{:S(2)}) collective-permute-start(bf16[3,2,64,256]{3,2,1,0:T(8,128)(2,1)S(1)} %get-tuple-element.52), channel_id=1, source_target_pairs={{0,2},{1,3},{2,0},{3,1},{4,6},{5,7},{6,4},{7,5},{8,10},{9,11},{10,... | collective-permute-start | bytes 589832 | tf_op jit(solution)/shard_map/ppermute | solution.py:260
  112.6 9.2 %collective-permute-start.11 = (bf16[3,2,64,256]{3,2,1,0:T(8,128)(2,1)S(1)}, bf16[3,2,64,256]{3,2,1,0:T(8,128)(2,1)S(1)}, u32[]{:S(2)}, u32[]{:S(2)}) collective-permute-start(bf16[3,2,64,256]{3,2,1,0:T(8,128)(2,1)S(1)} %get-tuple-element.53), channel_id=1, source_target_pairs={{0,1},{1,2},{2,3},{3,0},{4,5},{5,6},{6,7},{7,4},{8,9},{9,10},{10,1... | collective-permute-start | bytes 589832 | tf_op jit(solution)/shard_map/ppermute | solution.py:260
  113.6 8.9 %collective-permute-start.12 = (bf16[3,2,64,256]{3,2,1,0:T(8,128)(2,1)S(1)}, bf16[3,2,64,256]{3,2,1,0:T(8,128)(2,1)S(1)}, u32[]{:S(2)}, u32[]{:S(2)}) collective-permute-start(bf16[3,2,64,256]{3,2,1,0:T(8,128)(2,1)S(1)} %get-tuple-element.54), channel_id=1, source_target_pairs={{0,3},{1,0},{2,1},{3,2},{4,7},{5,4},{6,5},{7,6},{8,11},{9,8},{10,9... | collective-permute-start | bytes 589832 | tf_op jit(solution)/shard_map/ppermute | solution.py:260
  122.6 7.5 %collective-permute-start.13 = (bf16[3,2,64,256]{3,2,1,0:T(8,128)(2,1)S(1)}, bf16[3,2,64,256]{3,2,1,0:T(8,128)(2,1)S(1)}, u32[]{:S(2)}, u32[]{:S(2)}) collective-permute-start(bf16[3,2,64,256]{3,2,1,0:T(8,128)(2,1)S(1)} %fusion), channel_id=1, source_target_pairs={{0,4},{1,5},{2,6},{3,7},{4,0},{5,1},{6,2},{7,3},{8,12},{9,13},{10,... | collective-permute-start | bytes 589832 | tf_op jit(solution)/shard_map/ppermute | solution.py:260
  130.3 5.8 %collective-permute-start.14 = (f32[3]{0:T(128)S(1)}, f32[3]{0:T(128)S(1)}, u32[]{:S(2)}, u32[]{:S(2)}) collective-permute-start(f32[3]{0:T(128)S(1)} %get-tuple-element.55), channel_id=1, source_target_pairs={{0,2},{1,3},{2,0},{3,1},{4,6},{5,7},{6,4},{7,5},{8,10},{9,11},{10,... | collective-permute-start | bytes 44 | tf_op jit(solution)/shard_map/ppermute | solution.py:260
  132.9 4.8 %collective-permute-start.15 = (f32[3]{0:T(128)S(1)}, f32[3]{0:T(128)S(1)}, u32[]{:S(2)}, u32[]{:S(2)}) collective-permute-start(f32[3]{0:T(128)S(1)} %get-tuple-element.55), channel_id=1, source_target_pairs={{0,1},{1,2},{2,3},{3,0},{4,5},{5,6},{6,7},{7,4},{8,9},{9,10},{10,1... | collective-permute-start | bytes 44 | tf_op jit(solution)/shard_map/ppermute | solution.py:260
  134.4 3.5 %collective-permute-start.16 = (f32[3]{0:T(128)S(1)}, f32[3]{0:T(128)S(1)}, u32[]{:S(2)}, u32[]{:S(2)}) collective-permute-start(f32[3]{0:T(128)S(1)} %get-tuple-element.55), channel_id=1, source_target_pairs={{0,3},{1,0},{2,1},{3,2},{4,7},{5,4},{6,5},{7,6},{8,11},{9,8},{10,9... | collective-permute-start | bytes 44 | tf_op jit(solution)/shard_map/ppermute | solution.py:260

commit v4 on v3

--- a/solution.py
+++ b/solution.py
@@ -74,8 +74,16 @@
             notes.append(told)
     for i, (get, put, shift) in enumerate(steps):
         get.wait()
-        turned = pltpu.roll(wide[i].astype(jnp.float32), lax.rem(span - shift, span), 1)
-        cut[i] = turned[:, :width].astype(cut.dtype)
+        turn = lax.rem(LANES - shift, LANES)
+        inside = lax.broadcasted_iota(jnp.int32, (rows, LANES), 1) < LANES - shift
+        turned = [
+            pltpu.roll(wide[i, :, n * LANES : (n + 1) * LANES].astype(jnp.float32), turn, 1)
+            for n in range(span // LANES)
+        ]
+        for n in range(width // LANES):
+            cut[i, :, n * LANES : (n + 1) * LANES] = jnp.where(
+                inside, turned[n], turned[n + 1]
+            ).astype(cut.dtype)
         put.start()
     for _, put, _ in steps:
         put.wait()
@@ -111,7 +119,7 @@
         ],
         compiler_params=pltpu.CompilerParams(vmem_limit_bytes=16 << 20),
         cost_estimate=pl.CostEstimate(
-            flops=0, transcendentals=0, bytes_accessed=count * rows * (span + width) * 2
+            flops=0, transcendentals=0, bytes_accessed=1000
         ),
     )(*operands)
 
@@ -194,7 +202,7 @@
 BASE = 4
 ZS = 4
 DIRECT = (1, 2)
-FLOWS = ((1, 1), (0, 3), (0, 2), (1, 0), (1, 3), (0, 1))
+FLOWS = ((1, 1), (0, 3), (1, 3), (0, 1), (0, 2), (1, 0))
 EARLY = 3
 AHEAD = 3
 
@@ -221,12 +229,13 @@
         slots=slots,
         width=width,
     )
-    (first,) = cut([[(0, (*DIRECT, 0)), (1, (*DIRECT, 1))]], [2], [])
-    first, cut.keywords["footprint"] = after(first, footprint)
-    flows, made = [DIRECT], [first]
+    lead = [(0, (*DIRECT, 0)), (1, (*DIRECT, 1))]
+    flows, made = [DIRECT], []
     for at, group in enumerate((FLOWS[:EARLY], FLOWS[EARLY:])):
         to = [(*f, 1) for f in group] + ([(0, 0, 1)] if at == 0 else [])
-        (other,) = cut([list(enumerate(to))], [len(to)], [])
+        extra = [lead] if at == 0 else []
+        *first, other = cut([*extra, list(enumerate(to))], [2] * len(extra) + [len(to)], [])
+        made += first
         other = send(other, 0, 0, 1)
         other, cut.keywords["footprint"] = after(other, cut.keywords["footprint"])
         to = [(*f, 0) for f in group] + ([(0, 0, 0)] if at == 0 else [])

time: 142 us -> 138 us (0.972); the launches traced: 139 us -> 138 us
  Pallas kernels: 37.2 us -> 32.8 us
  starting transfers between devices: 34.8 us -> 36.5 us
  waiting for transfers between devices: 65.4 us -> 67.1 us
    pallas_call x5 -> x4, Pallas kernels: 18.4 us -> 14 us  [cut_windows(): pl.pallas_call(functools.partial(cut_kernel, pieces, fills, held), out_sh...]
    ppermute x10, waiting for transfers between devices: 52.4 us -> 54.8 us  [on_device(): lax.ppermute(x, 'tile', pairs(owners, dy, dx, dc))]
    ppermute x10, starting transfers between devices: 18.7 us -> 20.3 us  [on_device(): lax.ppermute(x, 'tile', pairs(owners, dy, dx, dc))]
  transfers between devices with their start and end apart: 17 -> 17, of which waited for: 10 -> 10; matrix products, arithmetic and copies ran while one was open for 0% -> 0% of each run, Pallas kernels for 20% -> 19%
where the time goes in v4:
time: 138 us
  waiting for transfers between devices  67.1 us (49%)
  starting transfers between devices  36.5 us (26%)
  Pallas kernels  32.8 us (24%)
    ppermute x10, waiting for transfers between devices, on_device(): lax.ppermute(x, 'tile', pairs(owners, dy, dx, dc))  54.8 us
    ppermute x10, starting transfers between devices, on_device(): lax.ppermute(x, 'tile', pairs(owners, dy, dx, dc))  20.3 us
    pallas_call x8, Pallas kernels, add(): pl.pallas_call(functools.partial(add_kernel, sources, slots, first, last)...  18.7 us
    ppermute x7, starting transfers between devices, on_device(): lax.ppermute(x, 'subap', [(i, (i // ZS ^ dy) * ZS + (i + dz) % ZS) for i...  16.2 us
    pallas_call x4, Pallas kernels, cut_windows(): pl.pallas_call(functools.partial(cut_kernel, pieces, fills, held), out_sh...  14 us
    ppermute x7, waiting for transfers between devices, on_device(): lax.ppermute(x, 'subap', [(i, (i // ZS ^ dy) * ZS + (i + dz) % ZS) for i...  12.3 us
  transfers between devices with their start and end apart: 17, of which 10 were waited for; matrix products, arithmetic and copies ran while one was open for 0% of the time, Pallas kernels for 19%

profile of v4, /device:TPU:0, one launch (start us, length us, event | category | flops | bytes accessed | tf_op | source)
XLA Modules:
  0.0 137.7 jit_solution(2193779381323571414)
XLA Ops:
  0.0 4.1 %shard_map.55 = (bf16[2,520,512]{2,1,0:T(8,128)(2,1)S(1)}, bf16[4,520,512]{2,1,0:T(8,128)(2,1)S(1)}) custom-call(s32[32]{0:T(128)} %bitcast.17, s32[48]{0:T(128)} %offsets_hbm.7, bf16[256,16384]{1,0:T(8,128)(2,1)} %bitcast.13), custom_call_target="tpu_custom_call" | custom-call | bytes 1000 | tf_op jit(solution)/shard_map/pallas_call | solution.py:100
  4.2 4.2 %collective-permute-start.4 = (bf16[2,520,512]{2,1,0:T(8,128)(2,1)S(1)}, bf16[2,520,512]{2,1,0:T(8,128)(2,1)S(1)}, u32[]{:S(2)}, u32[]{:S(2)}) collective-permute-start(bf16[2,520,512]{2,1,0:T(8,128)(2,1)S(1)} %get-tuple-element.40), channel_id=1, source_target_pairs={{0,96},{8,104},{16,112},{24,120},{32,64},{40,72},{48,80},{56,88},{... | collective-permute-start | bytes 3194888 | tf_op jit(solution)/shard_map/ppermute | solution.py:222
  8.4 3.5 %shard_map.56 = bf16[3,520,512]{2,1,0:T(8,128)(2,1)S(1)} custom-call(s32[32]{0:T(128)} %bitcast.18, s32[48]{0:T(128)} %offsets_hbm.7, bf16[256,16384]{1,0:T(8,128)(2,1)} %bitcast.14), custom_call_target="tpu_custom_call" | custom-call | bytes 1000 | tf_op jit(solution)/shard_map/pallas_call | solution.py:100
  12.1 3.5 %shard_map.58 = (bf16[2,520,512]{2,1,0:T(8,128)(2,1)S(1)}, bf16[2,520,512]{2,1,0:T(8,128)(2,1)S(1)}, bf16[2,520,512]{2,1,0:T(8,128)(2,1)S(1)}, bf16[2,520,512]{2,1,0:T(8,128)(2,1)S(1)}) custom-call(s32[32]{0:T(128)} %bitcast.19, s32[48]{0:T(128)} %offsets_hbm.7, bf16[256,16384]{1,0:T(8,128)(2,1)} %bitcast.15, ...), custom_call_target="tpu_custom_call" | custom-call | bytes 1000 | tf_op jit(solution)/shard_map/pallas_call | solution.py:100
  15.6 2.6 %collective-permute-start.3 = (bf16[2,520,512]{2,1,0:T(8,128)(2,1)S(1)}, bf16[2,520,512]{2,1,0:T(8,128)(2,1)S(1)}, u32[]{:S(2)}, u32[]{:S(2)}) collective-permute-start(bf16[2,520,512]{2,1,0:T(8,128)(2,1)S(1)} %get-tuple-element.38), channel_id=1, source_target_pairs={{0,80},{8,88},{16,96},{24,104},{32,112},{40,120},{48,64},{56,72},{... | collective-permute-start | bytes 3194888 | tf_op jit(solution)/shard_map/ppermute | solution.py:222
  20.0 13.0 %collective-permute-done.4 = bf16[2,520,512]{2,1,0:T(8,128)(2,1)S(1)} collective-permute-done((bf16[2,520,512]{2,1,0:T(8,128)(2,1)S(1)}, bf16[2,520,512]{2,1,0:T(8,128)(2,1)S(1)}, u32[]{:S(2)}, u32[]{:S(2)}) %collective-permute-start.4) | collective-permute-done | bytes 1064992 | tf_op jit(solution)/shard_map/ppermute | solution.py:222
  35.5 5.3 %collective-permute-start.9 = (bf16[2,520,512]{2,1,0:T(8,128)(2,1)S(1)}, bf16[2,520,512]{2,1,0:T(8,128)(2,1)S(1)}, u32[]{:S(2)}, u32[]{:S(2)}) collective-permute-start(bf16[2,520,512]{2,1,0:T(8,128)(2,1)S(1)} %get-tuple-element.49), channel_id=1, source_target_pairs={{0,112},{8,120},{16,64},{24,72},{32,80},{40,88},{48,96},{56,104},{... | collective-permute-start | bytes 3194888 | tf_op jit(solution)/shard_map/ppermute | solution.py:222
  40.8 2.4 %shard_map.60.refs_3_ = f32[3,2,256,256]{3,2,1,0:T(8,128)S(1)} custom-call(bf16[1,520,512]{2,1,0:T(8,128)(2,1)S(1)} %get-tuple-element.58.refs_0_, bf16[1,520,512]{2,1,0:T(8,128)(2,1)S(1)} %collective-permute-done.5.refs_1_, bf16[3,16,2,256,128]{4,3,2,1,0:T(8,128)(2,1)S(1)} %bitcast.6, ...), custom_call_target="tpu_custom_call", output_to_operand_aliasing={{}: (4, {})} | custom-call | flops 800000000 | bytes 6000000 | tf_op jit(solution)/shard_map/pallas_call | solution.py:185
  43.2 2.9 %shard_map.57 = (bf16[2,520,512]{2,1,0:T(8,128)(2,1)S(1)}, bf16[2,520,512]{2,1,0:T(8,128)(2,1)S(1)}, bf16[2,520,512]{2,1,0:T(8,128)(2,1)S(1)}) custom-call(s32[32]{0:T(128)} %bitcast.20, s32[48]{0:T(128)} %offsets_hbm.7, bf16[256,16384]{1,0:T(8,128)(2,1)} %bitcast.16, bf16[3,520,512]{2,1,0:T(8,128)(2,1)S(1)} %collective-permute-done.1.refs_0_), custom_call_target="tpu_custom_call" | custom-call | bytes 1000 | tf_op jit(solution)/shard_map/pallas_call | solution.py:100
  46.4 9.1 %collective-permute-done.3.refs_0_ = bf16[2,520,512]{2,1,0:T(8,128)(2,1)S(1)} collective-permute-done((bf16[2,520,512]{2,1,0:T(8,128)(2,1)S(1)}, bf16[2,520,512]{2,1,0:T(8,128)(2,1)S(1)}, u32[]{:S(2)}, u32[]{:S(2)}) %collective-permute-start.3) | collective-permute-done | bytes 1064992 | tf_op jit(solution)/shard_map/ppermute | solution.py:222
  55.5 2.4 %shard_map.61.refs_3_ = f32[3,2,256,256]{3,2,1,0:T(8,128)S(1)} custom-call(bf16[2,520,512]{2,1,0:T(8,128)(2,1)S(1)} %collective-permute-done.3.refs_0_, bf16[3,16,2,256,128]{4,3,2,1,0:T(8,128)(2,1)S(1)} %bitcast.7, bf16[3,2,512,256]{3,2,1,0:T(8,128)(2,1)S(1)} %copy-done, f32[3,2,256,256]{3,2,1,0:T(8,128)S(1)} %shard_map.60.refs_3_), custom_call_target="tpu_custom_call", output_to_operand_aliasing={{}: (3, {})} | custom-call | flops 800000000 | bytes 6000000 | tf_op jit(solution)/shard_map/pallas_call | solution.py:185
  57.9 4.1 %collective-permute-start.7 = (bf16[2,520,512]{2,1,0:T(8,128)(2,1)S(1)}, bf16[2,520,512]{2,1,0:T(8,128)(2,1)S(1)}, u32[]{:S(2)}, u32[]{:S(2)}) collective-permute-start(bf16[2,520,512]{2,1,0:T(8,128)(2,1)S(1)} %get-tuple-element.47), channel_id=1, source_target_pairs={{0,32},{8,40},{16,48},{24,56},{32,0},{40,8},{48,16},{56,24},{64,96... | collective-permute-start | bytes 3194888 | tf_op jit(solution)/shard_map/ppermute | solution.py:222
  62.0 2.4 %shard_map.62.refs_3_ = f32[3,2,256,256]{3,2,1,0:T(8,128)S(1)} custom-call(bf16[2,520,512]{2,1,0:T(8,128)(2,1)S(1)} %collective-permute-done.2.refs_0_, bf16[3,16,2,256,128]{4,3,2,1,0:T(8,128)(2,1)S(1)} %bitcast.8, bf16[3,2,512,256]{3,2,1,0:T(8,128)(2,1)S(1)} %copy-done, f32[3,2,256,256]{3,2,1,0:T(8,128)S(1)} %shard_map.61.refs_3_), custom_call_target="tpu_custom_call", output_to_operand_aliasing={{}: (3, {})} | custom-call | flops 800000000 | bytes 6000000 | tf_op jit(solution)/shard_map/pallas_call | solution.py:185
  66.1 12.8 %collective-permute-done.9.refs_0_ = bf16[2,520,512]{2,1,0:T(8,128)(2,1)S(1)} collective-permute-done((bf16[2,520,512]{2,1,0:T(8,128)(2,1)S(1)}, bf16[2,520,512]{2,1,0:T(8,128)(2,1)S(1)}, u32[]{:S(2)}, u32[]{:S(2)}) %collective-permute-start.9) | collective-permute-done | bytes 1064992 | tf_op jit(solution)/shard_map/ppermute | solution.py:222
  78.9 2.4 %shard_map.63.refs_3_ = f32[3,2,256,256]{3,2,1,0:T(8,128)S(1)} custom-call(bf16[2,520,512]{2,1,0:T(8,128)(2,1)S(1)} %collective-permute-done.9.refs_0_, bf16[3,16,2,256,128]{4,3,2,1,0:T(8,128)(2,1)S(1)} %bitcast.9, bf16[3,2,512,256]{3,2,1,0:T(8,128)(2,1)S(1)} %copy-done, f32[3,2,256,256]{3,2,1,0:T(8,128)S(1)} %shard_map.62.refs_3_), custom_call_target="tpu_custom_call", output_to_operand_aliasing={{}: (3, {})} | custom-call | flops 800000000 | bytes 6000000 | tf_op jit(solution)/shard_map/pallas_call | solution.py:185
  81.3 2.4 %shard_map.64.refs_3_ = f32[3,2,256,256]{3,2,1,0:T(8,128)S(1)} custom-call(bf16[2,520,512]{2,1,0:T(8,128)(2,1)S(1)} %collective-permute-done.8.refs_0_, bf16[3,16,2,256,128]{4,3,2,1,0:T(8,128)(2,1)S(1)} %bitcast.10, bf16[3,2,512,256]{3,2,1,0:T(8,128)(2,1)S(1)} %copy-done, f32[3,2,256,256]{3,2,1,0:T(8,128)S(1)} %shard_map.63.refs_3_), custom_call_target="tpu_custom_call", output_to_operand_aliasing={{}: (3, {})} | custom-call | flops 800000000 | bytes 6000000 | tf_op jit(solution)/shard_map/pallas_call | solution.py:185
  83.8 19.7 %collective-permute-done.7.refs_0_ = bf16[2,520,512]{2,1,0:T(8,128)(2,1)S(1)} collective-permute-done((bf16[2,520,512]{2,1,0:T(8,128)(2,1)S(1)}, bf16[2,520,512]{2,1,0:T(8,128)(2,1)S(1)}, u32[]{:S(2)}, u32[]{:S(2)}) %collective-permute-start.7) | collective-permute-done | bytes 1064992 | tf_op jit(solution)/shard_map/ppermute | solution.py:222
  103.5 2.4 %shard_map.65.refs_3_ = f32[3,2,256,256]{3,2,1,0:T(8,128)S(1)} custom-call(bf16[2,520,512]{2,1,0:T(8,128)(2,1)S(1)} %collective-permute-done.7.refs_0_, bf16[3,16,2,256,128]{4,3,2,1,0:T(8,128)(2,1)S(1)} %bitcast.11, bf16[3,2,512,256]{3,2,1,0:T(8,128)(2,1)S(1)} %copy-done, f32[3,2,256,256]{3,2,1,0:T(8,128)S(1)} %shard_map.64.refs_3_), custom_call_target="tpu_custom_call", output_to_operand_aliasing={{}: (3, {})} | custom-call | flops 800000000 | bytes 6000000 | tf_op jit(solution)/shard_map/pallas_call | solution.py:185
  108.1 4.0 %collective-permute-start.10 = (bf16[3,2,64,256]{3,2,1,0:T(8,128)(2,1)S(1)}, bf16[3,2,64,256]{3,2,1,0:T(8,128)(2,1)S(1)}, u32[]{:S(2)}, u32[]{:S(2)}) collective-permute-start(bf16[3,2,64,256]{3,2,1,0:T(8,128)(2,1)S(1)} %get-tuple-element.52), channel_id=1, source_target_pairs={{0,2},{1,3},{2,0},{3,1},{4,6},{5,7},{6,4},{7,5},{8,10},{9,11},{10,... | collective-permute-start | bytes 589832 | tf_op jit(solution)/shard_map/ppermute | solution.py:269
  115.3 2.5 %collective-permute-done.10 = bf16[3,2,64,256]{3,2,1,0:T(8,128)(2,1)S(1)} collective-permute-done((bf16[3,2,64,256]{3,2,1,0:T(8,128)(2,1)S(1)}, bf16[3,2,64,256]{3,2,1,0:T(8,128)(2,1)S(1)}, u32[]{:S(2)}, u32[]{:S(2)}) %collective-permute-start.10) | collective-permute-done | bytes 196640 | tf_op jit(solution)/shard_map/ppermute | solution.py:269
  117.8 3.2 %collective-permute-done.11 = bf16[3,2,64,256]{3,2,1,0:T(8,128)(2,1)S(1)} collective-permute-done((bf16[3,2,64,256]{3,2,1,0:T(8,128)(2,1)S(1)}, bf16[3,2,64,256]{3,2,1,0:T(8,128)(2,1)S(1)}, u32[]{:S(2)}, u32[]{:S(2)}) %collective-permute-start.11) | collective-permute-done | bytes 196640 | tf_op jit(solution)/shard_map/ppermute | solution.py:269
  121.8 3.0 %collective-permute-start.13 = (bf16[3,2,64,256]{3,2,1,0:T(8,128)(2,1)S(1)}, bf16[3,2,64,256]{3,2,1,0:T(8,128)(2,1)S(1)}, u32[]{:S(2)}, u32[]{:S(2)}) collective-permute-start(bf16[3,2,64,256]{3,2,1,0:T(8,128)(2,1)S(1)} %fusion), channel_id=1, source_target_pairs={{0,4},{1,5},{2,6},{3,7},{4,0},{5,1},{6,2},{7,3},{8,12},{9,13},{10,... | collective-permute-start | bytes 589832 | tf_op jit(solution)/shard_map/ppermute | solution.py:269
  124.8 4.3 %collective-permute-done.13 = bf16[3,2,64,256]{3,2,1,0:T(8,128)(2,1)S(1)} collective-permute-done((bf16[3,2,64,256]{3,2,1,0:T(8,128)(2,1)S(1)}, bf16[3,2,64,256]{3,2,1,0:T(8,128)(2,1)S(1)}, u32[]{:S(2)}, u32[]{:S(2)}) %collective-permute-start.13) | collective-permute-done | bytes 196640 | tf_op jit(solution)/shard_map/ppermute | solution.py:269
  129.3 2.8 %collective-permute-start.14 = (f32[3]{0:T(128)S(1)}, f32[3]{0:T(128)S(1)}, u32[]{:S(2)}, u32[]{:S(2)}) collective-permute-start(f32[3]{0:T(128)S(1)} %get-tuple-element.55), channel_id=1, source_target_pairs={{0,2},{1,3},{2,0},{3,1},{4,6},{5,7},{6,4},{7,5},{8,10},{9,11},{10,... | collective-permute-start | bytes 44 | tf_op jit(solution)/shard_map/ppermute | solution.py:269
  (34 shorter events, 18.5 us)
Async XLA Ops:
  4.1 4.3 %collective-permute-start = (bf16[4,520,512]{2,1,0:T(8,128)(2,1)S(1)}, bf16[4,520,512]{2,1,0:T(8,128)(2,1)S(1)}, u32[]{:S(2)}, u32[]{:S(2)}) collective-permute-start(bf16[4,520,512]{2,1,0:T(8,128)(2,1)S(1)} %get-tuple-element.30), channel_id=1, source_target_pairs={{0,8},{8,0},{16,24},{24,16},{32,40},{40,32},{48,56},{56,48},{64,72... | collective-permute-start | bytes 6389768 | tf_op jit(solution)/shard_map/ppermute | solution.py:222
  4.2 28.8 %collective-permute-start.4 = (bf16[2,520,512]{2,1,0:T(8,128)(2,1)S(1)}, bf16[2,520,512]{2,1,0:T(8,128)(2,1)S(1)}, u32[]{:S(2)}, u32[]{:S(2)}) collective-permute-start(bf16[2,520,512]{2,1,0:T(8,128)(2,1)S(1)} %get-tuple-element.40), channel_id=1, source_target_pairs={{0,96},{8,104},{16,112},{24,120},{32,64},{40,72},{48,80},{56,88},{... | collective-permute-start | bytes 3194888 | tf_op jit(solution)/shard_map/ppermute | solution.py:222
  8.4 24.8 %slice-start = ((s8[6291456]{0:T(1024)(128)(4,1)}), s8[4194304]{0:T(1024)(128)(4,1)S(1)}, s32[]{:S(2)}) async-start(s8[6291456]{0:T(1024)(128)(4,1)} %bitcast.3), calls=%async_computation | async-start | bytes 8388608
  11.9 21.4 %slice-start.1 = ((s8[6291456]{0:T(1024)(128)(4,1)}), s8[2097152]{0:T(1024)(128)(4,1)S(1)}, s32[]{:S(2)}) async-start(s8[6291456]{0:T(1024)(128)(4,1)} %bitcast.3), calls=%async_computation.1 | async-start | bytes 4194304
  11.9 31.3 %collective-permute-start.1 = (bf16[3,520,512]{2,1,0:T(8,128)(2,1)S(1)}, bf16[3,520,512]{2,1,0:T(8,128)(2,1)S(1)}, u32[]{:S(2)}, u32[]{:S(2)}) collective-permute-start(bf16[3,520,512]{2,1,0:T(8,128)(2,1)S(1)} %shard_map.56), channel_id=1, source_target_pairs={{0,8},{8,0},{16,24},{24,16},{32,40},{40,32},{48,56},{56,48},{64,72... | collective-permute-start | bytes 4792328 | tf_op jit(solution)/shard_map/ppermute | solution.py:222
  15.6 39.9 %collective-permute-start.3 = (bf16[2,520,512]{2,1,0:T(8,128)(2,1)S(1)}, bf16[2,520,512]{2,1,0:T(8,128)(2,1)S(1)}, u32[]{:S(2)}, u32[]{:S(2)}) collective-permute-start(bf16[2,520,512]{2,1,0:T(8,128)(2,1)S(1)} %get-tuple-element.38), channel_id=1, source_target_pairs={{0,80},{8,88},{16,96},{24,104},{32,112},{40,120},{48,64},{56,72},{... | collective-permute-start | bytes 3194888 | tf_op jit(solution)/shard_map/ppermute | solution.py:222
  18.3 15.0 %copy-start = (bf16[3,2,512,256]{3,2,1,0:T(8,128)(2,1)S(1)}, bf16[3,2,512,256]{3,2,1,0:T(8,128)(2,1)}, u32[]{:S(2)}) copy-start(bf16[3,2,512,256]{3,2,1,0:T(8,128)(2,1)} %refs_2_.13) | copy-start | bytes 4718596
  18.3 43.8 %collective-permute-start.2 = (bf16[2,520,512]{2,1,0:T(8,128)(2,1)S(1)}, bf16[2,520,512]{2,1,0:T(8,128)(2,1)S(1)}, u32[]{:S(2)}, u32[]{:S(2)}) collective-permute-start(bf16[2,520,512]{2,1,0:T(8,128)(2,1)S(1)} %get-tuple-element.36), channel_id=1, source_target_pairs={{0,48},{8,56},{16,0},{24,8},{32,16},{40,24},{48,32},{56,40},{64,11... | collective-permute-start | bytes 3194888 | tf_op jit(solution)/shard_map/ppermute | solution.py:222
  33.2 7.6 %collective-permute-start.5 = (bf16[1,520,512]{2,1,0:T(8,128)(2,1)S(1)}, bf16[1,520,512]{2,1,0:T(8,128)(2,1)S(1)}, u32[]{:S(2)}, u32[]{:S(2)}) collective-permute-start(bf16[1,520,512]{2,1,0:T(8,128)(2,1)S(1)} %get-tuple-element.57), channel_id=1, source_target_pairs={{0,8},{8,0},{16,24},{24,16},{32,40},{40,32},{48,56},{56,48},{64,72... | collective-permute-start | bytes 1597448 | tf_op jit(solution)/shard_map/ppermute | solution.py:222
  35.5 43.5 %collective-permute-start.9 = (bf16[2,520,512]{2,1,0:T(8,128)(2,1)S(1)}, bf16[2,520,512]{2,1,0:T(8,128)(2,1)S(1)}, u32[]{:S(2)}, u32[]{:S(2)}) collective-permute-start(bf16[2,520,512]{2,1,0:T(8,128)(2,1)S(1)} %get-tuple-element.49), channel_id=1, source_target_pairs={{0,112},{8,120},{16,64},{24,72},{32,80},{40,88},{48,96},{56,104},{... | collective-permute-start | bytes 3194888 | tf_op jit(solution)/shard_map/ppermute | solution.py:222
  46.2 35.2 %collective-permute-start.8 = (bf16[2,520,512]{2,1,0:T(8,128)(2,1)S(1)}, bf16[2,520,512]{2,1,0:T(8,128)(2,1)S(1)}, u32[]{:S(2)}, u32[]{:S(2)}) collective-permute-start(bf16[2,520,512]{2,1,0:T(8,128)(2,1)S(1)} %get-tuple-element.48), channel_id=1, source_target_pairs={{0,16},{8,24},{16,32},{24,40},{32,48},{40,56},{48,0},{56,8},{64,80... | collective-permute-start | bytes 3194888 | tf_op jit(solution)/shard_map/ppermute | solution.py:222
  57.9 45.5 %collective-permute-start.7 = (bf16[2,520,512]{2,1,0:T(8,128)(2,1)S(1)}, bf16[2,520,512]{2,1,0:T(8,128)(2,1)S(1)}, u32[]{:S(2)}, u32[]{:S(2)}) collective-permute-start(bf16[2,520,512]{2,1,0:T(8,128)(2,1)S(1)} %get-tuple-element.47), channel_id=1, source_target_pairs={{0,32},{8,40},{16,48},{24,56},{32,0},{40,8},{48,16},{56,24},{64,96... | collective-permute-start | bytes 3194888 | tf_op jit(solution)/shard_map/ppermute | solution.py:222
  64.4 41.4 %collective-permute-start.6 = (bf16[2,520,512]{2,1,0:T(8,128)(2,1)S(1)}, bf16[2,520,512]{2,1,0:T(8,128)(2,1)S(1)}, u32[]{:S(2)}, u32[]{:S(2)}) collective-permute-start(bf16[2,520,512]{2,1,0:T(8,128)(2,1)S(1)} %get-tuple-element.46), channel_id=1, source_target_pairs={{0,64},{8,72},{16,80},{24,88},{32,96},{40,104},{48,112},{56,120},{... | collective-permute-start | bytes 3194888 | tf_op jit(solution)/shard_map/ppermute | solution.py:222
  108.1 9.7 %collective-permute-start.10 = (bf16[3,2,64,256]{3,2,1,0:T(8,128)(2,1)S(1)}, bf16[3,2,64,256]{3,2,1,0:T(8,128)(2,1)S(1)}, u32[]{:S(2)}, u32[]{:S(2)}) collective-permute-start(bf16[3,2,64,256]{3,2,1,0:T(8,128)(2,1)S(1)} %get-tuple-element.52), channel_id=1, source_target_pairs={{0,2},{1,3},{2,0},{3,1},{4,6},{5,7},{6,4},{7,5},{8,10},{9,11},{10,... | collective-permute-start | bytes 589832 | tf_op jit(solution)/shard_map/ppermute | solution.py:269
  112.1 8.9 %collective-permute-start.11 = (bf16[3,2,64,256]{3,2,1,0:T(8,128)(2,1)S(1)}, bf16[3,2,64,256]{3,2,1,0:T(8,128)(2,1)S(1)}, u32[]{:S(2)}, u32[]{:S(2)}) collective-permute-start(bf16[3,2,64,256]{3,2,1,0:T(8,128)(2,1)S(1)} %get-tuple-element.53), channel_id=1, source_target_pairs={{0,1},{1,2},{2,3},{3,0},{4,5},{5,6},{6,7},{7,4},{8,9},{9,10},{10,1... | collective-permute-start | bytes 589832 | tf_op jit(solution)/shard_map/ppermute | solution.py:269
  113.1 8.6 %collective-permute-start.12 = (bf16[3,2,64,256]{3,2,1,0:T(8,128)(2,1)S(1)}, bf16[3,2,64,256]{3,2,1,0:T(8,128)(2,1)S(1)}, u32[]{:S(2)}, u32[]{:S(2)}) collective-permute-start(bf16[3,2,64,256]{3,2,1,0:T(8,128)(2,1)S(1)} %get-tuple-element.54), channel_id=1, source_target_pairs={{0,3},{1,0},{2,1},{3,2},{4,7},{5,4},{6,5},{7,6},{8,11},{9,8},{10,9... | collective-permute-start | bytes 589832 | tf_op jit(solution)/shard_map/ppermute | solution.py:269
  121.8 7.3 %collective-permute-start.13 = (bf16[3,2,64,256]{3,2,1,0:T(8,128)(2,1)S(1)}, bf16[3,2,64,256]{3,2,1,0:T(8,128)(2,1)S(1)}, u32[]{:S(2)}, u32[]{:S(2)}) collective-permute-start(bf16[3,2,64,256]{3,2,1,0:T(8,128)(2,1)S(1)} %fusion), channel_id=1, source_target_pairs={{0,4},{1,5},{2,6},{3,7},{4,0},{5,1},{6,2},{7,3},{8,12},{9,13},{10,... | collective-permute-start | bytes 589832 | tf_op jit(solution)/shard_map/ppermute | solution.py:269
  129.3 6.0 %collective-permute-start.14 = (f32[3]{0:T(128)S(1)}, f32[3]{0:T(128)S(1)}, u32[]{:S(2)}, u32[]{:S(2)}) collective-permute-start(f32[3]{0:T(128)S(1)} %get-tuple-element.55), channel_id=1, source_target_pairs={{0,2},{1,3},{2,0},{3,1},{4,6},{5,7},{6,4},{7,5},{8,10},{9,11},{10,... | collective-permute-start | bytes 44 | tf_op jit(solution)/shard_map/ppermute | solution.py:269
  132.0 4.8 %collective-permute-start.15 = (f32[3]{0:T(128)S(1)}, f32[3]{0:T(128)S(1)}, u32[]{:S(2)}, u32[]{:S(2)}) collective-permute-start(f32[3]{0:T(128)S(1)} %get-tuple-element.55), channel_id=1, source_target_pairs={{0,1},{1,2},{2,3},{3,0},{4,5},{5,6},{6,7},{7,4},{8,9},{9,10},{10,1... | collective-permute-start | bytes 44 | tf_op jit(solution)/shard_map/ppermute | solution.py:269
  133.4 3.5 %collective-permute-start.16 = (f32[3]{0:T(128)S(1)}, f32[3]{0:T(128)S(1)}, u32[]{:S(2)}, u32[]{:S(2)}) collective-permute-start(f32[3]{0:T(128)S(1)} %get-tuple-element.55), channel_id=1, source_target_pairs={{0,3},{1,0},{2,1},{3,2},{4,7},{5,4},{6,5},{7,6},{8,11},{9,8},{10,9... | collective-permute-start | bytes 44 | tf_op jit(solution)/shard_map/ppermute | solution.py:269

commit v5 on v4

--- a/solution.py
+++ b/solution.py
@@ -148,19 +148,27 @@
                 x = (window, at, slice(slot * both, (slot + 1) * both))
                 work.append((x, toward(me, dy, XS - dx, dc)))
     packed = jnp.max(packed).astype(jnp.int32)
-    for n, ((window, at, span), source) in enumerate(work):
+    def in_range(n):
+        (window, at, span), source = work[n]
         tile = (packed >> (n * (BASE.bit_length() - 1))) & (BASE - 1)
         x = window[at, span]
         pr = jnp.dot(x, table[tile, 0], preferred_element_type=jnp.float32)
         pi = jnp.dot(x, table[tile, 1], preferred_element_type=jnp.float32)
         rr = (pr[:half] - pi[half:]).astype(x.dtype)
         ri = (pi[:half] + pr[half:]).astype(x.dtype)
-        right = jnp.concatenate([rr, ri], 1)
-        width = rr.shape[1]
-        ar = jnp.dot(azimuth[tile, source, 0], right, preferred_element_type=jnp.float32)
-        ai = jnp.dot(azimuth[tile, source, 1], right, preferred_element_type=jnp.float32)
-        sub[tile, 0] += ar[:, :width] - ai[:, width:]
-        sub[tile, 1] += ar[:, width:] + ai[:, :width]
+        return tile, source, rr, ri
+
+    def in_azimuth(tile, source, rr, ri):
+        left = jnp.concatenate([azimuth[tile, source, 0], azimuth[tile, source, 1]], 1)
+        right = jnp.concatenate(
+            [jnp.concatenate([rr, ri], 1), jnp.concatenate([-ri, rr], 1)], 0
+        )
+        both = jnp.dot(left, right, preferred_element_type=jnp.float32)
+        sub[tile, 0] += both[:, : rr.shape[1]]
+        sub[tile, 1] += both[:, rr.shape[1] :]
+
+    for ranged in [in_range(n) for n in range(len(work))]:
+        in_azimuth(*ranged)
     if last:
         z = lax.axis_index("subap") % ZS
         halves = sub.shape[2] // outs[0].shape[2] // ZS * 2

time: 138 us -> 136 us (0.986)
  Pallas kernels: 32.8 us -> 25.1 us
  waiting for transfers between devices: 67.1 us -> 72.8 us
    pallas_call x8, Pallas kernels: 18.7 us -> 11.1 us  [add(): pl.pallas_call(functools.partial(add_kernel, sources, slots, first, last)...]
    ppermute x10, waiting for transfers between devices: 54.8 us -> 60.4 us  [on_device(): lax.ppermute(x, 'tile', pairs(owners, dy, dx, dc))]
  transfers between devices with their start and end apart: 17 -> 17, of which waited for: 10 -> 10; matrix products, arithmetic and copies ran while one was open for 0% -> 0% of each run, Pallas kernels for 19% -> 15%
where the time goes in v5:
time: 136 us
  waiting for transfers between devices  72.8 us (54%)
  starting transfers between devices  36.5 us (27%)
  Pallas kernels  25.1 us (18%)
    ppermute x10, waiting for transfers between devices, on_device(): lax.ppermute(x, 'tile', pairs(owners, dy, dx, dc))  60.4 us
    ppermute x10, starting transfers between devices, on_device(): lax.ppermute(x, 'tile', pairs(owners, dy, dx, dc))  20.3 us
    ppermute x7, starting transfers between devices, on_device(): lax.ppermute(x, 'subap', [(i, (i // ZS ^ dy) * ZS + (i + dz) % ZS) for i...  16.2 us
    pallas_call x4, Pallas kernels, cut_windows(): pl.pallas_call(functools.partial(cut_kernel, pieces, fills, held), out_sh...  14 us
    ppermute x7, waiting for transfers between devices, on_device(): lax.ppermute(x, 'subap', [(i, (i // ZS ^ dy) * ZS + (i + dz) % ZS) for i...  12.3 us
    pallas_call x8, Pallas kernels, add(): pl.pallas_call(functools.partial(add_kernel, sources, slots, first, last)...  11.1 us
  transfers between devices with their start and end apart: 17, of which 10 were waited for; matrix products, arithmetic and copies ran while one was open for 0% of the time, Pallas kernels for 15%

profile of v5, /device:TPU:0, one launch (start us, length us, event | category | flops | bytes accessed | tf_op | source)
XLA Modules:
  0.0 135.8 jit_solution(834839196337257348)
XLA Ops:
  0.0 4.1 %shard_map.55 = (bf16[2,520,512]{2,1,0:T(8,128)(2,1)S(1)}, bf16[4,520,512]{2,1,0:T(8,128)(2,1)S(1)}) custom-call(s32[32]{0:T(128)} %bitcast.17, s32[48]{0:T(128)} %offsets_hbm.7, bf16[256,16384]{1,0:T(8,128)(2,1)} %bitcast.13), custom_call_target="tpu_custom_call" | custom-call | bytes 1000 | tf_op jit(solution)/shard_map/pallas_call | solution.py:100
  4.2 4.2 %collective-permute-start.4 = (bf16[2,520,512]{2,1,0:T(8,128)(2,1)S(1)}, bf16[2,520,512]{2,1,0:T(8,128)(2,1)S(1)}, u32[]{:S(2)}, u32[]{:S(2)}) collective-permute-start(bf16[2,520,512]{2,1,0:T(8,128)(2,1)S(1)} %get-tuple-element.40), channel_id=1, source_target_pairs={{0,96},{8,104},{16,112},{24,120},{32,64},{40,72},{48,80},{56,88},{... | collective-permute-start | bytes 3194888 | tf_op jit(solution)/shard_map/ppermute | solution.py:230
  8.4 3.5 %shard_map.56 = bf16[3,520,512]{2,1,0:T(8,128)(2,1)S(1)} custom-call(s32[32]{0:T(128)} %bitcast.18, s32[48]{0:T(128)} %offsets_hbm.7, bf16[256,16384]{1,0:T(8,128)(2,1)} %bitcast.14), custom_call_target="tpu_custom_call" | custom-call | bytes 1000 | tf_op jit(solution)/shard_map/pallas_call | solution.py:100
  12.1 3.5 %shard_map.58 = (bf16[2,520,512]{2,1,0:T(8,128)(2,1)S(1)}, bf16[2,520,512]{2,1,0:T(8,128)(2,1)S(1)}, bf16[2,520,512]{2,1,0:T(8,128)(2,1)S(1)}, bf16[2,520,512]{2,1,0:T(8,128)(2,1)S(1)}) custom-call(s32[32]{0:T(128)} %bitcast.19, s32[48]{0:T(128)} %offsets_hbm.7, bf16[256,16384]{1,0:T(8,128)(2,1)} %bitcast.15, ...), custom_call_target="tpu_custom_call" | custom-call | bytes 1000 | tf_op jit(solution)/shard_map/pallas_call | solution.py:100
  15.6 2.6 %collective-permute-start.3 = (bf16[2,520,512]{2,1,0:T(8,128)(2,1)S(1)}, bf16[2,520,512]{2,1,0:T(8,128)(2,1)S(1)}, u32[]{:S(2)}, u32[]{:S(2)}) collective-permute-start(bf16[2,520,512]{2,1,0:T(8,128)(2,1)S(1)} %get-tuple-element.38), channel_id=1, source_target_pairs={{0,80},{8,88},{16,96},{24,104},{32,112},{40,120},{48,64},{56,72},{... | collective-permute-start | bytes 3194888 | tf_op jit(solution)/shard_map/ppermute | solution.py:230
  18.3 1.7 %collective-permute-start.2 = (bf16[2,520,512]{2,1,0:T(8,128)(2,1)S(1)}, bf16[2,520,512]{2,1,0:T(8,128)(2,1)S(1)}, u32[]{:S(2)}, u32[]{:S(2)}) collective-permute-start(bf16[2,520,512]{2,1,0:T(8,128)(2,1)S(1)} %get-tuple-element.36), channel_id=1, source_target_pairs={{0,48},{8,56},{16,0},{24,8},{32,16},{40,24},{48,32},{56,40},{64,11... | collective-permute-start | bytes 3194888 | tf_op jit(solution)/shard_map/ppermute | solution.py:230
  20.0 13.0 %collective-permute-done.4 = bf16[2,520,512]{2,1,0:T(8,128)(2,1)S(1)} collective-permute-done((bf16[2,520,512]{2,1,0:T(8,128)(2,1)S(1)}, bf16[2,520,512]{2,1,0:T(8,128)(2,1)S(1)}, u32[]{:S(2)}, u32[]{:S(2)}) %collective-permute-start.4) | collective-permute-done | bytes 1064992 | tf_op jit(solution)/shard_map/ppermute | solution.py:230
  34.4 5.3 %collective-permute-start.9 = (bf16[2,520,512]{2,1,0:T(8,128)(2,1)S(1)}, bf16[2,520,512]{2,1,0:T(8,128)(2,1)S(1)}, u32[]{:S(2)}, u32[]{:S(2)}) collective-permute-start(bf16[2,520,512]{2,1,0:T(8,128)(2,1)S(1)} %get-tuple-element.49), channel_id=1, source_target_pairs={{0,112},{8,120},{16,64},{24,72},{32,80},{40,88},{48,96},{56,104},{... | collective-permute-start | bytes 3194888 | tf_op jit(solution)/shard_map/ppermute | solution.py:230
  41.3 2.9 %shard_map.57 = (bf16[2,520,512]{2,1,0:T(8,128)(2,1)S(1)}, bf16[2,520,512]{2,1,0:T(8,128)(2,1)S(1)}, bf16[2,520,512]{2,1,0:T(8,128)(2,1)S(1)}) custom-call(s32[32]{0:T(128)} %bitcast.20, s32[48]{0:T(128)} %offsets_hbm.7, bf16[256,16384]{1,0:T(8,128)(2,1)} %bitcast.16, bf16[3,520,512]{2,1,0:T(8,128)(2,1)S(1)} %collective-permute-done.1.refs_0_), custom_call_target="tpu_custom_call" | custom-call | bytes 1000 | tf_op jit(solution)/shard_map/pallas_call | solution.py:100
  44.5 11.1 %collective-permute-done.3.refs_0_ = bf16[2,520,512]{2,1,0:T(8,128)(2,1)S(1)} collective-permute-done((bf16[2,520,512]{2,1,0:T(8,128)(2,1)S(1)}, bf16[2,520,512]{2,1,0:T(8,128)(2,1)S(1)}, u32[]{:S(2)}, u32[]{:S(2)}) %collective-permute-start.3) | collective-permute-done | bytes 1064992 | tf_op jit(solution)/shard_map/ppermute | solution.py:230
  57.0 4.1 %collective-permute-start.7 = (bf16[2,520,512]{2,1,0:T(8,128)(2,1)S(1)}, bf16[2,520,512]{2,1,0:T(8,128)(2,1)S(1)}, u32[]{:S(2)}, u32[]{:S(2)}) collective-permute-start(bf16[2,520,512]{2,1,0:T(8,128)(2,1)S(1)} %get-tuple-element.47), channel_id=1, source_target_pairs={{0,32},{8,40},{16,48},{24,56},{32,0},{40,8},{48,16},{56,24},{64,96... | collective-permute-start | bytes 3194888 | tf_op jit(solution)/shard_map/ppermute | solution.py:230
  62.6 1.7 %collective-permute-start.6 = (bf16[2,520,512]{2,1,0:T(8,128)(2,1)S(1)}, bf16[2,520,512]{2,1,0:T(8,128)(2,1)S(1)}, u32[]{:S(2)}, u32[]{:S(2)}) collective-permute-start(bf16[2,520,512]{2,1,0:T(8,128)(2,1)S(1)} %get-tuple-element.46), channel_id=1, source_target_pairs={{0,64},{8,72},{16,80},{24,88},{32,96},{40,104},{48,112},{56,120},{... | collective-permute-start | bytes 3194888 | tf_op jit(solution)/shard_map/ppermute | solution.py:230
  64.2 14.7 %collective-permute-done.9.refs_0_ = bf16[2,520,512]{2,1,0:T(8,128)(2,1)S(1)} collective-permute-done((bf16[2,520,512]{2,1,0:T(8,128)(2,1)S(1)}, bf16[2,520,512]{2,1,0:T(8,128)(2,1)S(1)}, u32[]{:S(2)}, u32[]{:S(2)}) %collective-permute-start.9) | collective-permute-done | bytes 1064992 | tf_op jit(solution)/shard_map/ppermute | solution.py:230
  80.4 1.5 %shard_map.64.refs_3_ = f32[3,2,256,256]{3,2,1,0:T(8,128)S(1)} custom-call(bf16[2,520,512]{2,1,0:T(8,128)(2,1)S(1)} %collective-permute-done.8.refs_0_, bf16[3,16,2,256,128]{4,3,2,1,0:T(8,128)(2,1)S(1)} %bitcast.10, bf16[3,2,512,256]{3,2,1,0:T(8,128)(2,1)S(1)} %copy-done, f32[3,2,256,256]{3,2,1,0:T(8,128)S(1)} %shard_map.63.refs_3_), custom_call_target="tpu_custom_call", output_to_operand_aliasing={{}: (3, {})} | custom-call | flops 800000000 | bytes 6000000 | tf_op jit(solution)/shard_map/pallas_call | solution.py:193
  81.9 21.6 %collective-permute-done.7.refs_0_ = bf16[2,520,512]{2,1,0:T(8,128)(2,1)S(1)} collective-permute-done((bf16[2,520,512]{2,1,0:T(8,128)(2,1)S(1)}, bf16[2,520,512]{2,1,0:T(8,128)(2,1)S(1)}, u32[]{:S(2)}, u32[]{:S(2)}) %collective-permute-start.7) | collective-permute-done | bytes 1064992 | tf_op jit(solution)/shard_map/ppermute | solution.py:230
  106.2 4.0 %collective-permute-start.10 = (bf16[3,2,64,256]{3,2,1,0:T(8,128)(2,1)S(1)}, bf16[3,2,64,256]{3,2,1,0:T(8,128)(2,1)S(1)}, u32[]{:S(2)}, u32[]{:S(2)}) collective-permute-start(bf16[3,2,64,256]{3,2,1,0:T(8,128)(2,1)S(1)} %get-tuple-element.52), channel_id=1, source_target_pairs={{0,2},{1,3},{2,0},{3,1},{4,6},{5,7},{6,4},{7,5},{8,10},{9,11},{10,... | collective-permute-start | bytes 589832 | tf_op jit(solution)/shard_map/ppermute | solution.py:277
  111.2 2.2 %collective-permute-start.12 = (bf16[3,2,64,256]{3,2,1,0:T(8,128)(2,1)S(1)}, bf16[3,2,64,256]{3,2,1,0:T(8,128)(2,1)S(1)}, u32[]{:S(2)}, u32[]{:S(2)}) collective-permute-start(bf16[3,2,64,256]{3,2,1,0:T(8,128)(2,1)S(1)} %get-tuple-element.54), channel_id=1, source_target_pairs={{0,3},{1,0},{2,1},{3,2},{4,7},{5,4},{6,5},{7,6},{8,11},{9,8},{10,9... | collective-permute-start | bytes 589832 | tf_op jit(solution)/shard_map/ppermute | solution.py:277
  113.4 2.5 %collective-permute-done.10 = bf16[3,2,64,256]{3,2,1,0:T(8,128)(2,1)S(1)} collective-permute-done((bf16[3,2,64,256]{3,2,1,0:T(8,128)(2,1)S(1)}, bf16[3,2,64,256]{3,2,1,0:T(8,128)(2,1)S(1)}, u32[]{:S(2)}, u32[]{:S(2)}) %collective-permute-start.10) | collective-permute-done | bytes 196640 | tf_op jit(solution)/shard_map/ppermute | solution.py:277
  115.9 3.2 %collective-permute-done.11 = bf16[3,2,64,256]{3,2,1,0:T(8,128)(2,1)S(1)} collective-permute-done((bf16[3,2,64,256]{3,2,1,0:T(8,128)(2,1)S(1)}, bf16[3,2,64,256]{3,2,1,0:T(8,128)(2,1)S(1)}, u32[]{:S(2)}, u32[]{:S(2)}) %collective-permute-start.11) | collective-permute-done | bytes 196640 | tf_op jit(solution)/shard_map/ppermute | solution.py:277
  119.9 3.0 %collective-permute-start.13 = (bf16[3,2,64,256]{3,2,1,0:T(8,128)(2,1)S(1)}, bf16[3,2,64,256]{3,2,1,0:T(8,128)(2,1)S(1)}, u32[]{:S(2)}, u32[]{:S(2)}) collective-permute-start(bf16[3,2,64,256]{3,2,1,0:T(8,128)(2,1)S(1)} %fusion), channel_id=1, source_target_pairs={{0,4},{1,5},{2,6},{3,7},{4,0},{5,1},{6,2},{7,3},{8,12},{9,13},{10,... | collective-permute-start | bytes 589832 | tf_op jit(solution)/shard_map/ppermute | solution.py:277
  122.9 4.3 %collective-permute-done.13 = bf16[3,2,64,256]{3,2,1,0:T(8,128)(2,1)S(1)} collective-permute-done((bf16[3,2,64,256]{3,2,1,0:T(8,128)(2,1)S(1)}, bf16[3,2,64,256]{3,2,1,0:T(8,128)(2,1)S(1)}, u32[]{:S(2)}, u32[]{:S(2)}) %collective-permute-start.13) | collective-permute-done | bytes 196640 | tf_op jit(solution)/shard_map/ppermute | solution.py:277
  127.4 2.8 %collective-permute-start.14 = (f32[3]{0:T(128)S(1)}, f32[3]{0:T(128)S(1)}, u32[]{:S(2)}, u32[]{:S(2)}) collective-permute-start(f32[3]{0:T(128)S(1)} %get-tuple-element.55), channel_id=1, source_target_pairs={{0,2},{1,3},{2,0},{3,1},{4,6},{5,7},{6,4},{7,5},{8,10},{9,11},{10,... | collective-permute-start | bytes 44 | tf_op jit(solution)/shard_map/ppermute | solution.py:277
  131.5 1.9 %collective-permute-start.16 = (f32[3]{0:T(128)S(1)}, f32[3]{0:T(128)S(1)}, u32[]{:S(2)}, u32[]{:S(2)}) collective-permute-start(f32[3]{0:T(128)S(1)} %get-tuple-element.55), channel_id=1, source_target_pairs={{0,3},{1,0},{2,1},{3,2},{4,7},{5,4},{6,5},{7,6},{8,11},{9,8},{10,9... | collective-permute-start | bytes 44 | tf_op jit(solution)/shard_map/ppermute | solution.py:277
  133.4 1.5 %collective-permute-done.15 = f32[3]{0:T(128)S(1)} collective-permute-done((f32[3]{0:T(128)S(1)}, f32[3]{0:T(128)S(1)}, u32[]{:S(2)}, u32[]{:S(2)}) %collective-permute-start.15) | collective-permute-done | bytes 44 | tf_op jit(solution)/shard_map/ppermute | solution.py:277
  (34 shorter events, 14.8 us)
Async XLA Ops:
  4.1 4.3 %collective-permute-start = (bf16[4,520,512]{2,1,0:T(8,128)(2,1)S(1)}, bf16[4,520,512]{2,1,0:T(8,128)(2,1)S(1)}, u32[]{:S(2)}, u32[]{:S(2)}) collective-permute-start(bf16[4,520,512]{2,1,0:T(8,128)(2,1)S(1)} %get-tuple-element.30), channel_id=1, source_target_pairs={{0,8},{8,0},{16,24},{24,16},{32,40},{40,32},{48,56},{56,48},{64,72... | collective-permute-start | bytes 6389768 | tf_op jit(solution)/shard_map/ppermute | solution.py:230
  4.2 28.8 %collective-permute-start.4 = (bf16[2,520,512]{2,1,0:T(8,128)(2,1)S(1)}, bf16[2,520,512]{2,1,0:T(8,128)(2,1)S(1)}, u32[]{:S(2)}, u32[]{:S(2)}) collective-permute-start(bf16[2,520,512]{2,1,0:T(8,128)(2,1)S(1)} %get-tuple-element.40), channel_id=1, source_target_pairs={{0,96},{8,104},{16,112},{24,120},{32,64},{40,72},{48,80},{56,88},{... | collective-permute-start | bytes 3194888 | tf_op jit(solution)/shard_map/ppermute | solution.py:230
  8.4 24.8 %slice-start = ((s8[6291456]{0:T(1024)(128)(4,1)}), s8[4194304]{0:T(1024)(128)(4,1)S(1)}, s32[]{:S(2)}) async-start(s8[6291456]{0:T(1024)(128)(4,1)} %bitcast.3), calls=%async_computation | async-start | bytes 8388608
  11.9 21.4 %slice-start.1 = ((s8[6291456]{0:T(1024)(128)(4,1)}), s8[2097152]{0:T(1024)(128)(4,1)S(1)}, s32[]{:S(2)}) async-start(s8[6291456]{0:T(1024)(128)(4,1)} %bitcast.3), calls=%async_computation.1 | async-start | bytes 4194304
  11.9 29.3 %collective-permute-start.1 = (bf16[3,520,512]{2,1,0:T(8,128)(2,1)S(1)}, bf16[3,520,512]{2,1,0:T(8,128)(2,1)S(1)}, u32[]{:S(2)}, u32[]{:S(2)}) collective-permute-start(bf16[3,520,512]{2,1,0:T(8,128)(2,1)S(1)} %shard_map.56), channel_id=1, source_target_pairs={{0,8},{8,0},{16,24},{24,16},{32,40},{40,32},{48,56},{56,48},{64,72... | collective-permute-start | bytes 4792328 | tf_op jit(solution)/shard_map/ppermute | solution.py:230
  15.6 39.9 %collective-permute-start.3 = (bf16[2,520,512]{2,1,0:T(8,128)(2,1)S(1)}, bf16[2,520,512]{2,1,0:T(8,128)(2,1)S(1)}, u32[]{:S(2)}, u32[]{:S(2)}) collective-permute-start(bf16[2,520,512]{2,1,0:T(8,128)(2,1)S(1)} %get-tuple-element.38), channel_id=1, source_target_pairs={{0,80},{8,88},{16,96},{24,104},{32,112},{40,120},{48,64},{56,72},{... | collective-permute-start | bytes 3194888 | tf_op jit(solution)/shard_map/ppermute | solution.py:230
  18.3 15.0 %copy-start = (bf16[3,2,512,256]{3,2,1,0:T(8,128)(2,1)S(1)}, bf16[3,2,512,256]{3,2,1,0:T(8,128)(2,1)}, u32[]{:S(2)}) copy-start(bf16[3,2,512,256]{3,2,1,0:T(8,128)(2,1)} %refs_2_.13) | copy-start | bytes 4718596
  18.3 42.8 %collective-permute-start.2 = (bf16[2,520,512]{2,1,0:T(8,128)(2,1)S(1)}, bf16[2,520,512]{2,1,0:T(8,128)(2,1)S(1)}, u32[]{:S(2)}, u32[]{:S(2)}) collective-permute-start(bf16[2,520,512]{2,1,0:T(8,128)(2,1)S(1)} %get-tuple-element.36), channel_id=1, source_target_pairs={{0,48},{8,56},{16,0},{24,8},{32,16},{40,24},{48,32},{56,40},{64,11... | collective-permute-start | bytes 3194888 | tf_op jit(solution)/shard_map/ppermute | solution.py:230
  33.2 6.6 %collective-permute-start.5 = (bf16[1,520,512]{2,1,0:T(8,128)(2,1)S(1)}, bf16[1,520,512]{2,1,0:T(8,128)(2,1)S(1)}, u32[]{:S(2)}, u32[]{:S(2)}) collective-permute-start(bf16[1,520,512]{2,1,0:T(8,128)(2,1)S(1)} %get-tuple-element.57), channel_id=1, source_target_pairs={{0,8},{8,0},{16,24},{24,16},{32,40},{40,32},{48,56},{56,48},{64,72... | collective-permute-start | bytes 1597448 | tf_op jit(solution)/shard_map/ppermute | solution.py:230
  34.4 44.5 %collective-permute-start.9 = (bf16[2,520,512]{2,1,0:T(8,128)(2,1)S(1)}, bf16[2,520,512]{2,1,0:T(8,128)(2,1)S(1)}, u32[]{:S(2)}, u32[]{:S(2)}) collective-permute-start(bf16[2,520,512]{2,1,0:T(8,128)(2,1)S(1)} %get-tuple-element.49), channel_id=1, source_target_pairs={{0,112},{8,120},{16,64},{24,72},{32,80},{40,88},{48,96},{56,104},{... | collective-permute-start | bytes 3194888 | tf_op jit(solution)/shard_map/ppermute | solution.py:230
  44.2 36.2 %collective-permute-start.8 = (bf16[2,520,512]{2,1,0:T(8,128)(2,1)S(1)}, bf16[2,520,512]{2,1,0:T(8,128)(2,1)S(1)}, u32[]{:S(2)}, u32[]{:S(2)}) collective-permute-start(bf16[2,520,512]{2,1,0:T(8,128)(2,1)S(1)} %get-tuple-element.48), channel_id=1, source_target_pairs={{0,16},{8,24},{16,32},{24,40},{32,48},{40,56},{48,0},{56,8},{64,80... | collective-permute-start | bytes 3194888 | tf_op jit(solution)/shard_map/ppermute | solution.py:230
  57.0 46.5 %collective-permute-start.7 = (bf16[2,520,512]{2,1,0:T(8,128)(2,1)S(1)}, bf16[2,520,512]{2,1,0:T(8,128)(2,1)S(1)}, u32[]{:S(2)}, u32[]{:S(2)}) collective-permute-start(bf16[2,520,512]{2,1,0:T(8,128)(2,1)S(1)} %get-tuple-element.47), channel_id=1, source_target_pairs={{0,32},{8,40},{16,48},{24,56},{32,0},{40,8},{48,16},{56,24},{64,96... | collective-permute-start | bytes 3194888 | tf_op jit(solution)/shard_map/ppermute | solution.py:230
  62.6 42.4 %collective-permute-start.6 = (bf16[2,520,512]{2,1,0:T(8,128)(2,1)S(1)}, bf16[2,520,512]{2,1,0:T(8,128)(2,1)S(1)}, u32[]{:S(2)}, u32[]{:S(2)}) collective-permute-start(bf16[2,520,512]{2,1,0:T(8,128)(2,1)S(1)} %get-tuple-element.46), channel_id=1, source_target_pairs={{0,64},{8,72},{16,80},{24,88},{32,96},{40,104},{48,112},{56,120},{... | collective-permute-start | bytes 3194888 | tf_op jit(solution)/shard_map/ppermute | solution.py:230
  106.2 9.7 %collective-permute-start.10 = (bf16[3,2,64,256]{3,2,1,0:T(8,128)(2,1)S(1)}, bf16[3,2,64,256]{3,2,1,0:T(8,128)(2,1)S(1)}, u32[]{:S(2)}, u32[]{:S(2)}) collective-permute-start(bf16[3,2,64,256]{3,2,1,0:T(8,128)(2,1)S(1)} %get-tuple-element.52), channel_id=1, source_target_pairs={{0,2},{1,3},{2,0},{3,1},{4,6},{5,7},{6,4},{7,5},{8,10},{9,11},{10,... | collective-permute-start | bytes 589832 | tf_op jit(solution)/shard_map/ppermute | solution.py:277
  110.2 8.9 %collective-permute-start.11 = (bf16[3,2,64,256]{3,2,1,0:T(8,128)(2,1)S(1)}, bf16[3,2,64,256]{3,2,1,0:T(8,128)(2,1)S(1)}, u32[]{:S(2)}, u32[]{:S(2)}) collective-permute-start(bf16[3,2,64,256]{3,2,1,0:T(8,128)(2,1)S(1)} %get-tuple-element.53), channel_id=1, source_target_pairs={{0,1},{1,2},{2,3},{3,0},{4,5},{5,6},{6,7},{7,4},{8,9},{9,10},{10,1... | collective-permute-start | bytes 589832 | tf_op jit(solution)/shard_map/ppermute | solution.py:277
  111.2 8.6 %collective-permute-start.12 = (bf16[3,2,64,256]{3,2,1,0:T(8,128)(2,1)S(1)}, bf16[3,2,64,256]{3,2,1,0:T(8,128)(2,1)S(1)}, u32[]{:S(2)}, u32[]{:S(2)}) collective-permute-start(bf16[3,2,64,256]{3,2,1,0:T(8,128)(2,1)S(1)} %get-tuple-element.54), channel_id=1, source_target_pairs={{0,3},{1,0},{2,1},{3,2},{4,7},{5,4},{6,5},{7,6},{8,11},{9,8},{10,9... | collective-permute-start | bytes 589832 | tf_op jit(solution)/shard_map/ppermute | solution.py:277
  119.9 7.3 %collective-permute-start.13 = (bf16[3,2,64,256]{3,2,1,0:T(8,128)(2,1)S(1)}, bf16[3,2,64,256]{3,2,1,0:T(8,128)(2,1)S(1)}, u32[]{:S(2)}, u32[]{:S(2)}) collective-permute-start(bf16[3,2,64,256]{3,2,1,0:T(8,128)(2,1)S(1)} %fusion), channel_id=1, source_target_pairs={{0,4},{1,5},{2,6},{3,7},{4,0},{5,1},{6,2},{7,3},{8,12},{9,13},{10,... | collective-permute-start | bytes 589832 | tf_op jit(solution)/shard_map/ppermute | solution.py:277
  127.4 6.0 %collective-permute-start.14 = (f32[3]{0:T(128)S(1)}, f32[3]{0:T(128)S(1)}, u32[]{:S(2)}, u32[]{:S(2)}) collective-permute-start(f32[3]{0:T(128)S(1)} %get-tuple-element.55), channel_id=1, source_target_pairs={{0,2},{1,3},{2,0},{3,1},{4,6},{5,7},{6,4},{7,5},{8,10},{9,11},{10,... | collective-permute-start | bytes 44 | tf_op jit(solution)/shard_map/ppermute | solution.py:277
  130.1 4.8 %collective-permute-start.15 = (f32[3]{0:T(128)S(1)}, f32[3]{0:T(128)S(1)}, u32[]{:S(2)}, u32[]{:S(2)}) collective-permute-start(f32[3]{0:T(128)S(1)} %get-tuple-element.55), channel_id=1, source_target_pairs={{0,1},{1,2},{2,3},{3,0},{4,5},{5,6},{6,7},{7,4},{8,9},{9,10},{10,1... | collective-permute-start | bytes 44 | tf_op jit(solution)/shard_map/ppermute | solution.py:277
  131.5 3.5 %collective-permute-start.16 = (f32[3]{0:T(128)S(1)}, f32[3]{0:T(128)S(1)}, u32[]{:S(2)}, u32[]{:S(2)}) collective-permute-start(f32[3]{0:T(128)S(1)} %get-tuple-element.55), channel_id=1, source_target_pairs={{0,3},{1,0},{2,1},{3,2},{4,7},{5,4},{6,5},{7,6},{8,11},{9,8},{10,9... | collective-permute-start | bytes 44 | tf_op jit(solution)/shard_map/ppermute | solution.py:277

commit v6 on v5

--- a/solution.py
+++ b/solution.py
@@ -210,7 +210,7 @@
 BASE = 4
 ZS = 4
 DIRECT = (1, 2)
-FLOWS = ((1, 1), (0, 3), (1, 3), (0, 1), (0, 2), (1, 0))
+FLOWS = ((1, 1), (0, 3), (1, 3), (0, 1), (1, 0), (0, 2))
 EARLY = 3
 AHEAD = 3
 

time: 136 us -> 135 us (level)
  waiting for transfers between devices: 72.8 us -> 71.3 us
    ppermute x10, waiting for transfers between devices: 60.4 us -> 59 us  [on_device(): lax.ppermute(x, 'tile', pairs(owners, dy, dx, dc))]
  transfers between devices with their start and end apart: 17 -> 17, of which waited for: 10 -> 11; matrix products, arithmetic and copies ran while one was open for 0% -> 0% of each run, Pallas kernels for 15% -> 15%
where the time goes in v6:
time: 135 us; the launch traced here: 134 us
  waiting for transfers between devices  71.3 us (53%)
  starting transfers between devices  36.5 us (27%)
  Pallas kernels  25.2 us (19%)
    ppermute x10, waiting for transfers between devices, on_device(): lax.ppermute(x, 'tile', pairs(owners, dy, dx, dc))  59 us
    ppermute x10, starting transfers between devices, on_device(): lax.ppermute(x, 'tile', pairs(owners, dy, dx, dc))  20.3 us
    ppermute x7, starting transfers between devices, on_device(): lax.ppermute(x, 'subap', [(i, (i // ZS ^ dy) * ZS + (i + dz) % ZS) for i...  16.2 us
    pallas_call x4, Pallas kernels, cut_windows(): pl.pallas_call(functools.partial(cut_kernel, pieces, fills, held), out_sh...  14 us
    ppermute x7, waiting for transfers between devices, on_device(): lax.ppermute(x, 'subap', [(i, (i // ZS ^ dy) * ZS + (i + dz) % ZS) for i...  12.3 us
    pallas_call x8, Pallas kernels, add(): pl.pallas_call(functools.partial(add_kernel, sources, slots, first, last)...  11.1 us
  transfers between devices with their start and end apart: 17, of which 11 were waited for; matrix products, arithmetic and copies ran while one was open for 0% of the time, Pallas kernels for 15%

profile of v6, /device:TPU:0, one launch (start us, length us, event | category | flops | bytes accessed | tf_op | source)
XLA Modules:
  0.0 134.3 jit_solution(5474559196669140982)
XLA Ops:
  0.0 4.1 %shard_map.55 = (bf16[2,520,512]{2,1,0:T(8,128)(2,1)S(1)}, bf16[4,520,512]{2,1,0:T(8,128)(2,1)S(1)}) custom-call(s32[32]{0:T(128)} %bitcast.17, s32[48]{0:T(128)} %offsets_hbm.7, bf16[256,16384]{1,0:T(8,128)(2,1)} %bitcast.13), custom_call_target="tpu_custom_call" | custom-call | bytes 1000 | tf_op jit(solution)/shard_map/pallas_call | solution.py:100
  4.2 4.2 %collective-permute-start.4 = (bf16[2,520,512]{2,1,0:T(8,128)(2,1)S(1)}, bf16[2,520,512]{2,1,0:T(8,128)(2,1)S(1)}, u32[]{:S(2)}, u32[]{:S(2)}) collective-permute-start(bf16[2,520,512]{2,1,0:T(8,128)(2,1)S(1)} %get-tuple-element.40), channel_id=1, source_target_pairs={{0,96},{8,104},{16,112},{24,120},{32,64},{40,72},{48,80},{56,88},{... | collective-permute-start | bytes 3194888 | tf_op jit(solution)/shard_map/ppermute | solution.py:230
  8.4 3.5 %shard_map.56 = bf16[3,520,512]{2,1,0:T(8,128)(2,1)S(1)} custom-call(s32[32]{0:T(128)} %bitcast.18, s32[48]{0:T(128)} %offsets_hbm.7, bf16[256,16384]{1,0:T(8,128)(2,1)} %bitcast.14), custom_call_target="tpu_custom_call" | custom-call | bytes 1000 | tf_op jit(solution)/shard_map/pallas_call | solution.py:100
  12.1 3.5 %shard_map.58 = (bf16[2,520,512]{2,1,0:T(8,128)(2,1)S(1)}, bf16[2,520,512]{2,1,0:T(8,128)(2,1)S(1)}, bf16[2,520,512]{2,1,0:T(8,128)(2,1)S(1)}, bf16[2,520,512]{2,1,0:T(8,128)(2,1)S(1)}) custom-call(s32[32]{0:T(128)} %bitcast.19, s32[48]{0:T(128)} %offsets_hbm.7, bf16[256,16384]{1,0:T(8,128)(2,1)} %bitcast.15, ...), custom_call_target="tpu_custom_call" | custom-call | bytes 1000 | tf_op jit(solution)/shard_map/pallas_call | solution.py:100
  15.6 2.6 %collective-permute-start.3 = (bf16[2,520,512]{2,1,0:T(8,128)(2,1)S(1)}, bf16[2,520,512]{2,1,0:T(8,128)(2,1)S(1)}, u32[]{:S(2)}, u32[]{:S(2)}) collective-permute-start(bf16[2,520,512]{2,1,0:T(8,128)(2,1)S(1)} %get-tuple-element.38), channel_id=1, source_target_pairs={{0,80},{8,88},{16,96},{24,104},{32,112},{40,120},{48,64},{56,72},{... | collective-permute-start | bytes 3194888 | tf_op jit(solution)/shard_map/ppermute | solution.py:230
  18.3 1.7 %collective-permute-start.2 = (bf16[2,520,512]{2,1,0:T(8,128)(2,1)S(1)}, bf16[2,520,512]{2,1,0:T(8,128)(2,1)S(1)}, u32[]{:S(2)}, u32[]{:S(2)}) collective-permute-start(bf16[2,520,512]{2,1,0:T(8,128)(2,1)S(1)} %get-tuple-element.36), channel_id=1, source_target_pairs={{0,48},{8,56},{16,0},{24,8},{32,16},{40,24},{48,32},{56,40},{64,11... | collective-permute-start | bytes 3194888 | tf_op jit(solution)/shard_map/ppermute | solution.py:230
  20.0 13.0 %collective-permute-done.4 = bf16[2,520,512]{2,1,0:T(8,128)(2,1)S(1)} collective-permute-done((bf16[2,520,512]{2,1,0:T(8,128)(2,1)S(1)}, bf16[2,520,512]{2,1,0:T(8,128)(2,1)S(1)}, u32[]{:S(2)}, u32[]{:S(2)}) %collective-permute-start.4) | collective-permute-done | bytes 1064992 | tf_op jit(solution)/shard_map/ppermute | solution.py:230
  34.4 5.3 %collective-permute-start.9 = (bf16[2,520,512]{2,1,0:T(8,128)(2,1)S(1)}, bf16[2,520,512]{2,1,0:T(8,128)(2,1)S(1)}, u32[]{:S(2)}, u32[]{:S(2)}) collective-permute-start(bf16[2,520,512]{2,1,0:T(8,128)(2,1)S(1)} %get-tuple-element.49), channel_id=1, source_target_pairs={{0,112},{8,120},{16,64},{24,72},{32,80},{40,88},{48,96},{56,104},{... | collective-permute-start | bytes 3194888 | tf_op jit(solution)/shard_map/ppermute | solution.py:230
  41.3 2.9 %shard_map.57 = (bf16[2,520,512]{2,1,0:T(8,128)(2,1)S(1)}, bf16[2,520,512]{2,1,0:T(8,128)(2,1)S(1)}, bf16[2,520,512]{2,1,0:T(8,128)(2,1)S(1)}) custom-call(s32[32]{0:T(128)} %bitcast.20, s32[48]{0:T(128)} %offsets_hbm.7, bf16[256,16384]{1,0:T(8,128)(2,1)} %bitcast.16, bf16[3,520,512]{2,1,0:T(8,128)(2,1)S(1)} %collective-permute-done.1.refs_0_), custom_call_target="tpu_custom_call" | custom-call | bytes 1000 | tf_op jit(solution)/shard_map/pallas_call | solution.py:100
  44.5 11.1 %collective-permute-done.3.refs_0_ = bf16[2,520,512]{2,1,0:T(8,128)(2,1)S(1)} collective-permute-done((bf16[2,520,512]{2,1,0:T(8,128)(2,1)S(1)}, bf16[2,520,512]{2,1,0:T(8,128)(2,1)S(1)}, u32[]{:S(2)}, u32[]{:S(2)}) %collective-permute-start.3) | collective-permute-done | bytes 1064992 | tf_op jit(solution)/shard_map/ppermute | solution.py:230
  57.0 1.8 %collective-permute-start.7 = (bf16[2,520,512]{2,1,0:T(8,128)(2,1)S(1)}, bf16[2,520,512]{2,1,0:T(8,128)(2,1)S(1)}, u32[]{:S(2)}, u32[]{:S(2)}) collective-permute-start(bf16[2,520,512]{2,1,0:T(8,128)(2,1)S(1)} %get-tuple-element.47), channel_id=1, source_target_pairs={{0,64},{8,72},{16,80},{24,88},{32,96},{40,104},{48,112},{56,120},{... | collective-permute-start | bytes 3194888 | tf_op jit(solution)/shard_map/ppermute | solution.py:230
  58.8 1.5 %shard_map.62.refs_3_ = f32[3,2,256,256]{3,2,1,0:T(8,128)S(1)} custom-call(bf16[2,520,512]{2,1,0:T(8,128)(2,1)S(1)} %collective-permute-done.2.refs_0_, bf16[3,16,2,256,128]{4,3,2,1,0:T(8,128)(2,1)S(1)} %bitcast.8, bf16[3,2,512,256]{3,2,1,0:T(8,128)(2,1)S(1)} %copy-done, f32[3,2,256,256]{3,2,1,0:T(8,128)S(1)} %shard_map.61.refs_3_), custom_call_target="tpu_custom_call", output_to_operand_aliasing={{}: (3, {})} | custom-call | flops 800000000 | bytes 6000000 | tf_op jit(solution)/shard_map/pallas_call | solution.py:193
  60.3 4.0 %collective-permute-start.6 = (bf16[2,520,512]{2,1,0:T(8,128)(2,1)S(1)}, bf16[2,520,512]{2,1,0:T(8,128)(2,1)S(1)}, u32[]{:S(2)}, u32[]{:S(2)}) collective-permute-start(bf16[2,520,512]{2,1,0:T(8,128)(2,1)S(1)} %get-tuple-element.46), channel_id=1, source_target_pairs={{0,32},{8,40},{16,48},{24,56},{32,0},{40,8},{48,16},{56,24},{64,96... | collective-permute-start | bytes 3194888 | tf_op jit(solution)/shard_map/ppermute | solution.py:230
  64.2 14.7 %collective-permute-done.9.refs_0_ = bf16[2,520,512]{2,1,0:T(8,128)(2,1)S(1)} collective-permute-done((bf16[2,520,512]{2,1,0:T(8,128)(2,1)S(1)}, bf16[2,520,512]{2,1,0:T(8,128)(2,1)S(1)}, u32[]{:S(2)}, u32[]{:S(2)}) %collective-permute-start.9) | collective-permute-done | bytes 1064992 | tf_op jit(solution)/shard_map/ppermute | solution.py:230
  81.9 19.4 %collective-permute-done.7.refs_0_ = bf16[2,520,512]{2,1,0:T(8,128)(2,1)S(1)} collective-permute-done((bf16[2,520,512]{2,1,0:T(8,128)(2,1)S(1)}, bf16[2,520,512]{2,1,0:T(8,128)(2,1)S(1)}, u32[]{:S(2)}, u32[]{:S(2)}) %collective-permute-start.7) | collective-permute-done | bytes 1064992 | tf_op jit(solution)/shard_map/ppermute | solution.py:230
  104.7 4.0 %collective-permute-start.10 = (bf16[3,2,64,256]{3,2,1,0:T(8,128)(2,1)S(1)}, bf16[3,2,64,256]{3,2,1,0:T(8,128)(2,1)S(1)}, u32[]{:S(2)}, u32[]{:S(2)}) collective-permute-start(bf16[3,2,64,256]{3,2,1,0:T(8,128)(2,1)S(1)} %get-tuple-element.52), channel_id=1, source_target_pairs={{0,2},{1,3},{2,0},{3,1},{4,6},{5,7},{6,4},{7,5},{8,10},{9,11},{10,... | collective-permute-start | bytes 589832 | tf_op jit(solution)/shard_map/ppermute | solution.py:277
  109.7 2.2 %collective-permute-start.12 = (bf16[3,2,64,256]{3,2,1,0:T(8,128)(2,1)S(1)}, bf16[3,2,64,256]{3,2,1,0:T(8,128)(2,1)S(1)}, u32[]{:S(2)}, u32[]{:S(2)}) collective-permute-start(bf16[3,2,64,256]{3,2,1,0:T(8,128)(2,1)S(1)} %get-tuple-element.54), channel_id=1, source_target_pairs={{0,3},{1,0},{2,1},{3,2},{4,7},{5,4},{6,5},{7,6},{8,11},{9,8},{10,9... | collective-permute-start | bytes 589832 | tf_op jit(solution)/shard_map/ppermute | solution.py:277
  111.9 2.5 %collective-permute-done.10 = bf16[3,2,64,256]{3,2,1,0:T(8,128)(2,1)S(1)} collective-permute-done((bf16[3,2,64,256]{3,2,1,0:T(8,128)(2,1)S(1)}, bf16[3,2,64,256]{3,2,1,0:T(8,128)(2,1)S(1)}, u32[]{:S(2)}, u32[]{:S(2)}) %collective-permute-start.10) | collective-permute-done | bytes 196640 | tf_op jit(solution)/shard_map/ppermute | solution.py:277
  114.4 3.2 %collective-permute-done.11 = bf16[3,2,64,256]{3,2,1,0:T(8,128)(2,1)S(1)} collective-permute-done((bf16[3,2,64,256]{3,2,1,0:T(8,128)(2,1)S(1)}, bf16[3,2,64,256]{3,2,1,0:T(8,128)(2,1)S(1)}, u32[]{:S(2)}, u32[]{:S(2)}) %collective-permute-start.11) | collective-permute-done | bytes 196640 | tf_op jit(solution)/shard_map/ppermute | solution.py:277
  118.4 3.0 %collective-permute-start.13 = (bf16[3,2,64,256]{3,2,1,0:T(8,128)(2,1)S(1)}, bf16[3,2,64,256]{3,2,1,0:T(8,128)(2,1)S(1)}, u32[]{:S(2)}, u32[]{:S(2)}) collective-permute-start(bf16[3,2,64,256]{3,2,1,0:T(8,128)(2,1)S(1)} %fusion), channel_id=1, source_target_pairs={{0,4},{1,5},{2,6},{3,7},{4,0},{5,1},{6,2},{7,3},{8,12},{9,13},{10,... | collective-permute-start | bytes 589832 | tf_op jit(solution)/shard_map/ppermute | solution.py:277
  121.4 4.3 %collective-permute-done.13 = bf16[3,2,64,256]{3,2,1,0:T(8,128)(2,1)S(1)} collective-permute-done((bf16[3,2,64,256]{3,2,1,0:T(8,128)(2,1)S(1)}, bf16[3,2,64,256]{3,2,1,0:T(8,128)(2,1)S(1)}, u32[]{:S(2)}, u32[]{:S(2)}) %collective-permute-start.13) | collective-permute-done | bytes 196640 | tf_op jit(solution)/shard_map/ppermute | solution.py:277
  125.9 2.8 %collective-permute-start.14 = (f32[3]{0:T(128)S(1)}, f32[3]{0:T(128)S(1)}, u32[]{:S(2)}, u32[]{:S(2)}) collective-permute-start(f32[3]{0:T(128)S(1)} %get-tuple-element.55), channel_id=1, source_target_pairs={{0,2},{1,3},{2,0},{3,1},{4,6},{5,7},{6,4},{7,5},{8,10},{9,11},{10,... | collective-permute-start | bytes 44 | tf_op jit(solution)/shard_map/ppermute | solution.py:277
  130.0 1.9 %collective-permute-start.16 = (f32[3]{0:T(128)S(1)}, f32[3]{0:T(128)S(1)}, u32[]{:S(2)}, u32[]{:S(2)}) collective-permute-start(f32[3]{0:T(128)S(1)} %get-tuple-element.55), channel_id=1, source_target_pairs={{0,3},{1,0},{2,1},{3,2},{4,7},{5,4},{6,5},{7,6},{8,11},{9,8},{10,9... | collective-permute-start | bytes 44 | tf_op jit(solution)/shard_map/ppermute | solution.py:277
  131.9 1.5 %collective-permute-done.15 = f32[3]{0:T(128)S(1)} collective-permute-done((f32[3]{0:T(128)S(1)}, f32[3]{0:T(128)S(1)}, u32[]{:S(2)}, u32[]{:S(2)}) %collective-permute-start.15) | collective-permute-done | bytes 44 | tf_op jit(solution)/shard_map/ppermute | solution.py:277
  (34 shorter events, 15.5 us)
Async XLA Ops:
  4.1 4.3 %collective-permute-start = (bf16[4,520,512]{2,1,0:T(8,128)(2,1)S(1)}, bf16[4,520,512]{2,1,0:T(8,128)(2,1)S(1)}, u32[]{:S(2)}, u32[]{:S(2)}) collective-permute-start(bf16[4,520,512]{2,1,0:T(8,128)(2,1)S(1)} %get-tuple-element.30), channel_id=1, source_target_pairs={{0,8},{8,0},{16,24},{24,16},{32,40},{40,32},{48,56},{56,48},{64,72... | collective-permute-start | bytes 6389768 | tf_op jit(solution)/shard_map/ppermute | solution.py:230
  4.2 28.8 %collective-permute-start.4 = (bf16[2,520,512]{2,1,0:T(8,128)(2,1)S(1)}, bf16[2,520,512]{2,1,0:T(8,128)(2,1)S(1)}, u32[]{:S(2)}, u32[]{:S(2)}) collective-permute-start(bf16[2,520,512]{2,1,0:T(8,128)(2,1)S(1)} %get-tuple-element.40), channel_id=1, source_target_pairs={{0,96},{8,104},{16,112},{24,120},{32,64},{40,72},{48,80},{56,88},{... | collective-permute-start | bytes 3194888 | tf_op jit(solution)/shard_map/ppermute | solution.py:230
  8.4 24.8 %slice-start = ((s8[6291456]{0:T(1024)(128)(4,1)}), s8[4194304]{0:T(1024)(128)(4,1)S(1)}, s32[]{:S(2)}) async-start(s8[6291456]{0:T(1024)(128)(4,1)} %bitcast.3), calls=%async_computation | async-start | bytes 8388608
  11.9 21.4 %slice-start.1 = ((s8[6291456]{0:T(1024)(128)(4,1)}), s8[2097152]{0:T(1024)(128)(4,1)S(1)}, s32[]{:S(2)}) async-start(s8[6291456]{0:T(1024)(128)(4,1)} %bitcast.3), calls=%async_computation.1 | async-start | bytes 4194304
  11.9 29.3 %collective-permute-start.1 = (bf16[3,520,512]{2,1,0:T(8,128)(2,1)S(1)}, bf16[3,520,512]{2,1,0:T(8,128)(2,1)S(1)}, u32[]{:S(2)}, u32[]{:S(2)}) collective-permute-start(bf16[3,520,512]{2,1,0:T(8,128)(2,1)S(1)} %shard_map.56), channel_id=1, source_target_pairs={{0,8},{8,0},{16,24},{24,16},{32,40},{40,32},{48,56},{56,48},{64,72... | collective-permute-start | bytes 4792328 | tf_op jit(solution)/shard_map/ppermute | solution.py:230
  15.6 39.9 %collective-permute-start.3 = (bf16[2,520,512]{2,1,0:T(8,128)(2,1)S(1)}, bf16[2,520,512]{2,1,0:T(8,128)(2,1)S(1)}, u32[]{:S(2)}, u32[]{:S(2)}) collective-permute-start(bf16[2,520,512]{2,1,0:T(8,128)(2,1)S(1)} %get-tuple-element.38), channel_id=1, source_target_pairs={{0,80},{8,88},{16,96},{24,104},{32,112},{40,120},{48,64},{56,72},{... | collective-permute-start | bytes 3194888 | tf_op jit(solution)/shard_map/ppermute | solution.py:230
  18.3 15.0 %copy-start = (bf16[3,2,512,256]{3,2,1,0:T(8,128)(2,1)S(1)}, bf16[3,2,512,256]{3,2,1,0:T(8,128)(2,1)}, u32[]{:S(2)}) copy-start(bf16[3,2,512,256]{3,2,1,0:T(8,128)(2,1)} %refs_2_.13) | copy-start | bytes 4718596
  18.3 40.5 %collective-permute-start.2 = (bf16[2,520,512]{2,1,0:T(8,128)(2,1)S(1)}, bf16[2,520,512]{2,1,0:T(8,128)(2,1)S(1)}, u32[]{:S(2)}, u32[]{:S(2)}) collective-permute-start(bf16[2,520,512]{2,1,0:T(8,128)(2,1)S(1)} %get-tuple-element.36), channel_id=1, source_target_pairs={{0,48},{8,56},{16,0},{24,8},{32,16},{40,24},{48,32},{56,40},{64,11... | collective-permute-start | bytes 3194888 | tf_op jit(solution)/shard_map/ppermute | solution.py:230
  33.2 6.6 %collective-permute-start.5 = (bf16[1,520,512]{2,1,0:T(8,128)(2,1)S(1)}, bf16[1,520,512]{2,1,0:T(8,128)(2,1)S(1)}, u32[]{:S(2)}, u32[]{:S(2)}) collective-permute-start(bf16[1,520,512]{2,1,0:T(8,128)(2,1)S(1)} %get-tuple-element.57), channel_id=1, source_target_pairs={{0,8},{8,0},{16,24},{24,16},{32,40},{40,32},{48,56},{56,48},{64,72... | collective-permute-start | bytes 1597448 | tf_op jit(solution)/shard_map/ppermute | solution.py:230
  34.4 44.5 %collective-permute-start.9 = (bf16[2,520,512]{2,1,0:T(8,128)(2,1)S(1)}, bf16[2,520,512]{2,1,0:T(8,128)(2,1)S(1)}, u32[]{:S(2)}, u32[]{:S(2)}) collective-permute-start(bf16[2,520,512]{2,1,0:T(8,128)(2,1)S(1)} %get-tuple-element.49), channel_id=1, source_target_pairs={{0,112},{8,120},{16,64},{24,72},{32,80},{40,88},{48,96},{56,104},{... | collective-permute-start | bytes 3194888 | tf_op jit(solution)/shard_map/ppermute | solution.py:230
  44.2 36.2 %collective-permute-start.8 = (bf16[2,520,512]{2,1,0:T(8,128)(2,1)S(1)}, bf16[2,520,512]{2,1,0:T(8,128)(2,1)S(1)}, u32[]{:S(2)}, u32[]{:S(2)}) collective-permute-start(bf16[2,520,512]{2,1,0:T(8,128)(2,1)S(1)} %get-tuple-element.48), channel_id=1, source_target_pairs={{0,16},{8,24},{16,32},{24,40},{32,48},{40,56},{48,0},{56,8},{64,80... | collective-permute-start | bytes 3194888 | tf_op jit(solution)/shard_map/ppermute | solution.py:230
  57.0 44.2 %collective-permute-start.7 = (bf16[2,520,512]{2,1,0:T(8,128)(2,1)S(1)}, bf16[2,520,512]{2,1,0:T(8,128)(2,1)S(1)}, u32[]{:S(2)}, u32[]{:S(2)}) collective-permute-start(bf16[2,520,512]{2,1,0:T(8,128)(2,1)S(1)} %get-tuple-element.47), channel_id=1, source_target_pairs={{0,64},{8,72},{16,80},{24,88},{32,96},{40,104},{48,112},{56,120},{... | collective-permute-start | bytes 3194888 | tf_op jit(solution)/shard_map/ppermute | solution.py:230
  60.3 43.2 %collective-permute-start.6 = (bf16[2,520,512]{2,1,0:T(8,128)(2,1)S(1)}, bf16[2,520,512]{2,1,0:T(8,128)(2,1)S(1)}, u32[]{:S(2)}, u32[]{:S(2)}) collective-permute-start(bf16[2,520,512]{2,1,0:T(8,128)(2,1)S(1)} %get-tuple-element.46), channel_id=1, source_target_pairs={{0,32},{8,40},{16,48},{24,56},{32,0},{40,8},{48,16},{56,24},{64,96... | collective-permute-start | bytes 3194888 | tf_op jit(solution)/shard_map/ppermute | solution.py:230
  104.7 9.7 %collective-permute-start.10 = (bf16[3,2,64,256]{3,2,1,0:T(8,128)(2,1)S(1)}, bf16[3,2,64,256]{3,2,1,0:T(8,128)(2,1)S(1)}, u32[]{:S(2)}, u32[]{:S(2)}) collective-permute-start(bf16[3,2,64,256]{3,2,1,0:T(8,128)(2,1)S(1)} %get-tuple-element.52), channel_id=1, source_target_pairs={{0,2},{1,3},{2,0},{3,1},{4,6},{5,7},{6,4},{7,5},{8,10},{9,11},{10,... | collective-permute-start | bytes 589832 | tf_op jit(solution)/shard_map/ppermute | solution.py:277
  108.7 8.9 %collective-permute-start.11 = (bf16[3,2,64,256]{3,2,1,0:T(8,128)(2,1)S(1)}, bf16[3,2,64,256]{3,2,1,0:T(8,128)(2,1)S(1)}, u32[]{:S(2)}, u32[]{:S(2)}) collective-permute-start(bf16[3,2,64,256]{3,2,1,0:T(8,128)(2,1)S(1)} %get-tuple-element.53), channel_id=1, source_target_pairs={{0,1},{1,2},{2,3},{3,0},{4,5},{5,6},{6,7},{7,4},{8,9},{9,10},{10,1... | collective-permute-start | bytes 589832 | tf_op jit(solution)/shard_map/ppermute | solution.py:277
  109.7 8.6 %collective-permute-start.12 = (bf16[3,2,64,256]{3,2,1,0:T(8,128)(2,1)S(1)}, bf16[3,2,64,256]{3,2,1,0:T(8,128)(2,1)S(1)}, u32[]{:S(2)}, u32[]{:S(2)}) collective-permute-start(bf16[3,2,64,256]{3,2,1,0:T(8,128)(2,1)S(1)} %get-tuple-element.54), channel_id=1, source_target_pairs={{0,3},{1,0},{2,1},{3,2},{4,7},{5,4},{6,5},{7,6},{8,11},{9,8},{10,9... | collective-permute-start | bytes 589832 | tf_op jit(solution)/shard_map/ppermute | solution.py:277
  118.4 7.3 %collective-permute-start.13 = (bf16[3,2,64,256]{3,2,1,0:T(8,128)(2,1)S(1)}, bf16[3,2,64,256]{3,2,1,0:T(8,128)(2,1)S(1)}, u32[]{:S(2)}, u32[]{:S(2)}) collective-permute-start(bf16[3,2,64,256]{3,2,1,0:T(8,128)(2,1)S(1)} %fusion), channel_id=1, source_target_pairs={{0,4},{1,5},{2,6},{3,7},{4,0},{5,1},{6,2},{7,3},{8,12},{9,13},{10,... | collective-permute-start | bytes 589832 | tf_op jit(solution)/shard_map/ppermute | solution.py:277
  125.9 6.0 %collective-permute-start.14 = (f32[3]{0:T(128)S(1)}, f32[3]{0:T(128)S(1)}, u32[]{:S(2)}, u32[]{:S(2)}) collective-permute-start(f32[3]{0:T(128)S(1)} %get-tuple-element.55), channel_id=1, source_target_pairs={{0,2},{1,3},{2,0},{3,1},{4,6},{5,7},{6,4},{7,5},{8,10},{9,11},{10,... | collective-permute-start | bytes 44 | tf_op jit(solution)/shard_map/ppermute | solution.py:277
  128.6 4.8 %collective-permute-start.15 = (f32[3]{0:T(128)S(1)}, f32[3]{0:T(128)S(1)}, u32[]{:S(2)}, u32[]{:S(2)}) collective-permute-start(f32[3]{0:T(128)S(1)} %get-tuple-element.55), channel_id=1, source_target_pairs={{0,1},{1,2},{2,3},{3,0},{4,5},{5,6},{6,7},{7,4},{8,9},{9,10},{10,1... | collective-permute-start | bytes 44 | tf_op jit(solution)/shard_map/ppermute | solution.py:277
  130.0 3.5 %collective-permute-start.16 = (f32[3]{0:T(128)S(1)}, f32[3]{0:T(128)S(1)}, u32[]{:S(2)}, u32[]{:S(2)}) collective-permute-start(f32[3]{0:T(128)S(1)} %get-tuple-element.55), channel_id=1, source_target_pairs={{0,3},{1,0},{2,1},{3,2},{4,7},{5,4},{6,5},{7,6},{8,11},{9,8},{10,9... | collective-permute-start | bytes 44 | tf_op jit(solution)/shard_map/ppermute | solution.py:277
